TPU v7x, 32 devices: a whole 2x2x4 slice. The times are simulated.
32 devices in a mesh: band: 16 (over z, x, core), fld: 2 (over y).
Axes of the slice: x: 2, y: 2, z: 4, core: 2. Of those that a mesh axis runs over, the one named last changes fastest.
Arguments:
- grid_field: bfloat16 [2, 4, 1280, 2, 5248], P(None, 'fld', 'band'), may hold values from -6 to 6
- coupling: float32 [2, 4], P(None, 'fld'), may hold values from 0.1 to 1
- points: int32 [1280], replicated, may hold values from 20 to 5136, as said below
- lat_ids: int32 [1280], P('band'), may hold values from 0 to 1279, each once
- wn_ids: int32 [128], P('band'), may hold values from 0 to 1279, as said below
Outputs:
- new_grid: bfloat16 [2, 4, 1280, 2, 5248], P(None, 'fld', 'band')
Inputs may be any that keep to these rules, and one draw needn't show every extreme that they name: Latitude i has 20 + 4 i points or up to 8 fewer, a multiple of 4, never under 20; the last latitude has exactly the most. `lat_ids`: each hemispheric latitude stands in exactly one slot. `wn_ids`: distinct wavenumbers; 0 and 1279 are always among them.
All inputs are finite; a program needn't handle non-finite values.
Results may differ from a plain program's by a relative error of at most 0.014.
Values may be sent and summed in bfloat16 or wider, within the bound.
No kernel may reach another device: no remote copies, remote signals or barrier semaphores. Data moves between devices by JAX's collectives and lax.ppermute only.
A program may use at most 128 MiB of HBM per device.

v0:
```python
import math

import jax
import jax.numpy as jnp
from jax import lax
from jax.sharding import PartitionSpec as P

NT = 1279
NH = 1280
PPAD = 5248


rescale_limit = 2.0**60
rescale_log = 60.0 * math.log(2.0)


def carried_in(array, axis, join, neutral):
    place = lax.axis_index(axis)
    gathered = lax.all_gather(array.astype(jnp.bfloat16), axis)
    state = jnp.zeros_like(array) + jnp.asarray(neutral, array.dtype)

    def one(step, state):
        return join(state, lax.dynamic_index_in_dim(gathered, step, 0, False).astype(array.dtype))

    return lax.fori_loop(0, place, one, state)


def latitude_angles(lat_index):
    colatitude = math.pi * (lat_index.astype(jnp.float32) + 0.5) / (2.0 * NH)
    return (jnp.cos(colatitude), jnp.sin(colatitude))


def damping(orders):
    row_index = jnp.arange(NT + 1).astype(jnp.float32).reshape((NT + 1) // 2, 2)
    degree = row_index[:, :, None] + orders.astype(jnp.float32)[None, None, :]
    return 1.0 / (1.0 + 4.0 * degree * (degree + 1.0) / (NT * (NT + 1.0)))


def legendre_rows(orders, cosines, sines):
    order_f = orders.astype(jnp.float32)[:, None]
    step_index = jnp.arange(1, NT + 1).astype(jnp.float32)
    log_terms = jnp.log1p(0.5 / step_index)
    log_norm = 0.5 * math.log(0.5) + 0.5 * jnp.sum(
        jnp.where(step_index[None, :] <= order_f, log_terms[None, :], 0.0), axis=1
    )
    scaled_log = log_norm[:, None] + order_f * jnp.log(sines)[None, :]
    start_row = jnp.ones(scaled_log.shape, jnp.float32)
    cosine_row = cosines[None, :]
    offsets = jnp.arange(1, NT + 2).astype(jnp.float32)[:, None, None]
    degrees = order_f[None] + offsets
    factors = jnp.sqrt(
        (4.0 * degrees * degrees - 1.0) / (offsets * (2.0 * order_f[None] + offsets))
    )
    backwards = jnp.sqrt(
        (offsets - 1.0)
        * (2.0 * order_f[None] + offsets - 1.0)
        / (4.0 * (degrees - 1.0) * (degrees - 1.0) - 1.0)
    )
    inside_rows = degrees - 1.0 <= NT

    def advance(state_now, step_terms):
        current, previous, running_log = state_now
        factor, backward, inside = step_terms
        row_value = jnp.where(inside, current * jnp.exp(running_log), 0.0).astype(jnp.bfloat16)
        newest = factor * (cosine_row * current - backward * previous)
        oversize = jnp.abs(newest) > rescale_limit
        shrink = jnp.where(oversize, 1.0 / rescale_limit, 1.0)
        running_log = running_log + jnp.where(oversize, rescale_log, 0.0)
        newest = newest * shrink
        current = current * shrink
        return ((newest, current, running_log), row_value)

    final_state, every_row = lax.scan(
        advance,
        (start_row, jnp.zeros_like(start_row), scaled_log),
        (factors, backwards, inside_rows),
        unroll=8,
    )
    return every_row.reshape(((NT + 1) // 2, 2) + every_row.shape[1:])


def fourier_tables(counts, orders, blocks):
    inner_index = jnp.arange(128)
    block_start = jnp.arange(blocks) * 128
    periods = counts[:, None, None]
    inner_residue = inner_index[None, :, None] * orders[None, None, :] % periods
    block_residue = block_start[None, :, None] * orders[None, None, :] % periods
    period_f = periods.astype(jnp.float32)
    inner_angle = 2.0 * math.pi * inner_residue.astype(jnp.float32) / period_f
    block_angle = 2.0 * math.pi * block_residue.astype(jnp.float32) / period_f
    return (
        jnp.cos(inner_angle).astype(jnp.bfloat16),
        jnp.sin(inner_angle).astype(jnp.bfloat16),
        jnp.cos(block_angle),
        jnp.sin(block_angle),
    )


def analyse(grid_field, counts, orders, weights):
    blocks = PPAD // 128
    order_count = orders.shape[0]
    cos_inner, sin_inner, cos_outer, sin_outer = fourier_tables(counts, orders, blocks)
    inside = jnp.arange(PPAD)[None, :] < counts[:, None]
    masked = jnp.where(inside[:, None, :], grid_field, jnp.zeros((), jnp.bfloat16))
    shaped = masked.reshape(grid_field.shape[:-1] + (blocks, 128))
    dft_table = jnp.concatenate([cos_inner, -sin_inner], axis=-1)
    partial_sums = jnp.einsum(
        "vlshbk,skc->vlshbc", shaped, dft_table, preferred_element_type=jnp.float32
    )
    real_sums = partial_sums[..., :order_count]
    imag_sums = partial_sums[..., order_count:]
    outer_cos = cos_outer[:, None]
    outer_sin = sin_outer[:, None]
    period_f = counts.astype(jnp.float32)[:, None, None]
    real_coef = jnp.sum(outer_cos * real_sums + outer_sin * imag_sums, axis=-2) / period_f
    imag_coef = jnp.sum(outer_cos * imag_sums - outer_sin * real_sums, axis=-2) / period_f
    kept_mask = (2 * orders[None, :] < counts[:, None])[:, None, :]
    real_coef = jnp.where(kept_mask, real_coef, 0.0)
    imag_coef = jnp.where(kept_mask, imag_coef, 0.0)
    even_real = real_coef[:, :, :, 0] + real_coef[:, :, :, 1]
    even_imag = imag_coef[:, :, :, 0] + imag_coef[:, :, :, 1]
    odd_real = real_coef[:, :, :, 0] - real_coef[:, :, :, 1]
    odd_imag = imag_coef[:, :, :, 0] - imag_coef[:, :, :, 1]
    stacked = jnp.stack(
        [jnp.stack([even_real, even_imag], 2), jnp.stack([odd_real, odd_imag], 2)], 2
    )
    rounded = (weights[:, None] * stacked).astype(jnp.bfloat16)
    return jnp.swapaxes(rounded, 4, 5)


def synthesise(fourier_rows, counts, orders):
    fourier = jnp.swapaxes(fourier_rows, 4, 5)
    blocks = PPAD // 128
    cos_inner, sin_inner, cos_outer, sin_outer = fourier_tables(counts, orders, blocks)
    even_parts = fourier[:, :, 0].astype(jnp.float32)
    odd_parts = fourier[:, :, 1].astype(jnp.float32)
    hemispheres = jnp.stack([even_parts + odd_parts, even_parts - odd_parts], axis=3)
    kept_mask = 2 * orders[None, :] < counts[:, None]
    factor = jnp.where(orders == 0, 1.0, 2.0)
    hemispheres = jnp.where(kept_mask, hemispheres, 0.0) * factor
    real_hemisphere = jnp.moveaxis(hemispheres[:, :, 0], 3, 2)[..., None, :]
    imag_hemisphere = jnp.moveaxis(hemispheres[:, :, 1], 3, 2)[..., None, :]
    outer_cos = cos_outer[:, None]
    outer_sin = sin_outer[:, None]
    real_phase = outer_cos * real_hemisphere - outer_sin * imag_hemisphere
    imag_phase = outer_sin * real_hemisphere + outer_cos * imag_hemisphere
    stacked = jnp.concatenate([real_phase, imag_phase], axis=-1).astype(jnp.bfloat16)
    dft_table = jnp.concatenate([cos_inner, -sin_inner], axis=-1)
    values = jnp.einsum(
        "vlshbc,skc->vlshbk", stacked, dft_table, preferred_element_type=jnp.float32
    )
    flattened = values.reshape(values.shape[:4] + (PPAD,))
    inside = jnp.arange(PPAD)[None, :] < counts[:, None]
    return jnp.where(inside[:, None, :], flattened, 0.0).astype(jnp.bfloat16)


def add_terms(earlier, later):
    return earlier + later


def on_device(grid_field, coupling, points, lat_ids, wn_ids):
    orders, all_slots = (
        lax.all_gather(wn_ids, "band", axis=0, tiled=True),
        lax.all_gather(lat_ids, "band", axis=0, tiled=True),
    )
    counts = jnp.take(points, lat_ids)
    local_cos, local_sin = latitude_angles(lat_ids)
    weights = math.pi / (2.0 * NH) * local_sin
    coeffs = analyse(grid_field, counts, orders, weights)
    received = lax.all_to_all(coeffs, "band", split_axis=4, concat_axis=5, tiled=True)
    all_cos, all_sin = latitude_angles(all_slots)
    legendre_table = legendre_rows(wn_ids, all_cos, all_sin)
    spectral = jnp.einsum(
        "vlprmi,qpmi->vlprmq", received, legendre_table, preferred_element_type=jnp.float32
    )
    weighted = coupling[:, :, None, None, None, None] * spectral
    running = jnp.cumsum(weighted, axis=1)
    level_total = running[:, -1]
    earlier = carried_in(level_total, "fld", add_terms, jnp.zeros_like(level_total))
    damping_rows = jnp.transpose(damping(wn_ids), (1, 2, 0))[None, None, :, None, :, :]
    updated = (damping_rows * (spectral + earlier[:, None] + running - weighted)).astype(
        jnp.bfloat16
    )
    outgoing = jnp.einsum(
        "vlprmq,qpmi->vlprmi", updated, legendre_table, preferred_element_type=jnp.float32
    ).astype(jnp.bfloat16)
    fourier = lax.all_to_all(outgoing, "band", split_axis=5, concat_axis=4, tiled=True)
    return synthesise(fourier, counts, orders)


def solution(mesh):
    in_specs = (P(None, "fld", "band", None, None), P(None, "fld"), P(), P("band"), P("band"))
    out_specs = P(None, "fld", "band", None, None)
    return jax.shard_map(
        on_device, mesh=mesh, in_specs=in_specs, out_specs=out_specs, check_vma=False
    )
```

profile of v0, /device:TPU:0, one launch (start us, length us, event | category | flops | bytes accessed | tf_op | source)
XLA Modules:
  0.0 945.1 jit_solution(17061320564376272332)
XLA Ops:
  0.7 1.1 gather_fusion
  2.6 1.2 dynamic-slice
  5.1 0.9 dynamic-update-slice.1
  6.0 0.8 dynamic-update-slice
  6.8 14.1 %all-reduce.2 = (s32[1280]{0:T(1024)S(1)}, s32[128]{0:T(128)S(1)}) all-reduce(s32[1280]{0:T(1024)S(1)} %dynamic-update-slice.1, s32[128]{0:T(128)S(1)} %dynamic-update-slice), channel_id=1, replica_groups=mesh['band'=16,'fld'=2] {'band'}, use_global_device_ids=true, to_apply=%add.1 | all-reduce | flops 1408 | bytes 11264
  21.0 68.9 %cosine_convert_fusion = bf16[80,128,128]{2,1,0:T(8,128)(2,1)} fusion(f32[80]{0:T(128)S(1)} %convert_element_type.160, pred[80]{0:T(512)(128)(4,1)S(1)} %compare_bitcast_fusion, s32[80]{0:T(128)S(1)} %get-tuple-element.179, s32[128,128]{1,0:T(8,128)S(1)} %multiply_bitcast_fusion), kind=kLoop, calls=%fused_computation.156 | loop fusion | flops 14417920 | bytes 2687696 | tf_op jit(solution)/shard_map/convert_element_type | solution.py:92
  89.8 69.3 %fusion.73 = bf16[80,128,128]{2,1,0:T(8,128)(2,1)} fusion(f32[80]{0:T(128)S(1)} %convert_element_type.160, pred[80]{0:T(512)(128)(4,1)S(1)} %compare_bitcast_fusion, s32[80]{0:T(128)S(1)} %get-tuple-element.179, s32[128,128]{1,0:T(8,128)S(1)} %multiply_bitcast_fusion), kind=kLoop, calls=%fused_computation.163 | loop fusion | flops 18350080 | bytes 2687696 | tf_op jit(solution)/shard_map/neg | solution.py:148
  159.5 7.6 copy_select_fusion.1
  167.1 11.7 %reshape.556 = bf16[2,2,80,2,41,128]{5,4,2,3,1,0:T(8,128)(2,1)} reshape(bf16[2,2,80,2,5248]{4,2,3,1,0:T(8,128)(2,1)} %copy_select_fusion.1) | data formatting | bytes 13434880 | tf_op jit(solution)/shard_map/reshape | solution.py:105
  178.9 27.8 %fusion.90 = (f32[80,41,128]{2,1,0:T(8,128)S(1)}, f32[80,41,128]{2,1,0:T(8,128)}) fusion(f32[80]{0:T(128)S(1)} %convert_element_type.160, pred[80]{0:T(512)(128)(4,1)S(1)} %compare_bitcast_fusion, s32[80]{0:T(128)S(1)} %get-tuple-element.179, s32[41,128]{1,0:T(8,128)S(1)} %multiply_bitcast_fusion.1), kind=kLoop, calls=%fused_computation.176 | loop fusion | flops 4198400 | bytes 3380432 | tf_op jit(solution)/shard_map/cos | solution.py:94
  206.8 15.3 %convolution_bitcast_fusion = f32[2,2,80,2,41,256]{5,4,3,1,0,2:T(8,128)} fusion(bf16[2,2,80,2,41,128]{5,4,2,3,1,0:T(8,128)(2,1)} %reshape.556, bf16[80,128,128]{2,1,0:T(8,128)(2,1)} %fusion.73, bf16[80,128,128]{2,1,0:T(8,128)(2,1)} %cosine_convert_fusion), kind=kOutput, calls=%fused_computation.143 | convolution fusion | flops 1730150400 | bytes 38830080 | tf_op jit(solution)/shard_map/vlshbk,skc->vlshbc/dot_general | solution.py:107
  222.1 13.3 %add_reduce_fusion = (f32[2,2,80,2,128]{4,3,1,0,2:T(2,128)S(1)}, f32[2,2,80,2,128]{4,3,1,0,2:T(2,128)S(1)}) fusion(f32[2,2,80,2,41,256]{5,4,3,1,0,2:T(8,128)} %convolution_bitcast_fusion, f32[80,41,128]{2,1,0:T(8,128)} %get-tuple-element.226, f32[80,41,128]{2,1,0:T(8,128)S(1)} %get-tuple-element.225), kind=kLoop, calls=%fused_computation.140 | loop fusion | flops 26705920 | bytes 30883840 | tf_op jit(solution)/shard_map/reduce_sum | solution.py:115
  237.1 2.0 copy.124
  239.1 3.7 all-to-all-start
  243.4 1.1 copy.112
  244.5 1.1 copy.113
  245.6 2.0 copy.114
  247.6 524.3 %while.28 = (s32[]{:T(128)}, f32[8,1280]{1,0:T(8,128)S(1)}, f32[8,1280]{1,0:T(8,128)S(1)}, f32[8,1280]{1,0:T(8,128)S(1)}, bf16[160,8,8,1280]{3,2,1,0:T(8,128)(2,...) while((s32[]{:T(128)}, f32[8,1280]{1,0:T(8,128)S(1)}, ...), condition=%wide.region_2.5_spmd.clone, body=%wide.region_1.4_spmd.clone.sunk | while | flops 2754569 | bytes 1978075 | solution.py:73
  258.3 0.8 fusion.130
  271.3 0.8 fusion.130
  336.9 0.8 fusion.130
  405.7 0.8 fusion.130
  451.6 0.8 fusion.130
  454.9 0.8 fusion.130
  602.4 0.8 fusion.130
  618.8 0.8 fusion.130
  648.3 0.8 fusion.130
  772.3 1.6 all_to_all.29
  773.9 22.5 %fusion.85 = f32[2,2,2,2,8,640]{5,3,1,0,4,2:T(2,128)S(1)} fusion(bf16[2,2,2,2,8,1280]{5,3,1,0,4,2:T(2,128)(2,1)} %all_to_all.29, bf16[640,2,8,1280,1,1]{3,2,1,0,5,4:T(8,128)(2,1)} %bitcast.216), kind=kOutput, calls=%fused_computation.172 | convolution fusion | flops 209715200 | bytes 26869760 | tf_op jit(solution)/shard_map/vlprmi,qpmi->vlprmq/dot_general | solution.py:173
  796.7 5.4 all-gather
  802.2 18.4 %fusion.77 = bf16[2,2,2,2,8,1280]{5,3,1,0,4,2:T(2,128)(2,1)} fusion(bf16[640,2,8,1280,1,1]{3,2,1,0,5,4:T(8,128)(2,1)} %bitcast.217, f32[2,2,2,2,8,640]{5,3,1,0,4,2:T(2,128)S(1)} %fusion.96, f32[2,2,2,2,8,640]{5,3,1,0,4,2:T(2,128)S(1)} %fusion.85, f32[2,2,2,8,640]{4,2,0,3,1:T(2,128)S(1)} %copy.129, f32[2,2]{1,0:T(2,128)S(1)} %copy-done.2, ...), kind=kOutput, calls=%fused_computation.165 | convolution fusion | flops 210370560 | bytes 27402256 | tf_op jit(solution)/shard_map/vlprmq,qpmi->vlprmi/dot_general | solution.py:184
  820.6 10.4 %copy.131 = bf16[2,2,2,2,8,1280]{4,3,2,1,0,5:T(2,128)(2,1)} copy(bf16[2,2,2,2,8,1280]{5,3,1,0,4,2:T(2,128)(2,1)} %fusion.77) | data formatting | bytes 655360 | tf_op jit(solution)/shard_map/convert_element_type | solution.py:186
  831.0 15.5 %reshape.584 = bf16[16,2,5120]{2,1,0:T(2,128)(2,1)} reshape(bf16[1280,2,2,2,2,8]{5,4,3,2,1,0:T(2,128)(2,1)} %bitcast.206) | data formatting | bytes 655360
  846.5 6.1 all-to-all-start.1
  852.7 10.9 %all-to-all-done.1 = bf16[16,2,5120]{2,1,0:T(2,128)(2,1)S(1)} async-done(((bf16[16,2,5120]{2,1,0:T(2,128)(2,1)}), bf16[16,2,5120]{2,1,0:T(2,128)(2,1)S(1)}, u32[]{:S(2)}, u32[]{:S(2)}) %all-to-all-start.1) | async-done | bytes 327712 | tf_op jit(solution)/shard_map/all_to_all | solution.py:187
  863.6 7.2 reshape.585
  870.8 9.5 %copy.132 = bf16[2,2,2,2,8,16,80]{6,4,5,3,2,1,0:T(8,128)(2,1)S(1)} copy(bf16[2,2,2,2,8,16,80]{4,3,2,1,0,6,5:T(2,128)(2,1)} %bitcast.204) | data formatting | bytes 655360 | tf_op jit(solution)/shard_map/all_to_all | solution.py:187
  880.3 10.6 %copy.147 = bf16[2,2,2,2,8,16,80]{6,4,5,3,1,0,2:T(8,128)(2,1)} copy(bf16[2,2,2,2,8,16,80]{4,3,2,1,0,6,5:T(2,128)(2,1)} %bitcast.205) | data formatting | bytes 655360 | tf_op jit(solution)/shard_map/transpose | solution.py:132
  890.9 1.0 fusion.92
  891.9 1.0 fusion.93
  893.1 0.9 slice_bitcast_fusion.1
  894.0 1.3 copy.136
  895.3 0.9 copy.137
  896.2 8.6 subtract_convert_fusion
  904.8 11.2 %fusion.64 = bf16[2,2,80,2,41,128]{5,4,3,1,0,2:T(8,128)(2,1)} fusion(bf16[2,2,80,2,41,128]{5,4,3,1,0,2:T(8,128)(2,1)} %get-tuple-element.217, bf16[2,2,80,2,41,128]{5,4,3,1,0,2:T(8,128)(2,1)} %get-tuple-element.216, bf16[80,128,128]{2,1,0:T(8,128)(2,1)} %fusion.73, bf16[80,128,128]{2,1,0:T(8,128)(2,1)} %cosine_convert_fusion), kind=kOutput, calls=%fused_computation.148 | convolution fusion | flops 1757020160 | bytes 25395200 | tf_op jit(solution)/shard_map/vlshbc,skc->vlshbk/dot_general | solution.py:149
  916.0 14.4 %reshape.582 = bf16[2,2,80,2,5248]{4,3,1,0,2:T(2,128)(2,1)} reshape(bf16[2,2,80,2,41,128]{5,4,3,1,0,2:T(8,128)(2,1)} %fusion.64) | data formatting | bytes 13434880 | tf_op jit(solution)/shard_map/reshape | solution.py:152
  930.5 4.1 fusion.63
  934.6 10.1 %copy.139 = bf16[2,2,80,2,5248]{4,3,2,1,0:T(2,128)(2,1)} copy(bf16[2,2,80,2,5248]{4,2,3,1,0:T(8,128)(2,1)S(1)} %fusion.63) | data formatting | bytes 13434880 | tf_op jit(solution)/shard_map/convert_element_type | solution.py:154
  (2131 shorter events, 514.0 us)
Async XLA Ops:
  0.0 0.7 copy-start
  0.0 159.5 %copy-start.3 = (s32[80]{0:T(128)S(1)}, s32[80]{0:T(128)}, u32[]{:S(2)}) copy-start(s32[80]{0:T(128)} %param.16) | copy-start | bytes 964
  235.4 7.4 copy-start.4
  239.1 533.0 %all-to-all-start = ((bf16[2,2,2,2,128,80]{5,3,2,1,0,4:T(2,128)(2,1)}), bf16[2,2,2,2,128,80]{5,3,2,1,0,4:T(2,128)(2,1)S(1)}, u32[]{:S(2)}, u32[]{:S(2)}) async-start(bf16[2,2,2,2,128,80]{5,3,2,1,0,4:T(2,128)(2,1)} %copy.124), calls=%async_computation | async-start | bytes 1048576 | tf_op jit(solution)/shard_map/all_to_all | solution.py:170
  773.9 22.6 %copy-start.2 = (f32[2,2]{1,0:T(2,128)S(1)}, f32[2,2]{1,0:T(2,128)}, u32[]{:S(2)}) copy-start(f32[2,2]{1,0:T(2,128)} %param.14) | copy-start | bytes 52
  846.5 17.1 %all-to-all-start.1 = ((bf16[16,2,5120]{2,1,0:T(2,128)(2,1)}), bf16[16,2,5120]{2,1,0:T(2,128)(2,1)S(1)}, u32[]{:S(2)}, u32[]{:S(2)}) async-start(bf16[16,2,5120]{2,1,0:T(2,128)(2,1)} %reshape.584), calls=%async_computation.1 | async-start | bytes 655360 | tf_op jit(solution)/shard_map/all_to_all | solution.py:187
  930.4 14.2 %copy-start.1 = (s32[1280]{0:T(1024)S(1)}, s32[1280]{0:T(1024)}, u32[]{:S(2)}) copy-start(s32[1280]{0:T(1024)} %param.15) | copy-start | bytes 15364
where the time goes:
time: 957 us; the launch traced here: 945 us
  local copies, waits for them, and re-layouts  458 us (48%)
  other arithmetic  370 us (39%)
  matrix products  67.4 us (7%)
  blocking collectives  19.5 us (2%)
  waiting for transfers between devices  10.9 us (1%)
  starting transfers between devices  9.8 us (1%)
    mul x160, local copies, waits for them, and re-layouts, advance(): newest = factor * (cosine_row * current - backward * previous)  128 us
    while x1120, other arithmetic  119 us
    broadcast_in_dim x160, local copies, waits for them, and re-layouts, advance(): jnp.where(inside, current * jnp.exp(running_log), 0.0).astype(jnp.bfloat16)  115 us
    dynamic_update_slice x160, local copies, waits for them, and re-layouts, legendre_rows(): lax.scan(advance, (start_row, jnp.zeros_like(start_row), scaled_log), (fa...  109 us
    neg x1, other arithmetic, synthesise(): dft_table = jnp.concatenate([cos_inner, -sin_inner], axis=-1)  69.3 us
    convert_element_type x1, other arithmetic, fourier_tables(): jnp.cos(inner_angle).astype(jnp.bfloat16)  68.9 us
    unnamed x20, local copies, waits for them, and re-layouts  29.8 us
    cos x1, other arithmetic, fourier_tables(): jnp.cos(block_angle)  27.8 us
  transfers between devices with their start and end apart: 2, of which 1 were waited for; matrix products, arithmetic and copies ran while one was open for 55% of the time, Pallas kernels for 0%

commit v1 on v0

v1 whole, which is shorter than its diff:
```python
import math

import jax
import jax.numpy as jnp
from jax import lax
from jax.experimental import pallas as pl
from jax.experimental.pallas import tpu as pltpu
from jax.sharding import PartitionSpec as P

NT = 1279
NH = 1280
BF = jnp.bfloat16
F32 = jnp.float32
GROUP = 8
STEPS = 32
CHECK = 8
RESCALE_LOG = 60.0 * math.log(2.0)


def iota(shape, dim):
    return lax.broadcasted_iota(jnp.int32, shape, dim)


def turn_cos_sin(turns):
    x = turns * math.pi
    y = x * x
    s = 1.0 / 362880 - y * (1.0 / 39916800)
    s = -1.0 / 5040 + y * s
    s = 1.0 / 120 + y * s
    s = -1.0 / 6 + y * s
    s = x * (1.0 + y * s)
    c = -1.0 / 3628800 + y * (1.0 / 479001600)
    c = 1.0 / 40320 + y * c
    c = -1.0 / 720 + y * c
    c = 1.0 / 24 + y * c
    c = -0.5 + y * c
    c = 1.0 + y * c
    return 1.0 - 2.0 * s * s, 2.0 * s * c


def block_transpose(planes):
    lane = iota((1, 128), 1) // 8
    planes = list(planes)
    for bit in (8, 4, 2, 1):
        low = (lane & bit) == 0
        for at in range(16):
            if at & bit:
                continue
            a, b = planes[at], planes[at | bit]
            planes[at] = jnp.where(low, a, pltpu.roll(b, 8 * bit, 1))
            planes[at | bit] = jnp.where(low, pltpu.roll(a, 128 - 8 * bit, 1), b)
    return planes


def window(i, rows):
    start = i * rows
    base = start // 16 * 16
    return base, start - base


def analyse(grid_field, points, lat_ids, weights, orders, coupling):
    nv, nl, slots, _, width = grid_field.shape
    fields = nv * nl
    blocks = width // 128
    rows = 2 * blocks
    span = -(-(rows + 14) // 16) * 16
    tiles = span // 8
    count = orders.shape[1]
    bands = count // 8
    half = slots // 2
    grid = slots // GROUP
    field = grid_field.reshape(fields, slots, 2, width)

    def kernel(points_ref, lat_ref, weight_ref, coupling_ref, x_ref, order_ref, own_ref, sum_ref, table_ref, phase_ref, staged, planes):
        step = pl.program_id(0)
        for b in range(blocks):
            staged[:, :, b] = x_ref[..., b * 128 : (b + 1) * 128]
        flat = staged.reshape(fields, GROUP * rows, 128)
        order = order_ref[...]
        position = 128 * (iota((span, 128), 0) // 2) + iota((span, 128), 1)
        r8 = iota((8, count), 0)
        r16 = iota((16, count), 0)
        for i in range(GROUP):
            base, off = window(i, rows)
            slot = step * GROUP + i
            period = points_ref[lat_ref[slot]]
            period_v = jnp.full((1, count), period, jnp.int32).astype(F32)
            inverse = 1.0 / period_v
            multiple = jnp.concatenate([8 * r16, r8, 512 * r16, 128 * (r8 // 2 - off // 2)], axis=0).astype(F32)
            product = multiple * order
            turns = (product - jnp.floor(product * inverse + 0.5) * period_v) * inverse
            cosv, sinv = turn_cos_sin(turns)
            fc, fs = cosv[16:24], sinv[16:24]
            parts_c, parts_s = [], []
            for a in range(16):
                ec, es = cosv[a : a + 1], sinv[a : a + 1]
                parts_c.append(ec * fc - es * fs)
                parts_s.append(-(es * fc) - ec * fs)
            table = jnp.concatenate([jnp.concatenate(parts_c, 0), jnp.concatenate(parts_s, 0)], axis=1).astype(BF)
            table_ref[i] = table
            phase_ref[i] = jnp.concatenate([cosv[24:48], sinv[24:48]], axis=1)
            place = position - 64 * off
            keep = jnp.where((place >= 0) & (place < period), 1.0, 0.0).astype(BF)
            data = jnp.concatenate([flat[f, base : base + span, :] * keep for f in range(fields)], axis=0)
            sums = jnp.dot(data, table, preferred_element_type=F32)
            hc, hs = cosv[40:48], sinv[40:48]
            re = [jnp.zeros((8, count), F32) for _ in range(fields)]
            im = [jnp.zeros((8, count), F32) for _ in range(fields)]
            for t in range(tiles):
                gc, gs = cosv[24 + t : 25 + t], sinv[24 + t : 25 + t]
                pc = gc * hc - gs * hs
                ps = gs * hc + gc * hs
                for f in range(fields):
                    at = f * span + 8 * t
                    yr = sums[at : at + 8, :count]
                    yi = sums[at : at + 8, count:]
                    re[f] = re[f] + (pc * yr + ps * yi)
                    im[f] = im[f] + (pc * yi - ps * yr)
            factor = jnp.where(2.0 * order < period_v, weight_ref[slot] * inverse, 0.0)
            for f in range(fields):
                for ri, acc in ((0, re[f]), (1, im[f])):
                    acc = acc + pltpu.roll(acc, 2, 0)
                    acc = acc + pltpu.roll(acc, 4, 0)
                    other = pltpu.roll(acc, 1, 0)
                    planes[2 * f + ri, pl.ds(slot, 1), :] = ((acc + other)[0:1] * factor)
                    planes[2 * fields + 2 * f + ri, pl.ds(slot, 1), :] = ((acc - other)[0:1] * factor)

        @pl.when(step == grid - 1)
        def _():
            for tile in range(count // 128):
                lanes = slice(128 * tile, 128 * tile + 128)
                value = [planes[k, :, lanes].astype(BF).astype(F32) for k in range(16)]
                own, totals = [None] * 16, [None] * 8
                for p in range(2):
                    for v in range(nv):
                        for ri in range(2):
                            running = None
                            for l in range(nl):
                                at = ((p * nv + v) * nl + l) * 2 + ri
                                own[at] = value[at] if running is None else value[at] + running
                                term = coupling_ref[v, l] * value[at]
                                running = term if running is None else running + term
                            totals[(p * nv + v) * 2 + ri] = running
                for d, w in enumerate(block_transpose(own)):
                    own_ref[16 * tile + d] = w.astype(BF)
                packed = [t[:half] for t in totals] + [t[half:] for t in totals]
                for d, w in enumerate(block_transpose(packed)):
                    sum_ref[16 * tile + d] = w.astype(BF)

    smem = pl.BlockSpec(memory_space=pltpu.SMEM)
    return pl.pallas_call(
        kernel,
        name="analyse",
        grid=(grid,),
        in_specs=[
            smem,
            smem,
            smem,
            smem,
            pl.BlockSpec((fields, GROUP, 2, width), lambda i: (0, i, 0, 0)),
            pl.BlockSpec((1, count), lambda i: (0, 0)),
        ],
        out_specs=[
            pl.BlockSpec((bands, slots, 128), lambda i: (0, 0, 0)),
            pl.BlockSpec((bands, half, 128), lambda i: (0, 0, 0)),
            pl.BlockSpec((GROUP, 128, 2 * count), lambda i: (i, 0, 0)),
            pl.BlockSpec((GROUP, 24, 2 * count), lambda i: (i, 0, 0)),
        ],
        out_shape=[
            jax.ShapeDtypeStruct((bands, slots, 128), BF),
            jax.ShapeDtypeStruct((bands, half, 128), BF),
            jax.ShapeDtypeStruct((slots, 128, 2 * count), BF),
            jax.ShapeDtypeStruct((slots, 24, 2 * count), F32),
        ],
        scratch_shapes=[
            pltpu.VMEM((fields, GROUP, blocks, 2, 128), BF),
            pltpu.VMEM((16, slots, count), F32),
        ],
        compiler_params=pltpu.CompilerParams(dimension_semantics=("arbitrary",)),
    )(points, lat_ids, weights, coupling, field, orders)


def legendre(pairs, own, earlier, cosines, start_log, ahead, behind, order_rows, nv, nl):
    bands, slots, _ = own.shape
    half = slots // 2
    total = bands * slots
    chunk = total // 2
    height = 8 * STEPS

    def kernel(pairs_ref, own_ref, earlier_ref, cos_ref, log_ref, ahead_ref, behind_ref, order_ref, out_ref, mixed, weights, even_rows, odd_rows, acc, now, before, log_now):
        source, target = iota((128, 128), 0), iota((128, 128), 1)
        span_l = 16 * nl
        wanted = target // span_l * 16 + target % 16
        pick0 = jnp.where(source == wanted, 1.0, 0.0).astype(BF)
        pick1 = jnp.where(source == wanted + 64, 1.0, 0.0).astype(BF)
        for b in range(bands):
            part = earlier_ref[b]
            top = jnp.dot(part, pick0, preferred_element_type=F32)
            low = jnp.dot(part, pick1, preferred_element_type=F32)
            mixed[b * slots : (b + 1) * slots] = own_ref[b].astype(F32) + jnp.concatenate([top, low], axis=0)
        weights[...] = mixed[...].astype(BF)
        acc[...] = jnp.zeros((128, total), F32)
        now[...] = jnp.ones((8, total), F32)
        before[...] = jnp.zeros((8, total), F32)
        log_now[...] = log_ref[...]
        row, lane = iota((height, 128), 0), iota((height, 128), 1)
        select = (row % 8 == lane % 8) & (row // 8 % 2 == lane // 64)
        degree_base = jnp.concatenate([order_ref[...]] * STEPS, axis=0) + (row // 8).astype(F32)

        def make(block, rows_ref):
            a_all = ahead_ref[block]
            b_all = behind_ref[block]
            for h in range(total // chunk):
                lanes = slice(h * chunk, (h + 1) * chunk)
                current, previous, running = now[:, lanes], before[:, lanes], log_now[:, lanes]
                cosine = cos_ref[:, lanes]
                scale = None
                held = None
                for j in range(STEPS):
                    if j % CHECK == 0:
                        large = jnp.maximum(jnp.abs(current), jnp.abs(previous)) > 1.0
                        shrink = jnp.where(large, 2.0**-60, 1.0)
                        running = running + jnp.where(large, RESCALE_LOG, 0.0)
                        current = current * shrink
                        previous = previous * shrink
                        scale = jnp.exp(running)
                    value = current * scale
                    if j % 2 == 0:
                        held = value
                    else:
                        rows_ref[8 * (j - 1) : 8 * (j + 1), lanes] = jnp.concatenate([held, value], axis=0).astype(BF)
                    a = a_all[:, j : j + 1]
                    b = b_all[:, j : j + 1]
                    current, previous = (a * cosine) * current - b * previous, current
                now[:, lanes] = current
                before[:, lanes] = previous
                log_now[:, lanes] = running

        def use(block, rows_ref):
            rows = rows_ref[...]
            found = jnp.dot(rows, weights[...], preferred_element_type=F32)
            degree = degree_base + (block * STEPS).astype(F32)
            damp = 1.0 / (1.0 + 4.0 * degree * (degree + 1.0) / (NT * (NT + 1.0)))
            kept = jnp.where(select, found * damp, 0.0).astype(BF)
            acc[...] += lax.dot_general(kept, rows, (((0,), (0,)), ((), ())), preferred_element_type=F32)

        make(0, even_rows)

        def body(i, carry):
            make(2 * i + 1, odd_rows)
            use(2 * i, even_rows)
            make(2 * i + 2, even_rows)
            use(2 * i + 1, odd_rows)
            return carry

        lax.fori_loop(0, pairs_ref[0], body, 0)
        for c in range(total // 128):
            mixed[128 * c : 128 * (c + 1)] = jnp.transpose(acc[:, 128 * c : 128 * (c + 1)])
        for b in range(bands):
            out_ref[b] = mixed[b * slots : (b + 1) * slots].astype(BF)

    vmem = pl.BlockSpec(memory_space=pltpu.VMEM)
    return pl.pallas_call(
        kernel,
        name="legendre",
        in_specs=[pl.BlockSpec(memory_space=pltpu.SMEM)] + [vmem] * 7,
        out_specs=vmem,
        out_shape=jax.ShapeDtypeStruct((bands, slots, 128), BF),
        scratch_shapes=[
            pltpu.VMEM((total, 128), F32),
            pltpu.VMEM((total, 128), BF),
            pltpu.VMEM((height, total), BF),
            pltpu.VMEM((height, total), BF),
            pltpu.VMEM((128, total), F32),
            pltpu.VMEM((8, total), F32),
            pltpu.VMEM((8, total), F32),
            pltpu.VMEM((8, total), F32),
        ],
    )(pairs, own, earlier, cosines, start_log, ahead, behind, order_rows)


def synthesise(back, table, phases, points, lat_ids, orders, nv, nl, width):
    bands, slots, _ = back.shape
    fields = nv * nl
    blocks = width // 128
    rows = 2 * blocks
    span = -(-(rows + 14) // 16) * 16
    tiles = span // 8
    count = orders.shape[1]
    grid = slots // GROUP

    def kernel(points_ref, lat_ref, back_ref, table_ref, phase_ref, order_ref, out_ref, planes, waves, staged):
        step = pl.program_id(0)
        result = staged.reshape(fields, GROUP * rows, 128)

        @pl.when(step == 0)
        def _():
            for tile in range(count // 128):
                value = [back_ref[16 * tile + d].astype(F32) for d in range(16)]
                for k, w in enumerate(block_transpose(value)):
                    planes[k, :, 128 * tile : 128 * tile + 128] = w

        order = order_ref[...]
        position = 128 * (iota((span, 128), 0) // 2) + iota((span, 128), 1)
        sign = jnp.where(iota((8, count), 0) % 2 == 0, 1.0, -1.0)
        row8 = iota((8, count), 0)
        for i in range(GROUP):
            base, off = window(i, rows)
            slot = step * GROUP + i
            period = points_ref[lat_ref[slot]]
            period_v = jnp.full((1, count), period, jnp.int32).astype(F32)
            factor = jnp.where(2.0 * order < period_v, jnp.where(order == 0.0, 1.0, 2.0), 0.0)
            hc, hs = phase_ref[i, 16:24, :count], phase_ref[i, 16:24, count:]
            re, im = [], []
            for f in range(fields):
                for ri, keep in ((0, re), (1, im)):
                    even = planes[2 * f + ri, pl.ds(slot, 1), :] * factor
                    odd = planes[2 * fields + 2 * f + ri, pl.ds(slot, 1), :] * factor
                    keep.append(even + sign * odd)
            for t in range(0, tiles, 2):
                pair = []
                for u in (t, t + 1):
                    gc, gs = phase_ref[i, u : u + 1, :count], phase_ref[i, u : u + 1, count:]
                    pc = gc * hc - gs * hs
                    ps = gs * hc + gc * hs
                    if 8 * u < off or 8 * u + 8 > off + rows:
                        valid = (row8 + 8 * u >= off) & (row8 + 8 * u < off + rows)
                        pc = jnp.where(valid, pc, 0.0)
                        ps = jnp.where(valid, ps, 0.0)
                    pair.append((pc, ps))
                for f in range(fields):
                    zr = jnp.concatenate([pc * re[f] - ps * im[f] for pc, ps in pair], axis=0)
                    zi = jnp.concatenate([ps * re[f] + pc * im[f] for pc, ps in pair], axis=0)
                    at = f * span + 8 * t
                    waves[at : at + 16, :count] = zr.astype(BF)
                    waves[at : at + 16, count:] = zi.astype(BF)
            values = lax.dot_general(waves[...], table_ref[i], (((1,), (1,)), ((), ())), preferred_element_type=F32)
            inside = position - 64 * off < period
            for f in range(fields):
                part = jnp.where(inside, values[f * span : (f + 1) * span], 0.0)
                if off:
                    first = part[:16] + result[f, base : base + 16, :].astype(F32)
                    result[f, base : base + 16, :] = first.astype(BF)
                    result[f, base + 16 : base + span, :] = part[16:].astype(BF)
                else:
                    result[f, base : base + span, :] = part.astype(BF)
        for b in range(blocks):
            out_ref[..., b * 128 : (b + 1) * 128] = staged[:, :, b]

    smem = pl.BlockSpec(memory_space=pltpu.SMEM)
    out = pl.pallas_call(
        kernel,
        name="synthesise",
        grid=(grid,),
        in_specs=[
            smem,
            smem,
            pl.BlockSpec((bands, slots, 128), lambda i: (0, 0, 0)),
            pl.BlockSpec((GROUP, 128, 2 * count), lambda i: (i, 0, 0)),
            pl.BlockSpec((GROUP, 24, 2 * count), lambda i: (i, 0, 0)),
            pl.BlockSpec((1, count), lambda i: (0, 0)),
        ],
        out_specs=pl.BlockSpec((fields, GROUP, 2, width), lambda i: (0, i, 0, 0)),
        out_shape=jax.ShapeDtypeStruct((fields, slots, 2, width), BF),
        scratch_shapes=[
            pltpu.VMEM((16, slots, count), F32),
            pltpu.VMEM((fields * span, 2 * count), BF),
            pltpu.VMEM((fields, GROUP, blocks, 2, 128), BF),
        ],
        compiler_params=pltpu.CompilerParams(dimension_semantics=("arbitrary",)),
    )(points, lat_ids, back, table, phases, orders)
    return out.reshape(nv, nl, slots, 2, width)


def recurrence_terms(orders):
    order = orders.astype(F32)[None, :, None]
    blocks = 2 * (-(-(NT + 1) // (2 * STEPS))) + 1
    offset = (jnp.arange(blocks)[:, None] * STEPS + jnp.arange(STEPS)[None, :] + 1).astype(F32)[:, None, :]
    degree = order + offset
    ahead = jnp.sqrt((4.0 * degree * degree - 1.0) / (offset * (2.0 * order + offset)))
    below = 4.0 * (degree - 1.0) * (degree - 1.0) - 1.0
    behind = jnp.sqrt(jnp.maximum((offset - 1.0) * (2.0 * order + offset - 1.0) / below, 0.0))
    ahead = jnp.where(degree <= NT, ahead, 0.0)
    return ahead, ahead * behind


def solution(mesh):
    bands, parts = mesh.shape["band"], mesh.shape["fld"]

    def on_device(grid_field, coupling, points, lat_ids, wn_ids):
        nv, nl, slots, _, width = grid_field.shape
        mine = wn_ids.shape[0]
        packed = jnp.concatenate([wn_ids, lat_ids])
        spread = jnp.broadcast_to(packed[None], (bands, mine + slots))
        known = lax.all_to_all(spread, "band", split_axis=0, concat_axis=0, tiled=True)
        orders = known[:, :mine].reshape(1, bands * mine).astype(F32)
        lats = known[:, mine:].reshape(1, bands * slots).astype(F32)
        weights = math.pi / (2.0 * NH) * jnp.sin(math.pi * (lat_ids.astype(F32) + 0.5) / (2.0 * NH))
        own, sums, table, phases = analyse(grid_field, points, lat_ids, weights, orders, coupling)
        earlier = jnp.zeros_like(sums)
        for shift in range(1, parts):
            moved = lax.ppermute(sums, "fld", [(k, k + shift) for k in range(parts - shift)])
            earlier = moved if shift == 1 else earlier + moved
        own = lax.all_to_all(own, "band", split_axis=0, concat_axis=0, tiled=True)
        earlier = lax.all_to_all(earlier, "band", split_axis=0, concat_axis=0, tiled=True)
        colatitude = math.pi * (lats + 0.5) / (2.0 * NH)
        order = wn_ids.astype(F32)[:, None]
        index = jnp.arange(1, NT + 1).astype(F32)
        log_norm = 0.5 * math.log(0.5) + 0.5 * jnp.sum(
            jnp.where(index[None, :] <= order, jnp.log1p(0.5 / index)[None, :], 0.0), axis=1
        )
        start_log = log_norm[:, None] + order * jnp.log(jnp.sin(colatitude))
        cosines = jnp.broadcast_to(jnp.cos(colatitude), (mine, bands * slots))
        ahead, behind = recurrence_terms(wn_ids)
        longest = NT + 1 - jnp.min(wn_ids)
        pairs = ((longest + 2 * STEPS - 1) // (2 * STEPS)).reshape(1).astype(jnp.int32)
        order_rows = jnp.broadcast_to(order, (mine, 128))
        back = legendre(pairs, own, earlier, cosines, start_log, ahead, behind, order_rows, nv, nl)
        back = lax.all_to_all(back, "band", split_axis=0, concat_axis=0, tiled=True)
        return synthesise(back, table, phases, points, lat_ids, orders, nv, nl, width)

    in_specs = (P(None, "fld", "band", None, None), P(None, "fld"), P(), P("band"), P("band"))
    return jax.shard_map(on_device, mesh=mesh, in_specs=in_specs, out_specs=in_specs[0], check_vma=False)
```

time: 957 us -> 137 us (0.14); the launches traced: 945 us -> 136 us
  local copies, waits for them, and re-layouts: 458 us -> 2.7 us
  other arithmetic: 370 us -> 6.3 us
  matrix products: 67.4 us -> 0 us
  Pallas kernels: 0 us -> 57.2 us
  waiting for transfers between devices: 10.9 us -> 22.5 us
    mul x160 -> x0, local copies, waits for them, and re-layouts: 128 us -> none  [advance(): newest = factor * (cosine_row * current - backward * previous)]
    while x1120 -> x0, other arithmetic: 119 us -> none
    broadcast_in_dim x162 -> x3, local copies, waits for them, and re-layouts: 115 us -> 1.91 us  [the longest x1 0.69 us: on_device(): order_rows = jnp.broadcast_to(order, (mine, 128))]
    dynamic_update_slice x160 -> x0, local copies, waits for them, and re-layouts: 109 us -> none  [legendre_rows(): lax.scan(advance, (start_row, jnp.zeros_like(start_row), scaled_log), (fa...]
    convert_element_type x7 -> x4, other arithmetic: 73 us -> 1.5 us  [the longest x1 1.42 us: on_device(): order = wn_ids.astype(F32)[:, None]]
    neg x1 -> x0, other arithmetic: 69.3 us -> none  [synthesise(): dft_table = jnp.concatenate([cos_inner, -sin_inner], axis=-1)]
    dot_general x4 -> x0, matrix products: 67.4 us -> none  [the longest x1 22.5 us: on_device(): jnp.einsum('vlprmi,qpmi->vlprmq', received, legendre_table, preferred_ele...]
    pallas_call x0 -> x3, Pallas kernels: none -> 57.2 us  [the longest x1 21.2 us: analyse(): pl.pallas_call(kernel, name='analyse', grid=(grid,), in_specs=[smem, smem...]
  transfers between devices with their start and end apart: 2 -> 4, of which waited for: 1 -> 4; matrix products, arithmetic and copies ran while one was open for 55% -> 4% of each run, Pallas kernels for 0% -> 0%
where the time goes in v1:
time: 137 us; the launch traced here: 136 us
  Pallas kernels  57.2 us (42%)
  blocking collectives  28 us (20%)
  waiting for transfers between devices  22.5 us (16%)
  starting transfers between devices  18.5 us (14%)
  other arithmetic  6.3 us (5%)
  local copies, waits for them, and re-layouts  2.7 us (2%)
    all_to_all x1, blocking collectives, on_device(): back = lax.all_to_all(back, 'band', split_axis=0, concat_axis=0, tiled=True)  28 us
    pallas_call x1, Pallas kernels, analyse(): pl.pallas_call(kernel, name='analyse', grid=(grid,), in_specs=[smem, smem...  21.2 us
    pallas_call x1, Pallas kernels, legendre(): pl.pallas_call(kernel, name='legendre', in_specs=[pl.BlockSpec(memory_spa...  19.5 us
    pallas_call x1, Pallas kernels, synthesise(): pl.pallas_call(kernel, name='synthesise', grid=(grid,), in_specs=[smem, s...  16.5 us
    all_to_all x1, waiting for transfers between devices, on_device(): own = lax.all_to_all(own, 'band', split_axis=0, concat_axis=0, tiled=True)  10.1 us
    all_to_all x1, starting transfers between devices, on_device(): lax.all_to_all(spread, 'band', split_axis=0, concat_axis=0, tiled=True)  7.39 us
    all_to_all x1, waiting for transfers between devices, on_device(): lax.all_to_all(earlier, 'band', split_axis=0, concat_axis=0, tiled=True)  6.79 us
    ppermute x1, starting transfers between devices, on_device(): lax.ppermute(sums, 'fld', [(k, k + shift) for k in range(parts - shift)])  4.08 us
  transfers between devices with their start and end apart: 4, of which 4 were waited for; matrix products, arithmetic and copies ran while one was open for 4% of the time, Pallas kernels for 0%

profile of v1, /device:TPU:0, one launch (start us, length us, event | category | flops | bytes accessed | tf_op | source)
XLA Modules:
  0.0 136.0 jit_solution(6903069940003873436)
XLA Ops:
  0.0 0.7 pad_add_fusion
  0.7 0.6 broadcast_in_dim.21
  1.4 7.4 %all-to-all-start = ((s32[16,1,88]{2,1,0:T(1,128)}), s32[16,1,88]{2,1,0:T(1,128)S(1)}, u32[]{:S(2)}, u32[]{:S(2)}) async-start(s32[16,1,88]{2,1,0:T(1,128)} %broadcast_in_dim.21), calls=%async_computation | async-start | bytes 16384 | tf_op jit(solution)/shard_map/all_to_all | solution.py:395
  8.8 0.7 broadcast_multiply_fusion
  9.4 1.3 sine_multiply_fusion.weight_ref
  10.7 1.4 %fusion.13 = (f32[8]{0:T(128)S(1)}, s32[]{:T(128)}) fusion(s32[8]{0:T(128)} %param.9), kind=kLoop, calls=%fused_computation.34 | loop fusion | flops 15 | bytes 68 | tf_op jit(solution)/shard_map/convert_element_type | solution.py:407
  12.1 0.1 broadcast_add_fusion
  12.2 0.1 add_convert_fusion
  12.3 2.8 %all-to-all-done = s32[16,1,88]{2,1,0:T(1,128)S(1)} async-done(((s32[16,1,88]{2,1,0:T(1,128)}), s32[16,1,88]{2,1,0:T(1,128)S(1)}, u32[]{:S(2)}, u32[]{:S(2)}) %all-to-all-start) | async-done | bytes 5664 | tf_op jit(solution)/shard_map/all_to_all | solution.py:395
  15.1 0.6 convert_element_type.54.order_ref
  15.7 21.2 %analyse.1 = (bf16[16,80,128]{2,1,0:T(8,128)(2,1)}, bf16[16,40,128]{2,1,0:T(8,128)(2,1)}, bf16[80,128,256]{2,1,0:T(8,128)(2,1)}, f32[80,24,256]{2,1,0:T(8,128)}) custom-call(s32[1280]{0:T(1024)} %points_ref.3, s32[80]{0:T(128)} %lat_ref.3, f32[80]{0:T(128)} %sine_multiply_fusion.weight_ref, f32[2,2]{1,0:T(2,128)} %coupling_ref.1, ...), custom_call_target="tpu_custom_call" | custom-call | tf_op jit(solution)/shard_map/analyse/pallas_call | solution.py:151
  37.0 4.1 %collective-permute-start = (bf16[16,40,128]{2,1,0:T(8,128)(2,1)}, bf16[16,40,128]{2,1,0:T(8,128)(2,1)}, u32[]{:S(2)}, u32[]{:S(2)}) collective-permute-start(bf16[16,40,128]{2,1,0:T(8,128)(2,1)} %get-tuple-element.10), channel_id=1, source_target_pairs={{0,1},{2,3},{4,5},{6,7},{8,9},{10,11},{12,13},{14,15},{16,17},{18,... | collective-permute-start | bytes 491528 | tf_op jit(solution)/shard_map/ppermute | solution.py:402
  41.1 0.2 select_reduce_fusion
  41.3 2.8 %collective-permute-done = bf16[16,40,128]{2,1,0:T(8,128)(2,1)} collective-permute-done((bf16[16,40,128]{2,1,0:T(8,128)(2,1)}, bf16[16,40,128]{2,1,0:T(8,128)(2,1)}, u32[]{:S(2)}, u32[]{:S(2)}) %collective-permute-start) | collective-permute-done | bytes 163872 | tf_op jit(solution)/shard_map/ppermute | solution.py:402
  44.1 3.5 %all-to-all-start.2 = ((bf16[16,40,128]{2,1,0:T(8,128)(2,1)}), bf16[16,40,128]{2,1,0:T(8,128)(2,1)S(1)}, u32[]{:S(2)}, u32[]{:S(2)}) async-start(bf16[16,40,128]{2,1,0:T(8,128)(2,1)} %collective-permute-done), calls=%async_computation.2 | async-start | bytes 327680 | tf_op jit(solution)/shard_map/all_to_all | solution.py:405
  48.3 1.0 fusion.7
  49.3 6.8 %all-to-all-done.2.earlier_ref = bf16[16,40,128]{2,1,0:T(8,128)(2,1)S(1)} async-done(((bf16[16,40,128]{2,1,0:T(8,128)(2,1)}), bf16[16,40,128]{2,1,0:T(8,128)(2,1)S(1)}, u32[]{:S(2)}, u32[]{:S(2)}) %all-to-all-start.2) | async-done | bytes 163872 | tf_op jit(solution)/shard_map/all_to_all | solution.py:405
  56.1 0.0 copy-start.1
  56.1 3.5 %all-to-all-start.1 = ((bf16[16,80,128]{2,1,0:T(8,128)(2,1)}), bf16[16,80,128]{2,1,0:T(8,128)(2,1)S(1)}, u32[]{:S(2)}, u32[]{:S(2)}) async-start(bf16[16,80,128]{2,1,0:T(8,128)(2,1)} %get-tuple-element.9), calls=%async_computation.1 | async-start | bytes 655360 | tf_op jit(solution)/shard_map/all_to_all | solution.py:404
  59.6 0.1 sine_log_fusion
  59.8 0.1 reshape.118
  59.8 0.1 cos.12
  59.9 0.7 multiply_add_fusion.log_ref
  60.6 10.1 %all-to-all-done.1.own_ref = bf16[16,80,128]{2,1,0:T(8,128)(2,1)S(1)} async-done(((bf16[16,80,128]{2,1,0:T(8,128)(2,1)}), bf16[16,80,128]{2,1,0:T(8,128)(2,1)S(1)}, u32[]{:S(2)}, u32[]{:S(2)}) %all-to-all-start.1) | async-done | bytes 327712 | tf_op jit(solution)/shard_map/all_to_all | solution.py:404
  70.7 0.0 copy-start
  70.7 0.7 broadcast_in_dim.27.order_ref
  71.4 0.6 broadcast_in_dim.22.cos_ref
  72.0 0.0 copy-done.1
  72.0 0.0 copy-done
  72.0 19.5 %legendre.1 = bf16[16,80,128]{2,1,0:T(8,128)(2,1)} custom-call(s32[1]{0:T(128)} %bitcast.pairs_ref, bf16[16,80,128]{2,1,0:T(8,128)(2,1)} %copy-done, bf16[16,40,128]{2,1,0:T(8,128)(2,1)} %copy-done.1, f32[8,1280]{1,0:T(8,128)} %broadcast_in_dim.22.cos_ref, f32[8,1280]{1,0:T(8,128)} %multiply_add_fusion.log_ref, f32[41,8,32]{2,1,0:T(8,128)} %get-tuple-element.14.ahead_ref, ...), custom_call_target="tpu_custom_call" | custom-call | tf_op jit(solution)/shard_map/legendre/pallas_call | solution.py:263
  91.5 28.0 %all_to_all.24.back_ref = bf16[16,80,128]{2,1,0:T(8,128)(2,1)} all-to-all(bf16[16,80,128]{2,1,0:T(8,128)(2,1)} %legendre.1), channel_id=1, replica_groups=mesh['band'=16,'fld'=2] {'band'}, dimensions={0} | all-to-all | bytes 655360 | tf_op jit(solution)/shard_map/all_to_all | solution.py:419
  119.5 16.5 %synthesise.1 = bf16[4,80,2,5248]{3,2,1,0:T(2,128)(2,1)} custom-call(s32[1280]{0:T(1024)} %points_ref.3, s32[80]{0:T(128)} %lat_ref.3, bf16[16,80,128]{2,1,0:T(8,128)(2,1)} %all_to_all.24.back_ref, bf16[80,128,256]{2,1,0:T(8,128)(2,1)} %get-tuple-element.11.table_ref, f32[80,24,256]{2,1,0:T(8,128)} %get-tuple-element.12.phase_ref, ...), custom_call_target="tpu_custom_call" | custom-call | tf_op jit(solution)/shard_map/synthesise/pallas_call | solution.py:351
  (5 shorter events, 0.0 us)
Async XLA Ops:
  1.4 13.8 %all-to-all-start = ((s32[16,1,88]{2,1,0:T(1,128)}), s32[16,1,88]{2,1,0:T(1,128)S(1)}, u32[]{:S(2)}, u32[]{:S(2)}) async-start(s32[16,1,88]{2,1,0:T(1,128)} %broadcast_in_dim.21), calls=%async_computation | async-start | bytes 16384 | tf_op jit(solution)/shard_map/all_to_all | solution.py:395
  37.0 7.1 %collective-permute-start = (bf16[16,40,128]{2,1,0:T(8,128)(2,1)}, bf16[16,40,128]{2,1,0:T(8,128)(2,1)}, u32[]{:S(2)}, u32[]{:S(2)}) collective-permute-start(bf16[16,40,128]{2,1,0:T(8,128)(2,1)} %get-tuple-element.10), channel_id=1, source_target_pairs={{0,1},{2,3},{4,5},{6,7},{8,9},{10,11},{12,13},{14,15},{16,17},{18,... | collective-permute-start | bytes 491528 | tf_op jit(solution)/shard_map/ppermute | solution.py:402
  44.1 12.0 %all-to-all-start.2 = ((bf16[16,40,128]{2,1,0:T(8,128)(2,1)}), bf16[16,40,128]{2,1,0:T(8,128)(2,1)S(1)}, u32[]{:S(2)}, u32[]{:S(2)}) async-start(bf16[16,40,128]{2,1,0:T(8,128)(2,1)} %collective-permute-done), calls=%async_computation.2 | async-start | bytes 327680 | tf_op jit(solution)/shard_map/all_to_all | solution.py:405
  56.1 15.9 %copy-start.1 = (bf16[16,40,128]{2,1,0:T(8,128)(2,1)}, bf16[16,40,128]{2,1,0:T(8,128)(2,1)S(1)}, u32[]{:S(2)}) copy-start(bf16[16,40,128]{2,1,0:T(8,128)(2,1)S(1)} %all-to-all-done.2.earlier_ref) | copy-start | bytes 491524
  56.1 14.6 %all-to-all-start.1 = ((bf16[16,80,128]{2,1,0:T(8,128)(2,1)}), bf16[16,80,128]{2,1,0:T(8,128)(2,1)S(1)}, u32[]{:S(2)}, u32[]{:S(2)}) async-start(bf16[16,80,128]{2,1,0:T(8,128)(2,1)} %get-tuple-element.9), calls=%async_computation.1 | async-start | bytes 655360 | tf_op jit(solution)/shard_map/all_to_all | solution.py:404
  70.7 1.3 copy-start

commit v2 on v1

--- a/solution.py
+++ b/solution.py
@@ -67,12 +67,16 @@
     tiles = span // 8
     count = orders.shape[1]
     bands = count // 8
-    half = slots // 2
     grid = slots // GROUP
     field = grid_field.reshape(fields, slots, 2, width)
 
-    def kernel(points_ref, lat_ref, weight_ref, coupling_ref, x_ref, order_ref, own_ref, sum_ref, table_ref, phase_ref, staged, planes):
+    def kernel(points_ref, lat_ref, weight_ref, coupling_ref, x_ref, given_ref, own_ref, sum_ref, table_ref, phase_ref, order_ref, staged, planes):
         step = pl.program_id(0)
+
+        @pl.when(step == 0)
+        def _():
+            order_ref[...] = deal(given_ref[...], bands)
+
         for b in range(blocks):
             staged[:, :, b] = x_ref[..., b * 128 : (b + 1) * 128]
         flat = staged.reshape(fields, GROUP * rows, 128)
@@ -127,25 +131,17 @@
 
         @pl.when(step == grid - 1)
         def _():
-            for tile in range(count // 128):
-                lanes = slice(128 * tile, 128 * tile + 128)
-                value = [planes[k, :, lanes].astype(BF).astype(F32) for k in range(16)]
-                own, totals = [None] * 16, [None] * 8
-                for p in range(2):
-                    for v in range(nv):
-                        for ri in range(2):
-                            running = None
-                            for l in range(nl):
-                                at = ((p * nv + v) * nl + l) * 2 + ri
-                                own[at] = value[at] if running is None else value[at] + running
-                                term = coupling_ref[v, l] * value[at]
-                                running = term if running is None else running + term
-                            totals[(p * nv + v) * 2 + ri] = running
-                for d, w in enumerate(block_transpose(own)):
-                    own_ref[16 * tile + d] = w.astype(BF)
-                packed = [t[:half] for t in totals] + [t[half:] for t in totals]
-                for d, w in enumerate(block_transpose(packed)):
-                    sum_ref[16 * tile + d] = w.astype(BF)
+            for p in range(2):
+                for v in range(nv):
+                    for ri in range(2):
+                        running = None
+                        for l in range(nl):
+                            at = ((p * nv + v) * nl + l) * 2 + ri
+                            value = planes[at].astype(BF).astype(F32)
+                            own_ref[at] = value if running is None else value + running
+                            term = coupling_ref[v, l] * value
+                            running = term if running is None else running + term
+                        sum_ref[(p * nv + v) * 2 + ri] = running.astype(BF)
 
     smem = pl.BlockSpec(memory_space=pltpu.SMEM)
     return pl.pallas_call(
@@ -161,16 +157,18 @@
             pl.BlockSpec((1, count), lambda i: (0, 0)),
         ],
         out_specs=[
-            pl.BlockSpec((bands, slots, 128), lambda i: (0, 0, 0)),
-            pl.BlockSpec((bands, half, 128), lambda i: (0, 0, 0)),
+            pl.BlockSpec((16, slots, count), lambda i: (0, 0, 0)),
+            pl.BlockSpec((16 // nl, slots, count), lambda i: (0, 0, 0)),
             pl.BlockSpec((GROUP, 128, 2 * count), lambda i: (i, 0, 0)),
             pl.BlockSpec((GROUP, 24, 2 * count), lambda i: (i, 0, 0)),
+            pl.BlockSpec((1, count), lambda i: (0, 0)),
         ],
         out_shape=[
-            jax.ShapeDtypeStruct((bands, slots, 128), BF),
-            jax.ShapeDtypeStruct((bands, half, 128), BF),
+            jax.ShapeDtypeStruct((16, slots, count), F32),
+            jax.ShapeDtypeStruct((16 // nl, slots, count), BF),
             jax.ShapeDtypeStruct((slots, 128, 2 * count), BF),
             jax.ShapeDtypeStruct((slots, 24, 2 * count), F32),
+            jax.ShapeDtypeStruct((1, count), F32),
         ],
         scratch_shapes=[
             pltpu.VMEM((fields, GROUP, blocks, 2, 128), BF),
@@ -180,68 +178,97 @@
     )(points, lat_ids, weights, coupling, field, orders)
 
 
-def legendre(pairs, own, earlier, cosines, start_log, ahead, behind, order_rows, nv, nl):
+def deal(row, bands):
+    count = row.shape[1]
+    line, lane = iota((count, count), 0), iota((count, count), 1)
+    column = jnp.sum(jnp.where(line == lane, row, 0.0), axis=1, keepdims=True)
+    rank = jnp.sum(jnp.where(row < column, 1.0, 0.0), axis=1, keepdims=True).astype(jnp.int32)
+    upper = rank >= count // 2
+    pair = jnp.where(upper, count - 1 - rank, rank)
+    place = pair % bands * 8 + pair // bands * 2 + jnp.where(upper, 1, 0)
+    return jnp.sum(jnp.where(place == lane, column, 0.0), axis=0, keepdims=True)
+
+
+def mix(own, earlier, bands, nv, nl):
+    _, slots, count = own.shape
+
+    def kernel(own_ref, earlier_ref, out_ref):
+        for tile in range(count // 128):
+            lanes = slice(128 * tile, 128 * tile + 128)
+            value = []
+            for k in range(16):
+                source = k // (2 * nl) * 2 + k % 2
+                value.append(own_ref[k, :, lanes] + earlier_ref[source, :, lanes].astype(F32))
+            for d, w in enumerate(block_transpose(value)):
+                out_ref[16 * tile + d] = w.astype(BF)
+
+    return pl.pallas_call(kernel, name="mix", out_shape=jax.ShapeDtypeStruct((bands, slots, 128), BF))(own, earlier)
+
+
+def legendre(pairs, own, cosines, first_log, second_log, terms):
     bands, slots, _ = own.shape
-    half = slots // 2
     total = bands * slots
-    chunk = total // 2
+    half = total // 2
     height = 8 * STEPS
 
-    def kernel(pairs_ref, own_ref, earlier_ref, cos_ref, log_ref, ahead_ref, behind_ref, order_ref, out_ref, mixed, weights, even_rows, odd_rows, acc, now, before, log_now):
-        source, target = iota((128, 128), 0), iota((128, 128), 1)
-        span_l = 16 * nl
-        wanted = target // span_l * 16 + target % 16
-        pick0 = jnp.where(source == wanted, 1.0, 0.0).astype(BF)
-        pick1 = jnp.where(source == wanted + 64, 1.0, 0.0).astype(BF)
+    def kernel(pairs_ref, own_ref, cos_ref, first_ref, second_ref, term_ref, out_ref, mixed, weights, even_rows, odd_rows, acc, now, before, log_now):
         for b in range(bands):
-            part = earlier_ref[b]
-            top = jnp.dot(part, pick0, preferred_element_type=F32)
-            low = jnp.dot(part, pick1, preferred_element_type=F32)
-            mixed[b * slots : (b + 1) * slots] = own_ref[b].astype(F32) + jnp.concatenate([top, low], axis=0)
-        weights[...] = mixed[...].astype(BF)
-        acc[...] = jnp.zeros((128, total), F32)
-        now[...] = jnp.ones((8, total), F32)
-        before[...] = jnp.zeros((8, total), F32)
-        log_now[...] = log_ref[...]
-        row, lane = iota((height, 128), 0), iota((height, 128), 1)
-        select = (row % 8 == lane % 8) & (row // 8 % 2 == lane // 64)
-        degree_base = jnp.concatenate([order_ref[...]] * STEPS, axis=0) + (row // 8).astype(F32)
+            mixed[b * slots : (b + 1) * slots] = own_ref[b].astype(F32)
+        weights[...] = jnp.concatenate([mixed[:half], mixed[half:]], axis=1).astype(BF)
+        acc[...] = jnp.zeros((256, half), F32)
+        now[...] = jnp.ones((8, half), F32)
+        before[...] = jnp.zeros((8, half), F32)
+        log_now[...] = first_ref[...]
+        line, lane = iota((8, 128), 0), iota((8, 128), 1)
+        low = line < 4
 
         def make(block, rows_ref):
-            a_all = ahead_ref[block]
-            b_all = behind_ref[block]
-            for h in range(total // chunk):
-                lanes = slice(h * chunk, (h + 1) * chunk)
-                current, previous, running = now[:, lanes], before[:, lanes], log_now[:, lanes]
-                cosine = cos_ref[:, lanes]
-                scale = None
-                held = None
-                for j in range(STEPS):
-                    if j % CHECK == 0:
-                        large = jnp.maximum(jnp.abs(current), jnp.abs(previous)) > 1.0
-                        shrink = jnp.where(large, 2.0**-60, 1.0)
-                        running = running + jnp.where(large, RESCALE_LOG, 0.0)
-                        current = current * shrink
-                        previous = previous * shrink
-                        scale = jnp.exp(running)
-                    value = current * scale
-                    if j % 2 == 0:
-                        held = value
-                    else:
-                        rows_ref[8 * (j - 1) : 8 * (j + 1), lanes] = jnp.concatenate([held, value], axis=0).astype(BF)
-                    a = a_all[:, j : j + 1]
-                    b = b_all[:, j : j + 1]
-                    current, previous = (a * cosine) * current - b * previous, current
-                now[:, lanes] = current
-                before[:, lanes] = previous
-                log_now[:, lanes] = running
+            info = term_ref[block]
+            restart = jnp.broadcast_to(info[:, 97:98], (8, half)) > 0.5
+            current = jnp.where(restart, 1.0, now[...])
+            previous = jnp.where(restart, 0.0, before[...])
+            running = jnp.where(restart, second_ref[...], log_now[...])
+            cosine = cos_ref[...]
+            scale = None
+            held = None
+            for j in range(STEPS):
+                if j % CHECK == 0:
+                    large = jnp.maximum(jnp.abs(current), jnp.abs(previous)) > 1.0
+                    shrink = jnp.where(large, 2.0**-60, 1.0)
+                    running = running + jnp.where(large, RESCALE_LOG, 0.0)
+                    current = current * shrink
+                    previous = previous * shrink
+                    scale = jnp.exp(running)
+                value = current * scale
+                if j % 2 == 0:
+                    held = value
+                else:
+                    rows_ref[8 * (j - 1) : 8 * (j + 1), :] = jnp.concatenate([held, value], axis=0).astype(BF)
+                a = info[:, j : j + 1]
+                b = info[:, STEPS + j : STEPS + j + 1]
+                current, previous = (a * cosine) * current - b * previous, current
+            now[...] = current
+            before[...] = previous
+            log_now[...] = running
 
         def use(block, rows_ref):
+            info = term_ref[block]
             rows = rows_ref[...]
             found = jnp.dot(rows, weights[...], preferred_element_type=F32)
-            degree = degree_base + (block * STEPS).astype(F32)
-            damp = 1.0 / (1.0 + 4.0 * degree * (degree + 1.0) / (NT * (NT + 1.0)))
-            kept = jnp.where(select, found * damp, 0.0).astype(BF)
+            which = jnp.broadcast_to(info[:, 96:97], (8, 128)).astype(jnp.int32)
+            hit = lane % 8 == which
+            masks = []
+            for parity in range(2):
+                match = hit & (lane // 64 == parity)
+                masks.append((match & low, match & ~low))
+            tops, lows = [], []
+            for j in range(STEPS):
+                part = found[8 * j : 8 * j + 8]
+                part = jnp.where(low, part[:, :128], part[:, 128:])
+                part = (part + pltpu.roll(part, 4, 0)) * info[:, 2 * STEPS + j : 2 * STEPS + j + 1]
+                tops.append(jnp.where(masks[j % 2][0], part, 0.0))
+                lows.append(jnp.where(masks[j % 2][1], part, 0.0))
+            kept = jnp.concatenate([jnp.concatenate(tops, axis=0), jnp.concatenate(lows, axis=0)], axis=1).astype(BF)
             acc[...] += lax.dot_general(kept, rows, (((0,), (0,)), ((), ())), preferred_element_type=F32)
 
         make(0, even_rows)
@@ -254,8 +281,10 @@
             return carry
 
         lax.fori_loop(0, pairs_ref[0], body, 0)
-        for c in range(total // 128):
-            mixed[128 * c : 128 * (c + 1)] = jnp.transpose(acc[:, 128 * c : 128 * (c + 1)])
+        for h in range(2):
+            for c in range(half // 128):
+                at = h * half + 128 * c
+                mixed[at : at + 128] = jnp.transpose(acc[128 * h : 128 * h + 128, 128 * c : 128 * c + 128])
         for b in range(bands):
             out_ref[b] = mixed[b * slots : (b + 1) * slots].astype(BF)
 
@@ -263,20 +292,20 @@
     return pl.pallas_call(
         kernel,
         name="legendre",
-        in_specs=[pl.BlockSpec(memory_space=pltpu.SMEM)] + [vmem] * 7,
+        in_specs=[pl.BlockSpec(memory_space=pltpu.SMEM)] + [vmem] * 5,
         out_specs=vmem,
         out_shape=jax.ShapeDtypeStruct((bands, slots, 128), BF),
         scratch_shapes=[
             pltpu.VMEM((total, 128), F32),
-            pltpu.VMEM((total, 128), BF),
-            pltpu.VMEM((height, total), BF),
-            pltpu.VMEM((height, total), BF),
-            pltpu.VMEM((128, total), F32),
-            pltpu.VMEM((8, total), F32),
-            pltpu.VMEM((8, total), F32),
-            pltpu.VMEM((8, total), F32),
-        ],
-    )(pairs, own, earlier, cosines, start_log, ahead, behind, order_rows)
+            pltpu.VMEM((half, 256), BF),
+            pltpu.VMEM((height, half), BF),
+            pltpu.VMEM((height, half), BF),
+            pltpu.VMEM((256, half), F32),
+            pltpu.VMEM((8, half), F32),
+            pltpu.VMEM((8, half), F32),
+            pltpu.VMEM((8, half), F32),
+        ],
+    )(pairs, own, cosines, first_log, second_log, terms)
 
 
 def synthesise(back, table, phases, points, lat_ids, orders, nv, nl, width):
@@ -372,16 +401,32 @@
     return out.reshape(nv, nl, slots, 2, width)
 
 
-def recurrence_terms(orders):
-    order = orders.astype(F32)[None, :, None]
-    blocks = 2 * (-(-(NT + 1) // (2 * STEPS))) + 1
-    offset = (jnp.arange(blocks)[:, None] * STEPS + jnp.arange(STEPS)[None, :] + 1).astype(F32)[:, None, :]
+def recurrence_terms(mine):
+    first, second = mine[0::2], mine[1::2]
+    ends = jnp.floor((NT + STEPS - first) / STEPS)
+    stops = ends + jnp.floor((NT + STEPS - second) / STEPS)
+    pairs = jnp.floor((jnp.max(stops) + 1.0) / 2.0).astype(jnp.int32).reshape(1)
+    blocks = 4 * (-(-(NT + 1) // (2 * STEPS))) + 2
+    block = jnp.arange(blocks).astype(F32)[:, None]
+    late = block >= ends[None]
+    order = jnp.tile(jnp.where(late, second[None], first[None]), (1, 2))[:, :, None]
+    start = jnp.tile(STEPS * jnp.where(late, block - ends[None], block), (1, 2))[:, :, None]
+    which = jnp.tile(2.0 * jnp.arange(4).astype(F32)[None] + late, (1, 2))[:, :, None]
+    restart = jnp.tile((block == ends[None]).astype(F32), (1, 2))[:, :, None]
+    lane = jnp.arange(128)[None, None, :]
+    step = (lane % STEPS).astype(F32)
+    offset = start + step + 1.0
     degree = order + offset
     ahead = jnp.sqrt((4.0 * degree * degree - 1.0) / (offset * (2.0 * order + offset)))
     below = 4.0 * (degree - 1.0) * (degree - 1.0) - 1.0
     behind = jnp.sqrt(jnp.maximum((offset - 1.0) * (2.0 * order + offset - 1.0) / below, 0.0))
     ahead = jnp.where(degree <= NT, ahead, 0.0)
-    return ahead, ahead * behind
+    row = order + start + step
+    damp = 1.0 / (1.0 + 4.0 * row * (row + 1.0) / (NT * (NT + 1.0)))
+    kind = lane // STEPS
+    last = jnp.where(lane == 96, which, restart)
+    terms = jnp.where(kind == 0, ahead, jnp.where(kind == 1, ahead * behind, jnp.where(kind == 2, damp, last)))
+    return pairs, terms
 
 
 def solution(mesh):
@@ -396,26 +441,27 @@
         orders = known[:, :mine].reshape(1, bands * mine).astype(F32)
         lats = known[:, mine:].reshape(1, bands * slots).astype(F32)
         weights = math.pi / (2.0 * NH) * jnp.sin(math.pi * (lat_ids.astype(F32) + 0.5) / (2.0 * NH))
-        own, sums, table, phases = analyse(grid_field, points, lat_ids, weights, orders, coupling)
+        own, sums, table, phases, orders = analyse(grid_field, points, lat_ids, weights, orders, coupling)
         earlier = jnp.zeros_like(sums)
         for shift in range(1, parts):
             moved = lax.ppermute(sums, "fld", [(k, k + shift) for k in range(parts - shift)])
             earlier = moved if shift == 1 else earlier + moved
+        own = mix(own, earlier, bands, nv, nl)
         own = lax.all_to_all(own, "band", split_axis=0, concat_axis=0, tiled=True)
-        earlier = lax.all_to_all(earlier, "band", split_axis=0, concat_axis=0, tiled=True)
-        colatitude = math.pi * (lats + 0.5) / (2.0 * NH)
-        order = wn_ids.astype(F32)[:, None]
+        half = bands * slots // 2
+        colatitude = (math.pi * (lats + 0.5) / (2.0 * NH)).reshape(2, 1, half)
+        local = lax.dynamic_index_in_dim(orders.reshape(bands, mine), lax.axis_index("band"), 0, False)
         index = jnp.arange(1, NT + 1).astype(F32)
         log_norm = 0.5 * math.log(0.5) + 0.5 * jnp.sum(
-            jnp.where(index[None, :] <= order, jnp.log1p(0.5 / index)[None, :], 0.0), axis=1
+            jnp.where(index[None, :] <= local[:, None], jnp.log1p(0.5 / index)[None, :], 0.0), axis=1
         )
-        start_log = log_norm[:, None] + order * jnp.log(jnp.sin(colatitude))
-        cosines = jnp.broadcast_to(jnp.cos(colatitude), (mine, bands * slots))
-        ahead, behind = recurrence_terms(wn_ids)
-        longest = NT + 1 - jnp.min(wn_ids)
-        pairs = ((longest + 2 * STEPS - 1) // (2 * STEPS)).reshape(1).astype(jnp.int32)
-        order_rows = jnp.broadcast_to(order, (mine, 128))
-        back = legendre(pairs, own, earlier, cosines, start_log, ahead, behind, order_rows, nv, nl)
+        log_sine = jnp.log(jnp.sin(colatitude))
+        start_log = log_norm[None, :, None] + local[None, :, None] * log_sine
+        first_log = start_log[:, 0::2].reshape(mine, half)
+        second_log = start_log[:, 1::2].reshape(mine, half)
+        cosines = jnp.broadcast_to(jnp.cos(colatitude), (2, mine // 2, half)).reshape(mine, half)
+        pairs, terms = recurrence_terms(local)
+        back = legendre(pairs, own, cosines, first_log, second_log, terms)
         back = lax.all_to_all(back, "band", split_axis=0, concat_axis=0, tiled=True)
         return synthesise(back, table, phases, points, lat_ids, orders, nv, nl, width)
 

time: 137 us -> 119 us (0.87)
  blocking collectives: 28 us -> 15.3 us
  waiting for transfers between devices: 22.5 us -> 14.3 us
  Pallas kernels: 57.2 us -> 61.8 us
  starting transfers between devices: 18.5 us -> 14.4 us
  local copies, waits for them, and re-layouts: 2.7 us -> 6.09 us
    all_to_all x1, blocking collectives: 28 us -> 15.3 us  [on_device(): back = lax.all_to_all(back, 'band', split_axis=0, concat_axis=0, tiled=True)]
    all_to_all x1 -> x0, waiting for transfers between devices: 6.79 us -> none  [on_device(): lax.all_to_all(earlier, 'band', split_axis=0, concat_axis=0, tiled=True)]
    all_to_all x1, waiting for transfers between devices: 10.1 us -> 6.36 us  [on_device(): own = lax.all_to_all(own, 'band', split_axis=0, concat_axis=0, tiled=True)]
    all_to_all x1 -> x0, starting transfers between devices: 3.53 us -> none  [on_device(): lax.all_to_all(earlier, 'band', split_axis=0, concat_axis=0, tiled=True)]
    pallas_call x1, Pallas kernels: 19.5 us -> 22 us  [legendre(): pl.pallas_call(kernel, name='legendre', in_specs=[pl.BlockSpec(memory_spa...]
    pallas_call x0 -> x1, Pallas kernels: none -> 2.28 us  [mix(): pl.pallas_call(kernel, name='mix', out_shape=jax.ShapeDtypeStruct((bands,...]
    all_to_all x1, waiting for transfers between devices: 2.82 us -> 5.01 us  [on_device(): lax.all_to_all(spread, 'band', split_axis=0, concat_axis=0, tiled=True)]
    reshape x0 -> x4, local copies, waits for them, and re-layouts: none -> 1.9 us  [the longest x1 0.61 us: on_device(): jnp.broadcast_to(jnp.cos(colatitude), (2, mine // 2, half))]
  transfers between devices with their start and end apart: 4 -> 3, of which waited for: 4 -> 3; matrix products, arithmetic and copies ran while one was open for 4% -> 5% of each run, Pallas kernels for 0% -> 0%
where the time goes in v2:
time: 119 us; the launch traced here: 118 us
  Pallas kernels  61.8 us (52%)
  blocking collectives  15.3 us (13%)
  starting transfers between devices  14.4 us (12%)
  waiting for transfers between devices  14.3 us (12%)
  local copies, waits for them, and re-layouts  6.09 us (5%)
  other arithmetic  5.96 us (5%)
    pallas_call x1, Pallas kernels, legendre(): pl.pallas_call(kernel, name='legendre', in_specs=[pl.BlockSpec(memory_spa...  22 us
    pallas_call x1, Pallas kernels, analyse(): pl.pallas_call(kernel, name='analyse', grid=(grid,), in_specs=[smem, smem...  21 us
    pallas_call x1, Pallas kernels, synthesise(): pl.pallas_call(kernel, name='synthesise', grid=(grid,), in_specs=[smem, s...  16.5 us
    all_to_all x1, blocking collectives, on_device(): back = lax.all_to_all(back, 'band', split_axis=0, concat_axis=0, tiled=True)  15.3 us
    all_to_all x1, starting transfers between devices, on_device(): lax.all_to_all(spread, 'band', split_axis=0, concat_axis=0, tiled=True)  7.39 us
    all_to_all x1, waiting for transfers between devices, on_device(): own = lax.all_to_all(own, 'band', split_axis=0, concat_axis=0, tiled=True)  6.36 us
    all_to_all x1, waiting for transfers between devices, on_device(): lax.all_to_all(spread, 'band', split_axis=0, concat_axis=0, tiled=True)  5.01 us
    all_to_all x1, starting transfers between devices, on_device(): own = lax.all_to_all(own, 'band', split_axis=0, concat_axis=0, tiled=True)  3.54 us
  transfers between devices with their start and end apart: 3, of which 3 were waited for; matrix products, arithmetic and copies ran while one was open for 5% of the time, Pallas kernels for 0%

profile of v2, /device:TPU:0, one launch (start us, length us, event | category | flops | bytes accessed | tf_op | source)
XLA Modules:
  0.0 118.5 jit_solution(1999974064068835188)
XLA Ops:
  0.0 0.7 pad_add_fusion
  0.7 0.6 broadcast_in_dim.104
  1.4 7.4 %all-to-all-start = ((s32[16,1,88]{2,1,0:T(1,128)}), s32[16,1,88]{2,1,0:T(1,128)S(1)}, u32[]{:S(2)}, u32[]{:S(2)}) async-start(s32[16,1,88]{2,1,0:T(1,128)} %broadcast_in_dim.104), calls=%async_computation | async-start | bytes 16384 | tf_op jit(solution)/shard_map/all_to_all | solution.py:440
  8.8 1.3 %sine_multiply_fusion.weight_ref = f32[80]{0:T(128)} fusion(s32[80]{0:T(128)} %lat_ref.3), kind=kLoop, calls=%fused_computation.58 | loop fusion | flops 320 | bytes 640 | tf_op jit(solution)/shard_map/mul | solution.py:443
  10.1 5.0 %all-to-all-done = s32[16,1,88]{2,1,0:T(1,128)S(1)} async-done(((s32[16,1,88]{2,1,0:T(1,128)}), s32[16,1,88]{2,1,0:T(1,128)S(1)}, u32[]{:S(2)}, u32[]{:S(2)}) %all-to-all-start) | async-done | bytes 5664 | tf_op jit(solution)/shard_map/all_to_all | solution.py:440
  15.1 0.1 sine_log_fusion
  15.2 0.6 convert_element_type.84.given_ref
  15.8 21.0 %analyse.1 = (f32[16,80,128]{2,1,0:T(8,128)}, bf16[8,80,128]{2,1,0:T(8,128)(2,1)}, bf16[80,128,256]{2,1,0:T(8,128)(2,1)}, f32[80,24,256]{2,1,0:T(8,128)}, f32[1,128]{1,0:T(1,128)}) custom-call(s32[1280]{0:T(1024)} %points_ref.3, s32[80]{0:T(128)} %lat_ref.3, f32[80]{0:T(128)} %sine_multiply_fusion.weight_ref, f32[2,2]{1,0:T(2,128)} %coupling_ref.1, ...), custom_call_target="tpu_custom_call" | custom-call | tf_op jit(solution)/shard_map/analyse/pallas_call | solution.py:147
  36.8 0.6 broadcast.419
  37.4 1.4 %reduce.3 = f32[128]{0:T(128)S(1)} reduce(f32[1,128]{1,0:T(1,128)} %get-tuple-element.10.order_ref, f32[]{:T(128)} %broadcast.419), dimensions={0}, to_apply=%get-tuple-element.10.reduce_sub_computation.3 | reduce | bytes 1028 | tf_op jit(solution)/shard_map/analyse/pallas_call | solution.py:147
  38.8 0.1 reshape.398
  38.9 0.1 slice.20
  39.0 0.1 slice.19
  39.1 0.1 reshape.404
  39.2 0.2 select_reduce_fusion
  39.4 3.4 %collective-permute-start = (bf16[8,80,128]{2,1,0:T(8,128)(2,1)}, bf16[8,80,128]{2,1,0:T(8,128)(2,1)S(1)}, u32[]{:S(2)}, u32[]{:S(2)}) collective-permute-start(bf16[8,80,128]{2,1,0:T(8,128)(2,1)} %get-tuple-element.12), channel_id=1, source_target_pairs={{0,1},{2,3},{4,5},{6,7},{8,9},{10,11},{12,13},{14,15},{16,17},{18,... | collective-permute-start | bytes 491528 | tf_op jit(solution)/shard_map/ppermute | solution.py:447
  42.8 0.6 multiply_floor_fusion
  43.4 0.1 multiply_add_fusion
  43.4 0.1 fusion.22
  43.5 3.0 %collective-permute-done.earlier_ref = bf16[8,80,128]{2,1,0:T(8,128)(2,1)S(1)} collective-permute-done((bf16[8,80,128]{2,1,0:T(8,128)(2,1)}, bf16[8,80,128]{2,1,0:T(8,128)(2,1)S(1)}, u32[]{:S(2)}, u32[]{:S(2)}) %collective-permute-start) | collective-permute-done | bytes 163872 | tf_op jit(solution)/shard_map/ppermute | solution.py:447
  46.5 0.0 copy-start.1
  46.5 0.7 copy-done.1
  47.1 2.3 %mix.1 = bf16[16,80,128]{2,1,0:T(8,128)(2,1)} custom-call(f32[16,80,128]{2,1,0:T(8,128)} %get-tuple-element.11.own_ref, bf16[8,80,128]{2,1,0:T(8,128)(2,1)} %copy-done.1), custom_call_target="tpu_custom_call" | custom-call | tf_op jit(solution)/shard_map/mix/pallas_call | solution.py:205
  49.4 3.5 %all-to-all-start.1 = ((bf16[16,80,128]{2,1,0:T(8,128)(2,1)}), bf16[16,80,128]{2,1,0:T(8,128)(2,1)S(1)}, u32[]{:S(2)}, u32[]{:S(2)}) async-start(bf16[16,80,128]{2,1,0:T(8,128)(2,1)} %mix.1), calls=%async_computation.1 | async-start | bytes 655360 | tf_op jit(solution)/shard_map/all_to_all | solution.py:450
  53.1 0.1 copy.19
  53.2 0.1 copy.18
  53.3 0.1 cos.12
  53.4 0.6 reshape.400.cos_ref
  54.5 0.6 reshape.401.first_ref
  55.1 0.6 reshape.402.second_ref
  55.7 0.1 copy.20
  55.8 0.1 copy.22
  56.0 0.1 compare_convert_fusion.1
  56.0 0.1 copy.23
  56.1 0.1 copy.21
  56.2 1.4 %fusion.8.term_ref = f32[82,8,128]{2,1,0:T(8,128)} fusion(f32[82,8]{1,0:T(8,128)S(1)} %copy.23, f32[82,8]{1,0:T(8,128)S(1)} %copy.22, f32[82,8]{1,0:T(8,128)S(1)} %copy.21, f32[82,8]{1,0:T(8,128)S(1)} %copy.20, f32[128]{0:T(128)S(1)} %fusion.24, f32[82,8]{1,0:T(8,128)S(1)} %copy.19, f32[82,8]{1,0:T(8,128)S(1)} %copy.18, ...), kind=kLoop, calls=%fused_computation.16 | loop fusion | flops 2603008 | bytes 352640 | tf_op jit(solution)/shard_map/jit(_where)/select_n | solution.py:428
  57.7 6.4 %all-to-all-done.1.own_ref = bf16[16,80,128]{2,1,0:T(8,128)(2,1)S(1)} async-done(((bf16[16,80,128]{2,1,0:T(8,128)(2,1)}), bf16[16,80,128]{2,1,0:T(8,128)(2,1)S(1)}, u32[]{:S(2)}, u32[]{:S(2)}) %all-to-all-start.1) | async-done | bytes 327712 | tf_op jit(solution)/shard_map/all_to_all | solution.py:450
  64.0 0.0 copy-start
  64.0 0.7 copy-done
  64.7 22.0 %legendre.1 = bf16[16,80,128]{2,1,0:T(8,128)(2,1)} custom-call(s32[1]{0:T(128)} %bitcast.3.pairs_ref, bf16[16,80,128]{2,1,0:T(8,128)(2,1)} %copy-done, f32[8,640]{1,0:T(8,128)} %reshape.400.cos_ref, f32[8,640]{1,0:T(8,128)} %reshape.401.first_ref, f32[8,640]{1,0:T(8,128)} %reshape.402.second_ref, f32[82,8,128]{2,1,0:T(8,128)} %fusion.8.term_ref), custom_call_target="tpu_custom_call" | custom-call | tf_op jit(solution)/shard_map/legendre/pallas_call | solution.py:292
  86.8 15.3 %all_to_all.19.back_ref = bf16[16,80,128]{2,1,0:T(8,128)(2,1)} all-to-all(bf16[16,80,128]{2,1,0:T(8,128)(2,1)} %legendre.1), channel_id=1, replica_groups=mesh['band'=16,'fld'=2] {'band'}, dimensions={0} | all-to-all | bytes 655360 | tf_op jit(solution)/shard_map/all_to_all | solution.py:465
  102.0 16.5 %synthesise.1 = bf16[4,80,2,5248]{3,2,1,0:T(2,128)(2,1)} custom-call(s32[1280]{0:T(1024)} %points_ref.3, s32[80]{0:T(128)} %lat_ref.3, bf16[16,80,128]{2,1,0:T(8,128)(2,1)} %all_to_all.19.back_ref, bf16[80,128,256]{2,1,0:T(8,128)(2,1)} %get-tuple-element.13.table_ref, f32[80,24,256]{2,1,0:T(8,128)} %get-tuple-element.14.phase_ref, ...), custom_call_target="tpu_custom_call" | custom-call | tf_op jit(solution)/shard_map/synthesise/pallas_call | solution.py:380
  (17 shorter events, 0.1 us)
Async XLA Ops:
  1.4 13.8 %all-to-all-start = ((s32[16,1,88]{2,1,0:T(1,128)}), s32[16,1,88]{2,1,0:T(1,128)S(1)}, u32[]{:S(2)}, u32[]{:S(2)}) async-start(s32[16,1,88]{2,1,0:T(1,128)} %broadcast_in_dim.104), calls=%async_computation | async-start | bytes 16384 | tf_op jit(solution)/shard_map/all_to_all | solution.py:440
  39.4 7.1 %collective-permute-start = (bf16[8,80,128]{2,1,0:T(8,128)(2,1)}, bf16[8,80,128]{2,1,0:T(8,128)(2,1)S(1)}, u32[]{:S(2)}, u32[]{:S(2)}) collective-permute-start(bf16[8,80,128]{2,1,0:T(8,128)(2,1)} %get-tuple-element.12), channel_id=1, source_target_pairs={{0,1},{2,3},{4,5},{6,7},{8,9},{10,11},{12,13},{14,15},{16,17},{18,... | collective-permute-start | bytes 491528 | tf_op jit(solution)/shard_map/ppermute | solution.py:447
  46.5 0.7 copy-start.1
  49.4 14.6 %all-to-all-start.1 = ((bf16[16,80,128]{2,1,0:T(8,128)(2,1)}), bf16[16,80,128]{2,1,0:T(8,128)(2,1)S(1)}, u32[]{:S(2)}, u32[]{:S(2)}) async-start(bf16[16,80,128]{2,1,0:T(8,128)(2,1)} %mix.1), calls=%async_computation.1 | async-start | bytes 655360 | tf_op jit(solution)/shard_map/all_to_all | solution.py:450
  64.0 0.7 copy-start

commit v3 on v2

--- a/solution.py
+++ b/solution.py
@@ -52,82 +52,105 @@
     return planes
 
 
-def window(i, rows):
-    start = i * rows
-    base = start // 16 * 16
-    return base, start - base
-
-
-def analyse(grid_field, points, lat_ids, weights, orders, coupling):
-    nv, nl, slots, _, width = grid_field.shape
+def padded_rows(width):
+    pairs = -(-(width // 128) // 2)
+    return 2 * (-(-pairs // 8) * 8)
+
+
+def regroup(field):
+    fields, slots, _, width = field.shape
+    blocks = width // 128
+    depth = padded_rows(width) // 2
+
+    def kernel(x_ref, even_ref, odd_ref):
+        for b in range(2 * depth):
+            target = odd_ref if b % 2 else even_ref
+            if b < blocks:
+                target[:, :, b // 2] = x_ref[..., b * 128 : (b + 1) * 128]
+            else:
+                target[:, :, b // 2] = jnp.zeros((fields, GROUP, 2, 128), BF)
+
+    spec = pl.BlockSpec((fields, GROUP, depth, 2, 128), lambda i: (0, i, 0, 0, 0))
+    shape = jax.ShapeDtypeStruct((fields, slots, depth, 2, 128), BF)
+    even, odd = pl.pallas_call(
+        kernel,
+        name="regroup",
+        grid=(slots // GROUP,),
+        in_specs=[pl.BlockSpec((fields, GROUP, 2, width), lambda i: (0, i, 0, 0))],
+        out_specs=[spec, spec],
+        out_shape=[shape, shape],
+        compiler_params=pltpu.CompilerParams(dimension_semantics=("arbitrary",)),
+    )(field)
+    return even.reshape(fields, slots * 2 * depth, 128), odd.reshape(fields, slots * 2 * depth, 128)
+
+
+def analyse(even, odd, points, lat_ids, weights, orders, coupling, nv, nl):
     fields = nv * nl
-    blocks = width // 128
-    rows = 2 * blocks
-    span = -(-(rows + 14) // 16) * 16
-    tiles = span // 8
+    slots = lat_ids.shape[0]
+    rows = even.shape[1] // slots
+    tiles = rows // 8
     count = orders.shape[1]
     bands = count // 8
     grid = slots // GROUP
-    field = grid_field.reshape(fields, slots, 2, width)
-
-    def kernel(points_ref, lat_ref, weight_ref, coupling_ref, x_ref, given_ref, own_ref, sum_ref, table_ref, phase_ref, order_ref, staged, planes):
+
+    def kernel(points_ref, lat_ref, weight_ref, coupling_ref, even_ref, odd_ref, given_ref, own_ref, sum_ref, table_ref, phase_ref, order_ref, planes):
         step = pl.program_id(0)
 
         @pl.when(step == 0)
         def _():
             order_ref[...] = deal(given_ref[...], bands)
 
-        for b in range(blocks):
-            staged[:, :, b] = x_ref[..., b * 128 : (b + 1) * 128]
-        flat = staged.reshape(fields, GROUP * rows, 128)
         order = order_ref[...]
-        position = 128 * (iota((span, 128), 0) // 2) + iota((span, 128), 1)
-        r8 = iota((8, count), 0)
-        r16 = iota((16, count), 0)
+        position = (256 * (iota((rows, 256), 0) // 2) + iota((rows, 256), 1)).astype(F32)
+        r8, r16 = iota((8, count), 0), iota((16, count), 0)
+        multiple = jnp.concatenate([16 * r16, r16, 1024 * r8, 256 * (r8 // 2)], axis=0).astype(F32)
+        product = multiple * order
         for i in range(GROUP):
-            base, off = window(i, rows)
             slot = step * GROUP + i
             period = points_ref[lat_ref[slot]]
             period_v = jnp.full((1, count), period, jnp.int32).astype(F32)
             inverse = 1.0 / period_v
-            multiple = jnp.concatenate([8 * r16, r8, 512 * r16, 128 * (r8 // 2 - off // 2)], axis=0).astype(F32)
-            product = multiple * order
             turns = (product - jnp.floor(product * inverse + 0.5) * period_v) * inverse
             cosv, sinv = turn_cos_sin(turns)
-            fc, fs = cosv[16:24], sinv[16:24]
+            fc, fs = cosv[16:32], sinv[16:32]
             parts_c, parts_s = [], []
             for a in range(16):
                 ec, es = cosv[a : a + 1], sinv[a : a + 1]
-                parts_c.append(ec * fc - es * fs)
-                parts_s.append(-(es * fc) - ec * fs)
-            table = jnp.concatenate([jnp.concatenate(parts_c, 0), jnp.concatenate(parts_s, 0)], axis=1).astype(BF)
+                parts_c.append((ec * fc - es * fs).astype(BF))
+                parts_s.append(((-es) * fc - ec * fs).astype(BF))
+            table = jnp.concatenate([jnp.concatenate(parts_c, 0), jnp.concatenate(parts_s, 0)], axis=1)
             table_ref[i] = table
-            phase_ref[i] = jnp.concatenate([cosv[24:48], sinv[24:48]], axis=1)
-            place = position - 64 * off
-            keep = jnp.where((place >= 0) & (place < period), 1.0, 0.0).astype(BF)
-            data = jnp.concatenate([flat[f, base : base + span, :] * keep for f in range(fields)], axis=0)
+            phase_ref[i] = jnp.concatenate([cosv[32:48], sinv[32:48]], axis=1)
+            limit = jnp.full((1, 256), period, jnp.int32).astype(F32)
+            keep = jnp.minimum(jnp.maximum(limit - position, 0.0), 1.0).astype(BF)
+            lines = slice(i * rows, (i + 1) * rows)
+            data = jnp.concatenate(
+                [jnp.concatenate([even_ref[f, lines], odd_ref[f, lines]], axis=1) * keep for f in range(fields)], axis=0
+            )
             sums = jnp.dot(data, table, preferred_element_type=F32)
             hc, hs = cosv[40:48], sinv[40:48]
-            re = [jnp.zeros((8, count), F32) for _ in range(fields)]
-            im = [jnp.zeros((8, count), F32) for _ in range(fields)]
+            re = [None] * fields
+            im = [None] * fields
             for t in range(tiles):
-                gc, gs = cosv[24 + t : 25 + t], sinv[24 + t : 25 + t]
+                gc, gs = cosv[32 + t : 33 + t], sinv[32 + t : 33 + t]
                 pc = gc * hc - gs * hs
                 ps = gs * hc + gc * hs
                 for f in range(fields):
-                    at = f * span + 8 * t
+                    at = f * rows + 8 * t
                     yr = sums[at : at + 8, :count]
                     yi = sums[at : at + 8, count:]
-                    re[f] = re[f] + (pc * yr + ps * yi)
-                    im[f] = im[f] + (pc * yi - ps * yr)
+                    r = pc * yr + ps * yi
+                    q = pc * yi - ps * yr
+                    re[f] = r if t == 0 else re[f] + r
+                    im[f] = q if t == 0 else im[f] + q
             factor = jnp.where(2.0 * order < period_v, weight_ref[slot] * inverse, 0.0)
             for f in range(fields):
                 for ri, acc in ((0, re[f]), (1, im[f])):
                     acc = acc + pltpu.roll(acc, 2, 0)
                     acc = acc + pltpu.roll(acc, 4, 0)
                     other = pltpu.roll(acc, 1, 0)
-                    planes[2 * f + ri, pl.ds(slot, 1), :] = ((acc + other)[0:1] * factor)
-                    planes[2 * fields + 2 * f + ri, pl.ds(slot, 1), :] = ((acc - other)[0:1] * factor)
+                    planes[2 * f + ri, pl.ds(slot, 1), :] = (acc + other)[0:1] * factor
+                    planes[2 * fields + 2 * f + ri, pl.ds(slot, 1), :] = (acc - other)[0:1] * factor
 
         @pl.when(step == grid - 1)
         def _():
@@ -144,38 +167,29 @@
                         sum_ref[(p * nv + v) * 2 + ri] = running.astype(BF)
 
     smem = pl.BlockSpec(memory_space=pltpu.SMEM)
+    data_spec = pl.BlockSpec((fields, GROUP * rows, 128), lambda i: (0, i, 0))
     return pl.pallas_call(
         kernel,
         name="analyse",
         grid=(grid,),
-        in_specs=[
-            smem,
-            smem,
-            smem,
-            smem,
-            pl.BlockSpec((fields, GROUP, 2, width), lambda i: (0, i, 0, 0)),
-            pl.BlockSpec((1, count), lambda i: (0, 0)),
-        ],
+        in_specs=[smem, smem, smem, smem, data_spec, data_spec, pl.BlockSpec((1, count), lambda i: (0, 0))],
         out_specs=[
             pl.BlockSpec((16, slots, count), lambda i: (0, 0, 0)),
             pl.BlockSpec((16 // nl, slots, count), lambda i: (0, 0, 0)),
-            pl.BlockSpec((GROUP, 128, 2 * count), lambda i: (i, 0, 0)),
-            pl.BlockSpec((GROUP, 24, 2 * count), lambda i: (i, 0, 0)),
+            pl.BlockSpec((GROUP, 256, 2 * count), lambda i: (i, 0, 0)),
+            pl.BlockSpec((GROUP, 16, 2 * count), lambda i: (i, 0, 0)),
             pl.BlockSpec((1, count), lambda i: (0, 0)),
         ],
         out_shape=[
             jax.ShapeDtypeStruct((16, slots, count), F32),
             jax.ShapeDtypeStruct((16 // nl, slots, count), BF),
-            jax.ShapeDtypeStruct((slots, 128, 2 * count), BF),
-            jax.ShapeDtypeStruct((slots, 24, 2 * count), F32),
+            jax.ShapeDtypeStruct((slots, 256, 2 * count), BF),
+            jax.ShapeDtypeStruct((slots, 16, 2 * count), F32),
             jax.ShapeDtypeStruct((1, count), F32),
         ],
-        scratch_shapes=[
-            pltpu.VMEM((fields, GROUP, blocks, 2, 128), BF),
-            pltpu.VMEM((16, slots, count), F32),
-        ],
+        scratch_shapes=[pltpu.VMEM((16, slots, count), F32)],
         compiler_params=pltpu.CompilerParams(dimension_semantics=("arbitrary",)),
-    )(points, lat_ids, weights, coupling, field, orders)
+    )(points, lat_ids, weights, coupling, even, odd, orders)
 
 
 def deal(row, bands):
@@ -312,15 +326,13 @@
     bands, slots, _ = back.shape
     fields = nv * nl
     blocks = width // 128
-    rows = 2 * blocks
-    span = -(-(rows + 14) // 16) * 16
-    tiles = span // 8
+    rows = padded_rows(width)
+    tiles = rows // 8
     count = orders.shape[1]
     grid = slots // GROUP
 
-    def kernel(points_ref, lat_ref, back_ref, table_ref, phase_ref, order_ref, out_ref, planes, waves, staged):
+    def kernel(points_ref, lat_ref, back_ref, table_ref, phase_ref, order_ref, out_ref, planes):
         step = pl.program_id(0)
-        result = staged.reshape(fields, GROUP * rows, 128)
 
         @pl.when(step == 0)
         def _():
@@ -330,51 +342,39 @@
                     planes[k, :, 128 * tile : 128 * tile + 128] = w
 
         order = order_ref[...]
-        position = 128 * (iota((span, 128), 0) // 2) + iota((span, 128), 1)
+        position = 256 * (iota((rows, 256), 0) // 2) + iota((rows, 256), 1)
         sign = jnp.where(iota((8, count), 0) % 2 == 0, 1.0, -1.0)
-        row8 = iota((8, count), 0)
+        double = jnp.where(order == 0.0, 1.0, 2.0)
         for i in range(GROUP):
-            base, off = window(i, rows)
             slot = step * GROUP + i
             period = points_ref[lat_ref[slot]]
             period_v = jnp.full((1, count), period, jnp.int32).astype(F32)
-            factor = jnp.where(2.0 * order < period_v, jnp.where(order == 0.0, 1.0, 2.0), 0.0)
-            hc, hs = phase_ref[i, 16:24, :count], phase_ref[i, 16:24, count:]
+            factor = jnp.where(2.0 * order < period_v, double, 0.0)
+            hc, hs = phase_ref[i, 8:16, :count], phase_ref[i, 8:16, count:]
             re, im = [], []
             for f in range(fields):
                 for ri, keep in ((0, re), (1, im)):
                     even = planes[2 * f + ri, pl.ds(slot, 1), :] * factor
                     odd = planes[2 * fields + 2 * f + ri, pl.ds(slot, 1), :] * factor
                     keep.append(even + sign * odd)
+            parts = [[] for _ in range(fields)]
             for t in range(0, tiles, 2):
                 pair = []
                 for u in (t, t + 1):
                     gc, gs = phase_ref[i, u : u + 1, :count], phase_ref[i, u : u + 1, count:]
-                    pc = gc * hc - gs * hs
-                    ps = gs * hc + gc * hs
-                    if 8 * u < off or 8 * u + 8 > off + rows:
-                        valid = (row8 + 8 * u >= off) & (row8 + 8 * u < off + rows)
-                        pc = jnp.where(valid, pc, 0.0)
-                        ps = jnp.where(valid, ps, 0.0)
-                    pair.append((pc, ps))
+                    pair.append((gc * hc - gs * hs, gs * hc + gc * hs))
                 for f in range(fields):
                     zr = jnp.concatenate([pc * re[f] - ps * im[f] for pc, ps in pair], axis=0)
                     zi = jnp.concatenate([ps * re[f] + pc * im[f] for pc, ps in pair], axis=0)
-                    at = f * span + 8 * t
-                    waves[at : at + 16, :count] = zr.astype(BF)
-                    waves[at : at + 16, count:] = zi.astype(BF)
-            values = lax.dot_general(waves[...], table_ref[i], (((1,), (1,)), ((), ())), preferred_element_type=F32)
-            inside = position - 64 * off < period
+                    parts[f].append(jnp.concatenate([zr.astype(BF), zi.astype(BF)], axis=1))
+            waves = jnp.concatenate([jnp.concatenate(p, axis=0) for p in parts], axis=0)
+            values = lax.dot_general(waves, table_ref[i], (((1,), (1,)), ((), ())), preferred_element_type=F32)
+            inside = position < period
             for f in range(fields):
-                part = jnp.where(inside, values[f * span : (f + 1) * span], 0.0)
-                if off:
-                    first = part[:16] + result[f, base : base + 16, :].astype(F32)
-                    result[f, base : base + 16, :] = first.astype(BF)
-                    result[f, base + 16 : base + span, :] = part[16:].astype(BF)
-                else:
-                    result[f, base : base + span, :] = part.astype(BF)
-        for b in range(blocks):
-            out_ref[..., b * 128 : (b + 1) * 128] = staged[:, :, b]
+                part = jnp.where(inside, values[f * rows : (f + 1) * rows], 0.0).astype(BF)
+                for b in range(blocks):
+                    at, lane = b // 2 * 2, b % 2 * 128
+                    out_ref[f, i, :, b * 128 : (b + 1) * 128] = part[at : at + 2, lane : lane + 128]
 
     smem = pl.BlockSpec(memory_space=pltpu.SMEM)
     out = pl.pallas_call(
@@ -385,17 +385,13 @@
             smem,
             smem,
             pl.BlockSpec((bands, slots, 128), lambda i: (0, 0, 0)),
-            pl.BlockSpec((GROUP, 128, 2 * count), lambda i: (i, 0, 0)),
-            pl.BlockSpec((GROUP, 24, 2 * count), lambda i: (i, 0, 0)),
+            pl.BlockSpec((GROUP, 256, 2 * count), lambda i: (i, 0, 0)),
+            pl.BlockSpec((GROUP, 16, 2 * count), lambda i: (i, 0, 0)),
             pl.BlockSpec((1, count), lambda i: (0, 0)),
         ],
         out_specs=pl.BlockSpec((fields, GROUP, 2, width), lambda i: (0, i, 0, 0)),
         out_shape=jax.ShapeDtypeStruct((fields, slots, 2, width), BF),
-        scratch_shapes=[
-            pltpu.VMEM((16, slots, count), F32),
-            pltpu.VMEM((fields * span, 2 * count), BF),
-            pltpu.VMEM((fields, GROUP, blocks, 2, 128), BF),
-        ],
+        scratch_shapes=[pltpu.VMEM((16, slots, count), F32)],
         compiler_params=pltpu.CompilerParams(dimension_semantics=("arbitrary",)),
     )(points, lat_ids, back, table, phases, orders)
     return out.reshape(nv, nl, slots, 2, width)
@@ -435,13 +431,14 @@
     def on_device(grid_field, coupling, points, lat_ids, wn_ids):
         nv, nl, slots, _, width = grid_field.shape
         mine = wn_ids.shape[0]
+        even, odd = regroup(grid_field.reshape(nv * nl, slots, 2, width))
         packed = jnp.concatenate([wn_ids, lat_ids])
         spread = jnp.broadcast_to(packed[None], (bands, mine + slots))
         known = lax.all_to_all(spread, "band", split_axis=0, concat_axis=0, tiled=True)
         orders = known[:, :mine].reshape(1, bands * mine).astype(F32)
         lats = known[:, mine:].reshape(1, bands * slots).astype(F32)
         weights = math.pi / (2.0 * NH) * jnp.sin(math.pi * (lat_ids.astype(F32) + 0.5) / (2.0 * NH))
-        own, sums, table, phases, orders = analyse(grid_field, points, lat_ids, weights, orders, coupling)
+        own, sums, table, phases, orders = analyse(even, odd, points, lat_ids, weights, orders, coupling, nv, nl)
         earlier = jnp.zeros_like(sums)
         for shift in range(1, parts):
             moved = lax.ppermute(sums, "fld", [(k, k + shift) for k in range(parts - shift)])

time: 119 us -> 121 us (1.017)
  waiting for transfers between devices: 14.3 us -> 9.77 us
  Pallas kernels: 61.8 us -> 65 us
  starting transfers between devices: 14.4 us -> 16.5 us
    pallas_call x0 -> x1, Pallas kernels: none -> 11 us  [regroup(): pl.pallas_call(kernel, name='regroup', grid=(slots // GROUP,), in_specs=[...]
    pallas_call x1, Pallas kernels: 21 us -> 15.7 us  [analyse(): pl.pallas_call(kernel, name='analyse', grid=(grid,), in_specs=[smem, smem...]
    all_to_all x1, waiting for transfers between devices: 5.01 us -> 0.01 us  [on_device(): lax.all_to_all(spread, 'band', split_axis=0, concat_axis=0, tiled=True)]
    pallas_call x1, Pallas kernels: 16.5 us -> 14 us  [synthesise(): pl.pallas_call(kernel, name='synthesise', grid=(grid,), in_specs=[smem, s...]
    all_to_all x1, starting transfers between devices: 3.54 us -> 5.72 us  [on_device(): own = lax.all_to_all(own, 'band', split_axis=0, concat_axis=0, tiled=True)]
  transfers between devices with their start and end apart: 3 -> 3, of which waited for: 3 -> 2; matrix products, arithmetic and copies ran while one was open for 5% -> 5% of each run, Pallas kernels for 0% -> 9%
where the time goes in v3:
time: 121 us; the launch traced here: 120 us
  Pallas kernels  65 us (54%)
  starting transfers between devices  16.5 us (14%)
  blocking collectives  15.3 us (13%)
  waiting for transfers between devices  9.77 us (8%)
  local copies, waits for them, and re-layouts  6.14 us (5%)
  other arithmetic  6.03 us (5%)
    pallas_call x1, Pallas kernels, legendre(): pl.pallas_call(kernel, name='legendre', in_specs=[pl.BlockSpec(memory_spa...  22 us
    pallas_call x1, Pallas kernels, analyse(): pl.pallas_call(kernel, name='analyse', grid=(grid,), in_specs=[smem, smem...  15.7 us
    all_to_all x1, blocking collectives, on_device(): back = lax.all_to_all(back, 'band', split_axis=0, concat_axis=0, tiled=True)  15.3 us
    pallas_call x1, Pallas kernels, synthesise(): pl.pallas_call(kernel, name='synthesise', grid=(grid,), in_specs=[smem, s...  14 us
    pallas_call x1, Pallas kernels, regroup(): pl.pallas_call(kernel, name='regroup', grid=(slots // GROUP,), in_specs=[...  11 us
    all_to_all x1, starting transfers between devices, on_device(): lax.all_to_all(spread, 'band', split_axis=0, concat_axis=0, tiled=True)  7.39 us
    all_to_all x1, waiting for transfers between devices, on_device(): own = lax.all_to_all(own, 'band', split_axis=0, concat_axis=0, tiled=True)  6.27 us
    all_to_all x1, starting transfers between devices, on_device(): own = lax.all_to_all(own, 'band', split_axis=0, concat_axis=0, tiled=True)  5.72 us
  transfers between devices with their start and end apart: 3, of which 2 were waited for; matrix products, arithmetic and copies ran while one was open for 5% of the time, Pallas kernels for 9%

profile of v3, /device:TPU:0, one launch (start us, length us, event | category | flops | bytes accessed | tf_op | source)
XLA Modules:
  0.0 119.5 jit_solution(5214479779521457668)
XLA Ops:
  0.0 0.7 pad_add_fusion
  0.7 0.6 broadcast_in_dim.104
  1.4 7.4 %all-to-all-start = ((s32[16,1,88]{2,1,0:T(1,128)}), s32[16,1,88]{2,1,0:T(1,128)S(1)}, u32[]{:S(2)}, u32[]{:S(2)}) async-start(s32[16,1,88]{2,1,0:T(1,128)} %broadcast_in_dim.104), calls=%async_computation | async-start | bytes 16384 | tf_op jit(solution)/shard_map/all_to_all | solution.py:437
  8.7 1.3 %sine_multiply_fusion.weight_ref = f32[80]{0:T(128)} fusion(s32[80]{0:T(128)} %lat_ref.3), kind=kLoop, calls=%fused_computation.58 | loop fusion | flops 320 | bytes 640 | tf_op jit(solution)/shard_map/mul | solution.py:440
  10.1 11.0 %regroup.1 = (bf16[4,80,24,2,128]{4,3,2,1,0:T(2,128)(2,1)}, bf16[4,80,24,2,128]{4,3,2,1,0:T(2,128)(2,1)}) custom-call(bf16[4,80,2,5248]{3,2,1,0:T(2,128)(2,1)} %bitcast.12), custom_call_target="tpu_custom_call" | custom-call | tf_op jit(solution)/shard_map/regroup/pallas_call | solution.py:75
  21.1 0.0 all-to-all-done
  21.1 0.7 convert_element_type.84.given_ref
  21.7 15.7 %analyse.1 = (f32[16,80,128]{2,1,0:T(8,128)}, bf16[8,80,128]{2,1,0:T(8,128)(2,1)}, bf16[80,256,256]{2,1,0:T(8,128)(2,1)}, f32[80,16,256]{2,1,0:T(8,128)}, f32[1,128]{1,0:T(1,128)}) custom-call(s32[1280]{0:T(1024)} %points_ref.3, s32[80]{0:T(128)} %lat_ref.3, f32[80]{0:T(128)} %sine_multiply_fusion.weight_ref, f32[2,2]{1,0:T(2,128)} %coupling_ref.1, ...), custom_call_target="tpu_custom_call" | custom-call | tf_op jit(solution)/shard_map/analyse/pallas_call | solution.py:171
  37.4 0.5 broadcast.419
  37.9 1.3 %reduce.3 = f32[128]{0:T(128)S(1)} reduce(f32[1,128]{1,0:T(1,128)} %get-tuple-element.14.order_ref, f32[]{:T(128)} %broadcast.419), dimensions={0}, to_apply=%get-tuple-element.14.reduce_sub_computation.3 | reduce | bytes 1028 | tf_op jit(solution)/shard_map/analyse/pallas_call | solution.py:171
  39.2 0.1 reshape.406
  39.3 0.1 slice.19
  39.4 0.1 slice.20
  39.5 0.1 sine_log_fusion
  39.7 0.2 select_reduce_fusion
  39.9 0.1 reshape.412
  39.9 3.4 %collective-permute-start = (bf16[8,80,128]{2,1,0:T(8,128)(2,1)}, bf16[8,80,128]{2,1,0:T(8,128)(2,1)S(1)}, u32[]{:S(2)}, u32[]{:S(2)}) collective-permute-start(bf16[8,80,128]{2,1,0:T(8,128)(2,1)} %get-tuple-element.16), channel_id=1, source_target_pairs={{0,1},{2,3},{4,5},{6,7},{8,9},{10,11},{12,13},{14,15},{16,17},{18,... | collective-permute-start | bytes 491528 | tf_op jit(solution)/shard_map/ppermute | solution.py:444
  43.4 0.7 multiply_floor_fusion
  44.1 0.1 multiply_add_fusion
  44.1 0.1 fusion.22
  44.2 3.5 %collective-permute-done.earlier_ref = bf16[8,80,128]{2,1,0:T(8,128)(2,1)S(1)} collective-permute-done((bf16[8,80,128]{2,1,0:T(8,128)(2,1)}, bf16[8,80,128]{2,1,0:T(8,128)(2,1)S(1)}, u32[]{:S(2)}, u32[]{:S(2)}) %collective-permute-start) | collective-permute-done | bytes 163872 | tf_op jit(solution)/shard_map/ppermute | solution.py:444
  47.7 0.0 copy-start.1
  47.7 0.7 copy-done.1
  48.4 2.3 %mix.1 = bf16[16,80,128]{2,1,0:T(8,128)(2,1)} custom-call(f32[16,80,128]{2,1,0:T(8,128)} %get-tuple-element.15.own_ref, bf16[8,80,128]{2,1,0:T(8,128)(2,1)} %copy-done.1), custom_call_target="tpu_custom_call" | custom-call | tf_op jit(solution)/shard_map/mix/pallas_call | solution.py:219
  50.7 5.7 %all-to-all-start.1 = ((bf16[16,80,128]{2,1,0:T(8,128)(2,1)}), bf16[16,80,128]{2,1,0:T(8,128)(2,1)S(1)}, u32[]{:S(2)}, u32[]{:S(2)}) async-start(bf16[16,80,128]{2,1,0:T(8,128)(2,1)} %mix.1), calls=%async_computation.1 | async-start | bytes 655360 | tf_op jit(solution)/shard_map/all_to_all | solution.py:447
  56.4 0.1 copy.18
  56.5 0.1 copy.19
  56.7 0.1 copy.20
  56.8 0.1 copy.21
  56.9 0.1 copy.22
  57.0 0.1 compare_convert_fusion.1
  57.1 0.1 copy.23
  57.8 0.6 reshape.409.first_ref
  58.5 0.6 reshape.410.second_ref
  59.1 0.1 cos.12
  59.2 0.6 reshape.408.cos_ref
  59.8 1.4 %fusion.8.term_ref = f32[82,8,128]{2,1,0:T(8,128)} fusion(f32[82,8]{1,0:T(8,128)S(1)} %copy.23, f32[82,8]{1,0:T(8,128)S(1)} %copy.22, f32[82,8]{1,0:T(8,128)S(1)} %copy.21, f32[82,8]{1,0:T(8,128)S(1)} %copy.20, f32[128]{0:T(128)S(1)} %fusion.24, f32[82,8]{1,0:T(8,128)S(1)} %copy.19, f32[82,8]{1,0:T(8,128)S(1)} %copy.18, ...), kind=kLoop, calls=%fused_computation.16 | loop fusion | flops 2603008 | bytes 352640 | tf_op jit(solution)/shard_map/jit(_where)/select_n | solution.py:424
  61.2 6.3 %all-to-all-done.1.own_ref = bf16[16,80,128]{2,1,0:T(8,128)(2,1)S(1)} async-done(((bf16[16,80,128]{2,1,0:T(8,128)(2,1)}), bf16[16,80,128]{2,1,0:T(8,128)(2,1)S(1)}, u32[]{:S(2)}, u32[]{:S(2)}) %all-to-all-start.1) | async-done | bytes 327712 | tf_op jit(solution)/shard_map/all_to_all | solution.py:447
  67.4 0.0 copy-start
  67.4 0.7 copy-done
  68.2 22.0 %legendre.1 = bf16[16,80,128]{2,1,0:T(8,128)(2,1)} custom-call(s32[1]{0:T(128)} %bitcast.5.pairs_ref, bf16[16,80,128]{2,1,0:T(8,128)(2,1)} %copy-done, f32[8,640]{1,0:T(8,128)} %reshape.408.cos_ref, f32[8,640]{1,0:T(8,128)} %reshape.409.first_ref, f32[8,640]{1,0:T(8,128)} %reshape.410.second_ref, f32[82,8,128]{2,1,0:T(8,128)} %fusion.8.term_ref), custom_call_target="tpu_custom_call" | custom-call | tf_op jit(solution)/shard_map/legendre/pallas_call | solution.py:306
  90.2 15.3 %all_to_all.19.back_ref = bf16[16,80,128]{2,1,0:T(8,128)(2,1)} all-to-all(bf16[16,80,128]{2,1,0:T(8,128)(2,1)} %legendre.1), channel_id=1, replica_groups=mesh['band'=16,'fld'=2] {'band'}, dimensions={0} | all-to-all | bytes 655360 | tf_op jit(solution)/shard_map/all_to_all | solution.py:462
  105.5 14.0 %synthesise.1 = bf16[4,80,2,5248]{3,2,1,0:T(2,128)(2,1)} custom-call(s32[1280]{0:T(1024)} %points_ref.3, s32[80]{0:T(128)} %lat_ref.3, bf16[16,80,128]{2,1,0:T(8,128)(2,1)} %all_to_all.19.back_ref, bf16[80,256,256]{2,1,0:T(8,128)(2,1)} %get-tuple-element.17.table_ref, f32[80,16,256]{2,1,0:T(8,128)} %get-tuple-element.18.phase_ref, ...), custom_call_target="tpu_custom_call" | custom-call | tf_op jit(solution)/shard_map/synthesise/pallas_call | solution.py:380
  (17 shorter events, 0.1 us)
Async XLA Ops:
  1.4 19.7 %all-to-all-start = ((s32[16,1,88]{2,1,0:T(1,128)}), s32[16,1,88]{2,1,0:T(1,128)S(1)}, u32[]{:S(2)}, u32[]{:S(2)}) async-start(s32[16,1,88]{2,1,0:T(1,128)} %broadcast_in_dim.104), calls=%async_computation | async-start | bytes 16384 | tf_op jit(solution)/shard_map/all_to_all | solution.py:437
  39.9 7.8 %collective-permute-start = (bf16[8,80,128]{2,1,0:T(8,128)(2,1)}, bf16[8,80,128]{2,1,0:T(8,128)(2,1)S(1)}, u32[]{:S(2)}, u32[]{:S(2)}) collective-permute-start(bf16[8,80,128]{2,1,0:T(8,128)(2,1)} %get-tuple-element.16), channel_id=1, source_target_pairs={{0,1},{2,3},{4,5},{6,7},{8,9},{10,11},{12,13},{14,15},{16,17},{18,... | collective-permute-start | bytes 491528 | tf_op jit(solution)/shard_map/ppermute | solution.py:444
  47.7 0.7 copy-start.1
  50.7 16.8 %all-to-all-start.1 = ((bf16[16,80,128]{2,1,0:T(8,128)(2,1)}), bf16[16,80,128]{2,1,0:T(8,128)(2,1)S(1)}, u32[]{:S(2)}, u32[]{:S(2)}) async-start(bf16[16,80,128]{2,1,0:T(8,128)(2,1)} %mix.1), calls=%async_computation.1 | async-start | bytes 655360 | tf_op jit(solution)/shard_map/all_to_all | solution.py:447
  67.4 0.7 copy-start

commit v4 on v2

--- a/solution.py
+++ b/solution.py
@@ -5,6 +5,7 @@
 from jax import lax
 from jax.experimental import pallas as pl
 from jax.experimental.pallas import tpu as pltpu
+from jax.experimental.layout import Layout, with_layout_constraint
 from jax.sharding import PartitionSpec as P
 
 NT = 1279
@@ -22,20 +23,17 @@
 
 
 def turn_cos_sin(turns):
-    x = turns * math.pi
-    y = x * x
-    s = 1.0 / 362880 - y * (1.0 / 39916800)
-    s = -1.0 / 5040 + y * s
-    s = 1.0 / 120 + y * s
-    s = -1.0 / 6 + y * s
-    s = x * (1.0 + y * s)
-    c = -1.0 / 3628800 + y * (1.0 / 479001600)
-    c = 1.0 / 40320 + y * c
-    c = -1.0 / 720 + y * c
-    c = 1.0 / 24 + y * c
-    c = -0.5 + y * c
-    c = 1.0 + y * c
-    return 1.0 - 2.0 * s * s, 2.0 * s * c
+    y = turns * turns
+    s = -0.59828975 + y * 0.07765416
+    s = 2.55007732 + y * s
+    s = -5.16771007 + y * s
+    s = turns * (3.14159264 + y * s)
+    c = -1.33187126 + y * 0.21967748
+    c = 4.05841064 + y * c
+    c = -4.9347928 + y * c
+    c = 0.99999995 + y * c
+    twice = s + s
+    return 1.0 - twice * s, twice * c
 
 
 def block_transpose(planes):
@@ -58,76 +56,115 @@
     return base, start - base
 
 
-def analyse(grid_field, points, lat_ids, weights, orders, coupling):
-    nv, nl, slots, _, width = grid_field.shape
+def window_rows(width):
+    return -(-(2 * (width // 128) + 14) // 16) * 16
+
+
+def as_rows(field):
+    nv, nl, slots, _, width = field.shape
+    blocks = width // 128
+    split = field.reshape(nv, nl, slots, 2, blocks, 128)
+    split = with_layout_constraint(split, Layout(major_to_minor=(0, 1, 2, 4, 3, 5)))
+    return split.transpose(0, 1, 2, 4, 3, 5).reshape(nv * nl, slots * 2 * blocks, 128)
+
+
+def from_rows(rows, nv, nl, slots, width):
+    split = rows.reshape(nv, nl, slots, width // 128, 2, 128).transpose(0, 1, 2, 4, 3, 5)
+    split = with_layout_constraint(split, Layout(major_to_minor=(0, 1, 2, 4, 3, 5)))
+    return split.reshape(nv, nl, slots, 2, width)
+
+
+def angle_rows(order, tiles):
+    count = order.shape[1]
+    row = iota((8, count), 0)
+    steps = jnp.where(row < tiles // 2, 256 * (2 * row + 1), 64)
+    shared = jnp.concatenate([row, 8 * row, steps], axis=0).astype(F32) * order
+    blocks = (128 * (2 * tiles - 2 + row // 2)).astype(F32)
+    return shared, blocks
+
+
+def slot_angles(shared, blocks, order, off, period):
+    product = jnp.concatenate([shared, (blocks - 64.0 * off) * order], axis=0)
+    period_v = jnp.full(order.shape, period, jnp.int32).astype(F32)
+    inverse = 1.0 / period_v
+    turns = (product - jnp.floor(product * inverse + 0.5) * period_v) * inverse
+    cosv, sinv = turn_cos_sin(turns)
+    return cosv, sinv, period_v, inverse
+
+
+def inner_table(cosv, sinv):
+    fc, fs = cosv[0:8], sinv[0:8]
+    ec, es = cosv[8:16], sinv[8:16]
+    wc, ws = cosv[23:24], sinv[23:24]
+    ec = jnp.concatenate([ec, ec * wc - es * ws], axis=0)
+    es = jnp.concatenate([es, es * wc + cosv[8:16] * ws], axis=0)
+    parts_c, parts_s = [], []
+    for a in range(16):
+        c, s = ec[a : a + 1], es[a : a + 1]
+        parts_c.append(c * fc - s * fs)
+        parts_s.append((-s) * fc - c * fs)
+    halves = [jnp.concatenate(p, axis=0).astype(BF) for p in (parts_c, parts_s)]
+    return jnp.concatenate(halves, axis=1)
+
+
+def analyse(points_rows, points, lat_ids, weights, orders, coupling, nv, nl, width):
     fields = nv * nl
-    blocks = width // 128
-    rows = 2 * blocks
-    span = -(-(rows + 14) // 16) * 16
+    slots = lat_ids.shape[0]
+    rows = 2 * (width // 128)
+    span = window_rows(width)
     tiles = span // 8
+    middle = tiles // 2
     count = orders.shape[1]
     bands = count // 8
     grid = slots // GROUP
-    field = grid_field.reshape(fields, slots, 2, width)
-
-    def kernel(points_ref, lat_ref, weight_ref, coupling_ref, x_ref, given_ref, own_ref, sum_ref, table_ref, phase_ref, order_ref, staged, planes):
+
+    def kernel(points_ref, lat_ref, weight_ref, coupling_ref, x_ref, given_ref, own_ref, sum_ref, order_ref, planes):
         step = pl.program_id(0)
 
         @pl.when(step == 0)
         def _():
             order_ref[...] = deal(given_ref[...], bands)
 
-        for b in range(blocks):
-            staged[:, :, b] = x_ref[..., b * 128 : (b + 1) * 128]
-        flat = staged.reshape(fields, GROUP * rows, 128)
         order = order_ref[...]
-        position = 128 * (iota((span, 128), 0) // 2) + iota((span, 128), 1)
-        r8 = iota((8, count), 0)
-        r16 = iota((16, count), 0)
+        position = (128 * (iota((span, 128), 0) // 2) + iota((span, 128), 1)).astype(F32)
+        shared, blocks = angle_rows(order, tiles)
         for i in range(GROUP):
             base, off = window(i, rows)
             slot = step * GROUP + i
             period = points_ref[lat_ref[slot]]
-            period_v = jnp.full((1, count), period, jnp.int32).astype(F32)
-            inverse = 1.0 / period_v
-            multiple = jnp.concatenate([8 * r16, r8, 512 * r16, 128 * (r8 // 2 - off // 2)], axis=0).astype(F32)
-            product = multiple * order
-            turns = (product - jnp.floor(product * inverse + 0.5) * period_v) * inverse
-            cosv, sinv = turn_cos_sin(turns)
-            fc, fs = cosv[16:24], sinv[16:24]
-            parts_c, parts_s = [], []
-            for a in range(16):
-                ec, es = cosv[a : a + 1], sinv[a : a + 1]
-                parts_c.append(ec * fc - es * fs)
-                parts_s.append(-(es * fc) - ec * fs)
-            table = jnp.concatenate([jnp.concatenate(parts_c, 0), jnp.concatenate(parts_s, 0)], axis=1).astype(BF)
-            table_ref[i] = table
-            phase_ref[i] = jnp.concatenate([cosv[24:48], sinv[24:48]], axis=1)
-            place = position - 64 * off
-            keep = jnp.where((place >= 0) & (place < period), 1.0, 0.0).astype(BF)
-            data = jnp.concatenate([flat[f, base : base + span, :] * keep for f in range(fields)], axis=0)
+            cosv, sinv, period_v, inverse = slot_angles(shared, blocks, order, off, period)
+            table = inner_table(cosv, sinv)
+            limit = jnp.full((1, 128), period, jnp.int32).astype(F32) + 64.0 * off
+            keep = jnp.minimum(jnp.maximum(limit - position, 0.0), 1.0)
+            if off:
+                head = jnp.where(position[:16] >= 64.0 * off, keep[:16], 0.0)
+                keep = jnp.concatenate([head, keep[16:]], axis=0)
+            keep = keep.astype(BF)
+            data = jnp.concatenate([x_ref[f, base : base + span, :] * keep for f in range(fields)], axis=0)
             sums = jnp.dot(data, table, preferred_element_type=F32)
-            hc, hs = cosv[40:48], sinv[40:48]
-            re = [jnp.zeros((8, count), F32) for _ in range(fields)]
-            im = [jnp.zeros((8, count), F32) for _ in range(fields)]
-            for t in range(tiles):
-                gc, gs = cosv[24 + t : 25 + t], sinv[24 + t : 25 + t]
-                pc = gc * hc - gs * hs
-                ps = gs * hc + gc * hs
+            re = [None] * fields
+            im = [None] * fields
+            for u in range(middle):
+                c, s = cosv[16 + u : 17 + u], sinv[16 + u : 17 + u]
                 for f in range(fields):
-                    at = f * span + 8 * t
-                    yr = sums[at : at + 8, :count]
-                    yi = sums[at : at + 8, count:]
-                    re[f] = re[f] + (pc * yr + ps * yi)
-                    im[f] = im[f] + (pc * yi - ps * yr)
+                    up = f * span + 8 * (middle + u)
+                    down = f * span + 8 * (middle - 1 - u)
+                    ur, ui = sums[up : up + 8, :count], sums[up : up + 8, count:]
+                    dr, di = sums[down : down + 8, :count], sums[down : down + 8, count:]
+                    r = c * (ur + dr) + s * (ui - di)
+                    q = c * (ui + di) - s * (ur - dr)
+                    re[f] = r if u == 0 else re[f] + r
+                    im[f] = q if u == 0 else im[f] + q
             factor = jnp.where(2.0 * order < period_v, weight_ref[slot] * inverse, 0.0)
+            hc, hs = cosv[24:32] * factor, sinv[24:32] * factor
             for f in range(fields):
-                for ri, acc in ((0, re[f]), (1, im[f])):
+                turned = (hc * re[f] + hs * im[f], hc * im[f] - hs * re[f])
+                for ri, acc in enumerate(turned):
                     acc = acc + pltpu.roll(acc, 2, 0)
                     acc = acc + pltpu.roll(acc, 4, 0)
                     other = pltpu.roll(acc, 1, 0)
-                    planes[2 * f + ri, pl.ds(slot, 1), :] = ((acc + other)[0:1] * factor)
-                    planes[2 * fields + 2 * f + ri, pl.ds(slot, 1), :] = ((acc - other)[0:1] * factor)
+                    planes[2 * f + ri, pl.ds(slot, 1), :] = (acc + other)[0:1]
+                    planes[2 * fields + 2 * f + ri, pl.ds(slot, 1), :] = (acc - other)[0:1]
 
         @pl.when(step == grid - 1)
         def _():
@@ -153,29 +190,22 @@
             smem,
             smem,
             smem,
-            pl.BlockSpec((fields, GROUP, 2, width), lambda i: (0, i, 0, 0)),
+            pl.BlockSpec((fields, GROUP * rows, 128), lambda i: (0, i, 0)),
             pl.BlockSpec((1, count), lambda i: (0, 0)),
         ],
         out_specs=[
             pl.BlockSpec((16, slots, count), lambda i: (0, 0, 0)),
             pl.BlockSpec((16 // nl, slots, count), lambda i: (0, 0, 0)),
-            pl.BlockSpec((GROUP, 128, 2 * count), lambda i: (i, 0, 0)),
-            pl.BlockSpec((GROUP, 24, 2 * count), lambda i: (i, 0, 0)),
             pl.BlockSpec((1, count), lambda i: (0, 0)),
         ],
         out_shape=[
             jax.ShapeDtypeStruct((16, slots, count), F32),
             jax.ShapeDtypeStruct((16 // nl, slots, count), BF),
-            jax.ShapeDtypeStruct((slots, 128, 2 * count), BF),
-            jax.ShapeDtypeStruct((slots, 24, 2 * count), F32),
             jax.ShapeDtypeStruct((1, count), F32),
         ],
-        scratch_shapes=[
-            pltpu.VMEM((fields, GROUP, blocks, 2, 128), BF),
-            pltpu.VMEM((16, slots, count), F32),
-        ],
+        scratch_shapes=[pltpu.VMEM((16, slots, count), F32)],
         compiler_params=pltpu.CompilerParams(dimension_semantics=("arbitrary",)),
-    )(points, lat_ids, weights, coupling, field, orders)
+    )(points, lat_ids, weights, coupling, points_rows, orders)
 
 
 def deal(row, bands):
@@ -308,19 +338,18 @@
     )(pairs, own, cosines, first_log, second_log, terms)
 
 
-def synthesise(back, table, phases, points, lat_ids, orders, nv, nl, width):
+def synthesise(back, points, lat_ids, orders, nv, nl, width):
     bands, slots, _ = back.shape
     fields = nv * nl
-    blocks = width // 128
-    rows = 2 * blocks
-    span = -(-(rows + 14) // 16) * 16
+    rows = 2 * (width // 128)
+    span = window_rows(width)
     tiles = span // 8
+    middle = tiles // 2
     count = orders.shape[1]
     grid = slots // GROUP
 
-    def kernel(points_ref, lat_ref, back_ref, table_ref, phase_ref, order_ref, out_ref, planes, waves, staged):
+    def kernel(points_ref, lat_ref, back_ref, order_ref, out_ref, planes):
         step = pl.program_id(0)
-        result = staged.reshape(fields, GROUP * rows, 128)
 
         @pl.when(step == 0)
         def _():
@@ -331,53 +360,48 @@
 
         order = order_ref[...]
         position = 128 * (iota((span, 128), 0) // 2) + iota((span, 128), 1)
+        shared, blocks = angle_rows(order, tiles)
         sign = jnp.where(iota((8, count), 0) % 2 == 0, 1.0, -1.0)
-        row8 = iota((8, count), 0)
+        double = jnp.where(order == 0.0, 1.0, 2.0)
         for i in range(GROUP):
             base, off = window(i, rows)
             slot = step * GROUP + i
             period = points_ref[lat_ref[slot]]
-            period_v = jnp.full((1, count), period, jnp.int32).astype(F32)
-            factor = jnp.where(2.0 * order < period_v, jnp.where(order == 0.0, 1.0, 2.0), 0.0)
-            hc, hs = phase_ref[i, 16:24, :count], phase_ref[i, 16:24, count:]
-            re, im = [], []
+            cosv, sinv, period_v, _ = slot_angles(shared, blocks, order, off, period)
+            table = inner_table(cosv, sinv)
+            factor = jnp.where(2.0 * order < period_v, double, 0.0)
+            hc, hs = cosv[24:32] * factor, sinv[24:32] * factor
+            parts = []
             for f in range(fields):
-                for ri, keep in ((0, re), (1, im)):
-                    even = planes[2 * f + ri, pl.ds(slot, 1), :] * factor
-                    odd = planes[2 * fields + 2 * f + ri, pl.ds(slot, 1), :] * factor
-                    keep.append(even + sign * odd)
-            for t in range(0, tiles, 2):
-                pair = []
-                for u in (t, t + 1):
-                    gc, gs = phase_ref[i, u : u + 1, :count], phase_ref[i, u : u + 1, count:]
-                    pc = gc * hc - gs * hs
-                    ps = gs * hc + gc * hs
-                    if 8 * u < off or 8 * u + 8 > off + rows:
-                        valid = (row8 + 8 * u >= off) & (row8 + 8 * u < off + rows)
-                        pc = jnp.where(valid, pc, 0.0)
-                        ps = jnp.where(valid, ps, 0.0)
-                    pair.append((pc, ps))
-                for f in range(fields):
-                    zr = jnp.concatenate([pc * re[f] - ps * im[f] for pc, ps in pair], axis=0)
-                    zi = jnp.concatenate([ps * re[f] + pc * im[f] for pc, ps in pair], axis=0)
-                    at = f * span + 8 * t
-                    waves[at : at + 16, :count] = zr.astype(BF)
-                    waves[at : at + 16, count:] = zi.astype(BF)
-            values = lax.dot_general(waves[...], table_ref[i], (((1,), (1,)), ((), ())), preferred_element_type=F32)
-            inside = position - 64 * off < period
+                both = []
+                for ri in range(2):
+                    even = planes[2 * f + ri, pl.ds(slot, 1), :]
+                    odd = planes[2 * fields + 2 * f + ri, pl.ds(slot, 1), :]
+                    both.append(even + sign * odd)
+                re, im = both
+                wr, wi = hc * re - hs * im, hs * re + hc * im
+                zr, zi = [None] * tiles, [None] * tiles
+                for u in range(middle):
+                    c, s = cosv[16 + u : 17 + u], sinv[16 + u : 17 + u]
+                    cr, si, ci, sr = c * wr, s * wi, c * wi, s * wr
+                    zr[middle + u], zr[middle - 1 - u] = cr - si, cr + si
+                    zi[middle + u], zi[middle - 1 - u] = ci + sr, ci - sr
+                parts.append(jnp.concatenate([jnp.concatenate(zr, 0).astype(BF), jnp.concatenate(zi, 0).astype(BF)], axis=1))
+            waves = jnp.concatenate(parts, axis=0)
+            values = lax.dot_general(waves, table, (((1,), (1,)), ((), ())), preferred_element_type=F32)
+            inside = position < period + 64 * off
+            starts = position[:16] >= 64 * off
             for f in range(fields):
                 part = jnp.where(inside, values[f * span : (f + 1) * span], 0.0)
                 if off:
-                    first = part[:16] + result[f, base : base + 16, :].astype(F32)
-                    result[f, base : base + 16, :] = first.astype(BF)
-                    result[f, base + 16 : base + span, :] = part[16:].astype(BF)
+                    first = jnp.where(starts, part[:16], out_ref[f, base : base + 16, :].astype(F32))
+                    out_ref[f, base : base + 16, :] = first.astype(BF)
+                    out_ref[f, base + 16 : base + span, :] = part[16:].astype(BF)
                 else:
-                    result[f, base : base + span, :] = part.astype(BF)
-        for b in range(blocks):
-            out_ref[..., b * 128 : (b + 1) * 128] = staged[:, :, b]
+                    out_ref[f, base : base + span, :] = part.astype(BF)
 
     smem = pl.BlockSpec(memory_space=pltpu.SMEM)
-    out = pl.pallas_call(
+    return pl.pallas_call(
         kernel,
         name="synthesise",
         grid=(grid,),
@@ -385,20 +409,13 @@
             smem,
             smem,
             pl.BlockSpec((bands, slots, 128), lambda i: (0, 0, 0)),
-            pl.BlockSpec((GROUP, 128, 2 * count), lambda i: (i, 0, 0)),
-            pl.BlockSpec((GROUP, 24, 2 * count), lambda i: (i, 0, 0)),
             pl.BlockSpec((1, count), lambda i: (0, 0)),
         ],
-        out_specs=pl.BlockSpec((fields, GROUP, 2, width), lambda i: (0, i, 0, 0)),
-        out_shape=jax.ShapeDtypeStruct((fields, slots, 2, width), BF),
-        scratch_shapes=[
-            pltpu.VMEM((16, slots, count), F32),
-            pltpu.VMEM((fields * span, 2 * count), BF),
-            pltpu.VMEM((fields, GROUP, blocks, 2, 128), BF),
-        ],
+        out_specs=pl.BlockSpec((fields, GROUP * rows, 128), lambda i: (0, i, 0)),
+        out_shape=jax.ShapeDtypeStruct((fields, slots * rows, 128), BF),
+        scratch_shapes=[pltpu.VMEM((16, slots, count), F32)],
         compiler_params=pltpu.CompilerParams(dimension_semantics=("arbitrary",)),
-    )(points, lat_ids, back, table, phases, orders)
-    return out.reshape(nv, nl, slots, 2, width)
+    )(points, lat_ids, back, orders)
 
 
 def recurrence_terms(mine):
@@ -441,12 +458,12 @@
         orders = known[:, :mine].reshape(1, bands * mine).astype(F32)
         lats = known[:, mine:].reshape(1, bands * slots).astype(F32)
         weights = math.pi / (2.0 * NH) * jnp.sin(math.pi * (lat_ids.astype(F32) + 0.5) / (2.0 * NH))
-        own, sums, table, phases, orders = analyse(grid_field, points, lat_ids, weights, orders, coupling)
+        own, sums, orders = analyse(as_rows(grid_field), points, lat_ids, weights, orders, coupling, nv, nl, width)
         earlier = jnp.zeros_like(sums)
         for shift in range(1, parts):
             moved = lax.ppermute(sums, "fld", [(k, k + shift) for k in range(parts - shift)])
             earlier = moved if shift == 1 else earlier + moved
-        own = mix(own, earlier, bands, nv, nl)
+        own, orders = lax.optimization_barrier((mix(own, earlier, bands, nv, nl), orders))
         own = lax.all_to_all(own, "band", split_axis=0, concat_axis=0, tiled=True)
         half = bands * slots // 2
         colatitude = (math.pi * (lats + 0.5) / (2.0 * NH)).reshape(2, 1, half)
@@ -463,7 +480,8 @@
         pairs, terms = recurrence_terms(local)
         back = legendre(pairs, own, cosines, first_log, second_log, terms)
         back = lax.all_to_all(back, "band", split_axis=0, concat_axis=0, tiled=True)
-        return synthesise(back, table, phases, points, lat_ids, orders, nv, nl, width)
+        rows = synthesise(back, points, lat_ids, orders, nv, nl, width)
+        return from_rows(rows, nv, nl, slots, width)
 
     in_specs = (P(None, "fld", "band", None, None), P(None, "fld"), P(), P("band"), P("band"))
     return jax.shard_map(on_device, mesh=mesh, in_specs=in_specs, out_specs=in_specs[0], check_vma=False)

time: 119 us -> 106 us (0.89)
  Pallas kernels: 61.8 us -> 48.6 us
    pallas_call x1, Pallas kernels: 21 us -> 12.9 us  [analyse(): pl.pallas_call(kernel, name='analyse', grid=(grid,), in_specs=[smem, smem...]
    pallas_call x1, Pallas kernels: 16.5 us -> 11.4 us  [synthesise(): pl.pallas_call(kernel, name='synthesise', grid=(grid,), in_specs=[smem, s...]
    pallas_call x1 -> x0, other arithmetic: 1.36 us -> none  [analyse(): pl.pallas_call(kernel, name='analyse', grid=(grid,), in_specs=[smem, smem...]
    optimization_barrier x0 -> x1, other arithmetic: none -> 1.28 us  [on_device(): lax.optimization_barrier((mix(own, earlier, bands, nv, nl), orders))]
  transfers between devices with their start and end apart: 3 -> 3, of which waited for: 3 -> 3; matrix products, arithmetic and copies ran while one was open for 5% -> 6% of each run, Pallas kernels for 0% -> 0%
where the time goes in v4:
time: 106 us; the launch traced here: 105 us
  Pallas kernels  48.6 us (46%)
  blocking collectives  15.3 us (14%)
  starting transfers between devices  14.4 us (14%)
  waiting for transfers between devices  14 us (13%)
  local copies, waits for them, and re-layouts  6.06 us (6%)
  other arithmetic  5.91 us (6%)
    pallas_call x1, Pallas kernels, legendre(): pl.pallas_call(kernel, name='legendre', in_specs=[pl.BlockSpec(memory_spa...  22 us
    all_to_all x1, blocking collectives, on_device(): back = lax.all_to_all(back, 'band', split_axis=0, concat_axis=0, tiled=True)  15.3 us
    pallas_call x1, Pallas kernels, analyse(): pl.pallas_call(kernel, name='analyse', grid=(grid,), in_specs=[smem, smem...  12.9 us
    pallas_call x1, Pallas kernels, synthesise(): pl.pallas_call(kernel, name='synthesise', grid=(grid,), in_specs=[smem, s...  11.4 us
    all_to_all x1, starting transfers between devices, on_device(): lax.all_to_all(spread, 'band', split_axis=0, concat_axis=0, tiled=True)  7.39 us
    all_to_all x1, waiting for transfers between devices, on_device(): own = lax.all_to_all(own, 'band', split_axis=0, concat_axis=0, tiled=True)  6.23 us
    all_to_all x1, waiting for transfers between devices, on_device(): lax.all_to_all(spread, 'band', split_axis=0, concat_axis=0, tiled=True)  5.01 us
    all_to_all x1, starting transfers between devices, on_device(): own = lax.all_to_all(own, 'band', split_axis=0, concat_axis=0, tiled=True)  3.55 us
  transfers between devices with their start and end apart: 3, of which 3 were waited for; matrix products, arithmetic and copies ran while one was open for 6% of the time, Pallas kernels for 0%

profile of v4, /device:TPU:0, one launch (start us, length us, event | category | flops | bytes accessed | tf_op | source)
XLA Modules:
  0.0 105.0 jit_solution(2089018102243454637)
XLA Ops:
  0.0 0.7 pad_add_fusion
  0.7 0.6 broadcast_in_dim.104
  1.4 7.4 %all-to-all-start = ((s32[16,1,88]{2,1,0:T(1,128)}), s32[16,1,88]{2,1,0:T(1,128)S(1)}, u32[]{:S(2)}, u32[]{:S(2)}) async-start(s32[16,1,88]{2,1,0:T(1,128)} %broadcast_in_dim.104), calls=%async_computation | async-start | bytes 16384 | tf_op jit(solution)/shard_map/all_to_all | solution.py:457
  8.8 1.3 %sine_multiply_fusion.weight_ref = f32[80]{0:T(128)} fusion(s32[80]{0:T(128)} %lat_ref.3), kind=kLoop, calls=%fused_computation.58 | loop fusion | flops 320 | bytes 640 | tf_op jit(solution)/shard_map/mul | solution.py:460
  10.1 5.0 %all-to-all-done = s32[16,1,88]{2,1,0:T(1,128)S(1)} async-done(((s32[16,1,88]{2,1,0:T(1,128)}), s32[16,1,88]{2,1,0:T(1,128)S(1)}, u32[]{:S(2)}, u32[]{:S(2)}) %all-to-all-start) | async-done | bytes 5664 | tf_op jit(solution)/shard_map/all_to_all | solution.py:457
  15.1 0.6 convert_element_type.84.given_ref
  15.7 12.9 %analyse.1 = (f32[16,80,128]{2,1,0:T(8,128)}, bf16[8,80,128]{2,1,0:T(8,128)(2,1)}, f32[1,128]{1,0:T(1,128)}) custom-call(s32[1280]{0:T(1024)} %points_ref.3, s32[80]{0:T(128)} %lat_ref.3, f32[80]{0:T(128)} %sine_multiply_fusion.weight_ref, f32[2,2]{1,0:T(2,128)} %coupling_ref.1, bf16[4,6560,128]{2,1,0:T(8,128)(2,1)} %bitcast.18, ...), custom_call_target="tpu_custom_call" | custom-call | tf_op jit(solution)/shard_map/analyse/pallas_call | solution.py:184
  28.7 3.4 %collective-permute-start = (bf16[8,80,128]{2,1,0:T(8,128)(2,1)}, bf16[8,80,128]{2,1,0:T(8,128)(2,1)S(1)}, u32[]{:S(2)}, u32[]{:S(2)}) collective-permute-start(bf16[8,80,128]{2,1,0:T(8,128)(2,1)} %get-tuple-element.11), channel_id=1, source_target_pairs={{0,1},{2,3},{4,5},{6,7},{8,9},{10,11},{12,13},{14,15},{16,17},{18,... | collective-permute-start | bytes 491528 | tf_op jit(solution)/shard_map/ppermute | solution.py:464
  32.1 0.1 sine_log_fusion
  32.2 0.1 reshape.412
  32.3 0.1 cos.12
  32.4 0.6 reshape.407.cos_ref
  33.0 2.8 %collective-permute-done.earlier_ref = bf16[8,80,128]{2,1,0:T(8,128)(2,1)S(1)} collective-permute-done((bf16[8,80,128]{2,1,0:T(8,128)(2,1)}, bf16[8,80,128]{2,1,0:T(8,128)(2,1)S(1)}, u32[]{:S(2)}, u32[]{:S(2)}) %collective-permute-start) | collective-permute-done | bytes 163872 | tf_op jit(solution)/shard_map/ppermute | solution.py:464
  35.8 0.0 copy-start.1
  35.8 0.7 copy-done.1
  36.4 2.3 %mix.1 = bf16[16,80,128]{2,1,0:T(8,128)(2,1)} custom-call(f32[16,80,128]{2,1,0:T(8,128)} %get-tuple-element.10.own_ref, bf16[8,80,128]{2,1,0:T(8,128)(2,1)} %copy-done.1), custom_call_target="tpu_custom_call" | custom-call | tf_op jit(solution)/shard_map/mix/pallas_call | solution.py:235
  38.7 0.5 broadcast.419
  39.2 1.3 %reduce.3 = f32[128]{0:T(128)S(1)} reduce(f32[1,128]{1,0:T(1,128)} %get-tuple-element.13.order_ref, f32[]{:T(128)} %broadcast.419), dimensions={0}, to_apply=%get-tuple-element.13.reduce_sub_computation.3 | reduce | bytes 1028 | tf_op jit(solution)/shard_map/optimization_barrier | solution.py:466
  40.5 0.1 reshape.405
  40.6 0.1 slice.20
  40.7 0.1 slice.19
  40.8 0.2 select_reduce_fusion
  41.0 3.6 %all-to-all-start.1 = ((bf16[16,80,128]{2,1,0:T(8,128)(2,1)}), bf16[16,80,128]{2,1,0:T(8,128)(2,1)S(1)}, u32[]{:S(2)}, u32[]{:S(2)}) async-start(bf16[16,80,128]{2,1,0:T(8,128)(2,1)} %mix.1), calls=%async_computation.1 | async-start | bytes 655360 | tf_op jit(solution)/shard_map/all_to_all | solution.py:467
  44.6 0.6 multiply_floor_fusion
  45.2 0.1 multiply_add_fusion
  45.3 0.1 fusion.22
  45.4 0.1 copy.19
  45.5 0.1 copy.18
  46.3 0.6 reshape.408.first_ref
  46.9 0.6 reshape.409.second_ref
  47.5 0.1 copy.20
  47.6 0.1 copy.22
  47.7 0.1 compare_convert_fusion.1
  47.8 0.1 copy.23
  47.9 0.1 copy.21
  48.0 1.4 %fusion.8.term_ref = f32[82,8,128]{2,1,0:T(8,128)} fusion(f32[82,8]{1,0:T(8,128)S(1)} %copy.23, f32[82,8]{1,0:T(8,128)S(1)} %copy.22, f32[82,8]{1,0:T(8,128)S(1)} %copy.21, f32[82,8]{1,0:T(8,128)S(1)} %copy.20, f32[128]{0:T(128)S(1)} %fusion.24, f32[82,8]{1,0:T(8,128)S(1)} %copy.19, f32[82,8]{1,0:T(8,128)S(1)} %copy.18, ...), kind=kLoop, calls=%fused_computation.16 | loop fusion | flops 2603008 | bytes 352640 | tf_op jit(solution)/shard_map/jit(_where)/select_n | solution.py:445
  49.4 6.2 %all-to-all-done.1.own_ref = bf16[16,80,128]{2,1,0:T(8,128)(2,1)S(1)} async-done(((bf16[16,80,128]{2,1,0:T(8,128)(2,1)}), bf16[16,80,128]{2,1,0:T(8,128)(2,1)S(1)}, u32[]{:S(2)}, u32[]{:S(2)}) %all-to-all-start.1) | async-done | bytes 327712 | tf_op jit(solution)/shard_map/all_to_all | solution.py:467
  55.6 0.0 copy-start
  55.6 0.7 copy-done
  56.3 22.0 %legendre.1 = bf16[16,80,128]{2,1,0:T(8,128)(2,1)} custom-call(s32[1]{0:T(128)} %bitcast.5.pairs_ref, bf16[16,80,128]{2,1,0:T(8,128)(2,1)} %copy-done, f32[8,640]{1,0:T(8,128)} %reshape.407.cos_ref, f32[8,640]{1,0:T(8,128)} %reshape.408.first_ref, f32[8,640]{1,0:T(8,128)} %reshape.409.second_ref, f32[82,8,128]{2,1,0:T(8,128)} %fusion.8.term_ref), custom_call_target="tpu_custom_call" | custom-call | tf_op jit(solution)/shard_map/legendre/pallas_call | solution.py:322
  78.4 15.3 %all_to_all.19.back_ref = bf16[16,80,128]{2,1,0:T(8,128)(2,1)} all-to-all(bf16[16,80,128]{2,1,0:T(8,128)(2,1)} %legendre.1), channel_id=1, replica_groups=mesh['band'=16,'fld'=2] {'band'}, dimensions={0} | all-to-all | bytes 655360 | tf_op jit(solution)/shard_map/all_to_all | solution.py:482
  93.6 11.4 %synthesise.1 = bf16[4,6560,128]{2,1,0:T(8,128)(2,1)} custom-call(s32[1280]{0:T(1024)} %points_ref.3, s32[80]{0:T(128)} %lat_ref.3, bf16[16,80,128]{2,1,0:T(8,128)(2,1)} %all_to_all.19.back_ref, f32[1,128]{1,0:T(1,128)} %get-tuple-element.13.order_ref), custom_call_target="tpu_custom_call" | custom-call | tf_op jit(solution)/shard_map/synthesise/pallas_call | solution.py:404
  (17 shorter events, 0.1 us)
Async XLA Ops:
  1.4 13.8 %all-to-all-start = ((s32[16,1,88]{2,1,0:T(1,128)}), s32[16,1,88]{2,1,0:T(1,128)S(1)}, u32[]{:S(2)}, u32[]{:S(2)}) async-start(s32[16,1,88]{2,1,0:T(1,128)} %broadcast_in_dim.104), calls=%async_computation | async-start | bytes 16384 | tf_op jit(solution)/shard_map/all_to_all | solution.py:457
  28.7 7.1 %collective-permute-start = (bf16[8,80,128]{2,1,0:T(8,128)(2,1)}, bf16[8,80,128]{2,1,0:T(8,128)(2,1)S(1)}, u32[]{:S(2)}, u32[]{:S(2)}) collective-permute-start(bf16[8,80,128]{2,1,0:T(8,128)(2,1)} %get-tuple-element.11), channel_id=1, source_target_pairs={{0,1},{2,3},{4,5},{6,7},{8,9},{10,11},{12,13},{14,15},{16,17},{18,... | collective-permute-start | bytes 491528 | tf_op jit(solution)/shard_map/ppermute | solution.py:464
  35.8 0.7 copy-start.1
  41.0 14.6 %all-to-all-start.1 = ((bf16[16,80,128]{2,1,0:T(8,128)(2,1)}), bf16[16,80,128]{2,1,0:T(8,128)(2,1)S(1)}, u32[]{:S(2)}, u32[]{:S(2)}) async-start(bf16[16,80,128]{2,1,0:T(8,128)(2,1)} %mix.1), calls=%async_computation.1 | async-start | bytes 655360 | tf_op jit(solution)/shard_map/all_to_all | solution.py:467
  55.6 0.7 copy-start

commit v5 on v4

--- a/solution.py
+++ b/solution.py
@@ -16,6 +16,8 @@
 STEPS = 32
 CHECK = 8
 RESCALE_LOG = 60.0 * math.log(2.0)
+EARLY = 16
+WIDE = 2
 
 
 def iota(shape, dim):
@@ -235,95 +237,209 @@
     return pl.pallas_call(kernel, name="mix", out_shape=jax.ShapeDtypeStruct((bands, slots, 128), BF))(own, earlier)
 
 
-def legendre(pairs, own, cosines, first_log, second_log, terms):
+def make_rows(block, term_ref, cos_ref, second_ref, state, rows_ref, base):
+    now, before, log_now = state
+    half = cos_ref.shape[1]
+    info = term_ref[block]
+    restart = jnp.broadcast_to(info[:, 97:98], (8, half)) > 0.5
+    current = jnp.where(restart, 1.0, now[...])
+    previous = jnp.where(restart, 0.0, before[...])
+    running = jnp.where(restart, second_ref[...], log_now[...])
+    cosine = cos_ref[...]
+    scale = None
+    held = None
+    for j in range(STEPS):
+        if j % CHECK == 0:
+            large = jnp.maximum(jnp.abs(current), jnp.abs(previous)) > 1.0
+            shrink = jnp.where(large, 2.0**-60, 1.0)
+            running = running + jnp.where(large, RESCALE_LOG, 0.0)
+            current = current * shrink
+            previous = previous * shrink
+            scale = jnp.exp(running)
+        value = current * scale
+        if j % 2 == 0:
+            held = value
+        else:
+            at = base + 8 * (j - 1)
+            rows_ref[at : at + 16, :] = jnp.concatenate([held, value], axis=0).astype(BF)
+        a = info[:, j : j + 1]
+        b = info[:, STEPS + j : STEPS + j + 1]
+        current, previous = (a * cosine) * current - b * previous, current
+    now[...] = current
+    before[...] = previous
+    log_now[...] = running
+
+
+def early_rows(band, orders, lats):
+    total = lats.shape[1]
+    half = total // 2
+    count = orders.shape[1]
+    height = 8 * STEPS
+    blocks = 4 * (-(-(NT + 1) // (2 * STEPS))) + 2
+
+    def kernel(band_ref, order_ref, lat_ref, rows_ref, term_ref, cos_ref, second_ref, now, before, log_now, pairs_ref):
+        step = pl.program_id(0)
+
+        @pl.when(step == 0)
+        def _():
+            line, lane = iota((8, count), 0), iota((8, count), 1)
+            target = 8 * band_ref[0] + 2 * (line % 4)
+            first = jnp.sum(jnp.where(lane == target, order_ref[...], 0.0), axis=1, keepdims=True)
+            second = jnp.sum(jnp.where(lane == target + 1, order_ref[...], 0.0), axis=1, keepdims=True)
+            index = (iota((1, NT + 1), 1) + 1).astype(F32)
+            terms = jnp.log(1.0 + 0.5 / index)
+            turned_cos, turned_sin = turn_cos_sin((lat_ref[...] + 0.5) * (1.0 / (4.0 * NH)))
+            log_sine = jnp.log(turned_sin)
+            top = iota((8, half), 0) < 4
+            cos_ref[...] = jnp.where(top, turned_cos[:, :half], turned_cos[:, half:])
+            side = jnp.where(top, log_sine[:, :half], log_sine[:, half:])
+            for order, target_ref in ((first, log_now), (second, second_ref)):
+                norm = jnp.sum(jnp.where(index <= order, terms, 0.0), axis=1, keepdims=True)
+                target_ref[...] = (0.5 * math.log(0.5) + 0.5 * norm) + order * side
+            now[...] = jnp.ones((8, half), F32)
+            before[...] = jnp.zeros((8, half), F32)
+            first = jnp.broadcast_to(first, (8, 128))
+            second = jnp.broadcast_to(second, (8, 128))
+            ends = jnp.floor((NT + STEPS - first) * (1.0 / STEPS))
+            stops = ends + jnp.floor((NT + STEPS - second) * (1.0 / STEPS))
+            pairs_ref[0] = jnp.max(jnp.floor((stops + 1.0) * 0.5).astype(jnp.int32))
+            lane = iota((8, 128), 1)
+            kind = lane // STEPS
+            tick = (lane % STEPS).astype(F32)
+            chain = 2.0 * (iota((8, 128), 0) % 4).astype(F32)
+
+            def fill(block, carry):
+                at = jnp.full((8, 128), block, jnp.int32).astype(F32)
+                late = at >= ends
+                order = jnp.where(late, second, first)
+                row = order + STEPS * jnp.where(late, at - ends, at) + tick
+                degree = row + 1.0
+                offset = degree - order
+                ahead = jnp.sqrt((4.0 * degree * degree - 1.0) / (offset * (degree + order)))
+                below = jnp.maximum(4.0 * row * row - 1.0, 1.0)
+                behind = jnp.sqrt((offset - 1.0) * (row + order) / below)
+                ahead = jnp.where(degree <= NT, ahead, 0.0)
+                damp = 1.0 / (1.0 + 4.0 * row * (row + 1.0) / (NT * (NT + 1.0)))
+                last = jnp.where(lane == 96, chain + jnp.where(late, 1.0, 0.0), jnp.where(at == ends, 1.0, 0.0))
+                rest = jnp.where(kind == 2, damp, last)
+                term_ref[block] = jnp.where(kind == 0, ahead, jnp.where(kind == 1, ahead * behind, rest))
+                return carry
+
+            lax.fori_loop(0, blocks, fill, 0)
+
+        @pl.when(step < (pairs_ref[0] + WIDE - 1) // WIDE * WIDE)
+        def _():
+            state = (now, before, log_now)
+            for k in range(2):
+                make_rows(2 * step + k, term_ref, cos_ref, second_ref, state, rows_ref, k * height)
+
+    whole = lambda *shape: pl.BlockSpec(shape, lambda i: (0,) * len(shape))
+    smem = pl.BlockSpec(memory_space=pltpu.SMEM)
+    wide = jax.ShapeDtypeStruct((8, half), F32)
+    return pl.pallas_call(
+        kernel,
+        name="early_rows",
+        grid=(EARLY,),
+        in_specs=[smem, whole(1, count), whole(1, total)],
+        out_specs=[pl.BlockSpec((2 * height, half), lambda i: (i, 0)), whole(blocks, 8, 128)] + [whole(8, half)] * 5 + [smem],
+        out_shape=[
+            jax.ShapeDtypeStruct((EARLY * 2 * height, half), BF),
+            jax.ShapeDtypeStruct((blocks, 8, 128), F32),
+            wide,
+            wide,
+            wide,
+            wide,
+            wide,
+            jax.ShapeDtypeStruct((1,), jnp.int32),
+        ],
+        compiler_params=pltpu.CompilerParams(dimension_semantics=("arbitrary",)),
+    )(band, orders, lats)
+
+
+def legendre(own, early):
     bands, slots, _ = own.shape
     total = bands * slots
     half = total // 2
     height = 8 * STEPS
-
-    def kernel(pairs_ref, own_ref, cos_ref, first_ref, second_ref, term_ref, out_ref, mixed, weights, even_rows, odd_rows, acc, now, before, log_now):
-        for b in range(bands):
-            mixed[b * slots : (b + 1) * slots] = own_ref[b].astype(F32)
-        weights[...] = jnp.concatenate([mixed[:half], mixed[half:]], axis=1).astype(BF)
-        acc[...] = jnp.zeros((256, half), F32)
-        now[...] = jnp.ones((8, half), F32)
-        before[...] = jnp.zeros((8, half), F32)
-        log_now[...] = first_ref[...]
+    blocks = early[1].shape[0]
+
+    def kernel(own_ref, early_ref, term_ref, cos_ref, second_ref, now_ref, before_ref, log_ref, pairs_ref, out_ref, mixed, weights, even_rows, odd_rows, acc, now, before, log_now):
+        step = pl.program_id(0)
+        pairs = pairs_ref[0]
         line, lane = iota((8, 128), 0), iota((8, 128), 1)
         low = line < 4
 
-        def make(block, rows_ref):
-            info = term_ref[block]
-            restart = jnp.broadcast_to(info[:, 97:98], (8, half)) > 0.5
-            current = jnp.where(restart, 1.0, now[...])
-            previous = jnp.where(restart, 0.0, before[...])
-            running = jnp.where(restart, second_ref[...], log_now[...])
-            cosine = cos_ref[...]
-            scale = None
-            held = None
-            for j in range(STEPS):
-                if j % CHECK == 0:
-                    large = jnp.maximum(jnp.abs(current), jnp.abs(previous)) > 1.0
-                    shrink = jnp.where(large, 2.0**-60, 1.0)
-                    running = running + jnp.where(large, RESCALE_LOG, 0.0)
-                    current = current * shrink
-                    previous = previous * shrink
-                    scale = jnp.exp(running)
-                value = current * scale
-                if j % 2 == 0:
-                    held = value
-                else:
-                    rows_ref[8 * (j - 1) : 8 * (j + 1), :] = jnp.concatenate([held, value], axis=0).astype(BF)
-                a = info[:, j : j + 1]
-                b = info[:, STEPS + j : STEPS + j + 1]
-                current, previous = (a * cosine) * current - b * previous, current
-            now[...] = current
-            before[...] = previous
-            log_now[...] = running
-
-        def use(block, rows_ref):
-            info = term_ref[block]
-            rows = rows_ref[...]
+        @pl.when(step == 0)
+        def _():
+            for b in range(bands):
+                mixed[b * slots : (b + 1) * slots] = own_ref[b].astype(F32)
+            weights[...] = jnp.concatenate([mixed[:half], mixed[half:]], axis=1).astype(BF)
+            acc[...] = jnp.zeros((256, half), F32)
+
+        def use(block, rows, number):
             found = jnp.dot(rows, weights[...], preferred_element_type=F32)
-            which = jnp.broadcast_to(info[:, 96:97], (8, 128)).astype(jnp.int32)
-            hit = lane % 8 == which
-            masks = []
-            for parity in range(2):
-                match = hit & (lane // 64 == parity)
-                masks.append((match & low, match & ~low))
             tops, lows = [], []
-            for j in range(STEPS):
-                part = found[8 * j : 8 * j + 8]
-                part = jnp.where(low, part[:, :128], part[:, 128:])
-                part = (part + pltpu.roll(part, 4, 0)) * info[:, 2 * STEPS + j : 2 * STEPS + j + 1]
-                tops.append(jnp.where(masks[j % 2][0], part, 0.0))
-                lows.append(jnp.where(masks[j % 2][1], part, 0.0))
+            for k in range(number):
+                info = term_ref[block + k]
+                which = jnp.broadcast_to(info[:, 96:97], (8, 128)).astype(jnp.int32)
+                hit = lane % 8 == which
+                masks = []
+                for parity in range(2):
+                    match = hit & (lane // 64 == parity)
+                    masks.append((match & low, match & ~low))
+                for j in range(STEPS):
+                    at = k * height + 8 * j
+                    part = found[at : at + 8]
+                    part = jnp.where(low, part[:, :128], part[:, 128:])
+                    part = (part + pltpu.roll(part, 4, 0)) * info[:, 2 * STEPS + j : 2 * STEPS + j + 1]
+                    tops.append(jnp.where(masks[j % 2][0], part, 0.0))
+                    lows.append(jnp.where(masks[j % 2][1], part, 0.0))
             kept = jnp.concatenate([jnp.concatenate(tops, axis=0), jnp.concatenate(lows, axis=0)], axis=1).astype(BF)
             acc[...] += lax.dot_general(kept, rows, (((0,), (0,)), ((), ())), preferred_element_type=F32)
 
-        make(0, even_rows)
-
-        def body(i, carry):
-            make(2 * i + 1, odd_rows)
-            use(2 * i, even_rows)
-            make(2 * i + 2, even_rows)
-            use(2 * i + 1, odd_rows)
-            return carry
-
-        lax.fori_loop(0, pairs_ref[0], body, 0)
-        for h in range(2):
-            for c in range(half // 128):
-                at = h * half + 128 * c
-                mixed[at : at + 128] = jnp.transpose(acc[128 * h : 128 * h + 128, 128 * c : 128 * c + 128])
-        for b in range(bands):
-            out_ref[b] = mixed[b * slots : (b + 1) * slots].astype(BF)
-
-    vmem = pl.BlockSpec(memory_space=pltpu.VMEM)
+        @pl.when(step * WIDE < pairs)
+        def _():
+            for k in range(0, 2 * WIDE, 2):
+                use(2 * WIDE * step + k, early_ref[k * height : (k + 2) * height], 2)
+
+        @pl.when(step == EARLY // WIDE - 1)
+        def _():
+            now[...] = now_ref[...]
+            before[...] = before_ref[...]
+            log_now[...] = log_ref[...]
+            state = (now, before, log_now)
+
+            def make(block, rows_ref):
+                make_rows(block, term_ref, cos_ref, second_ref, state, rows_ref, 0)
+
+            @pl.when(pairs > EARLY)
+            def _():
+                make(2 * EARLY, even_rows)
+
+            def body(i, carry):
+                make(2 * i + 1, odd_rows)
+                use(2 * i, even_rows[...], 1)
+                make(2 * i + 2, even_rows)
+                use(2 * i + 1, odd_rows[...], 1)
+                return carry
+
+            lax.fori_loop(EARLY, pairs, body, 0)
+            for h in range(2):
+                for c in range(half // 128):
+                    at = h * half + 128 * c
+                    mixed[at : at + 128] = jnp.transpose(acc[128 * h : 128 * h + 128, 128 * c : 128 * c + 128])
+            for b in range(bands):
+                out_ref[b] = mixed[b * slots : (b + 1) * slots].astype(BF)
+
+    whole = lambda *shape: pl.BlockSpec(shape, lambda i: (0,) * len(shape))
     return pl.pallas_call(
         kernel,
         name="legendre",
-        in_specs=[pl.BlockSpec(memory_space=pltpu.SMEM)] + [vmem] * 5,
-        out_specs=vmem,
+        grid=(EARLY // WIDE,),
+        in_specs=[whole(bands, slots, 128), pl.BlockSpec((2 * WIDE * height, half), lambda i: (i, 0)), whole(blocks, 8, 128)]
+        + [whole(8, half)] * 5
+        + [pl.BlockSpec(memory_space=pltpu.SMEM)],
+        out_specs=whole(bands, slots, 128),
         out_shape=jax.ShapeDtypeStruct((bands, slots, 128), BF),
         scratch_shapes=[
             pltpu.VMEM((total, 128), F32),
@@ -335,7 +451,8 @@
             pltpu.VMEM((8, half), F32),
             pltpu.VMEM((8, half), F32),
         ],
-    )(pairs, own, cosines, first_log, second_log, terms)
+        compiler_params=pltpu.CompilerParams(dimension_semantics=("arbitrary",)),
+    )(own, *early)
 
 
 def synthesise(back, points, lat_ids, orders, nv, nl, width):
@@ -418,34 +535,6 @@
     )(points, lat_ids, back, orders)
 
 
-def recurrence_terms(mine):
-    first, second = mine[0::2], mine[1::2]
-    ends = jnp.floor((NT + STEPS - first) / STEPS)
-    stops = ends + jnp.floor((NT + STEPS - second) / STEPS)
-    pairs = jnp.floor((jnp.max(stops) + 1.0) / 2.0).astype(jnp.int32).reshape(1)
-    blocks = 4 * (-(-(NT + 1) // (2 * STEPS))) + 2
-    block = jnp.arange(blocks).astype(F32)[:, None]
-    late = block >= ends[None]
-    order = jnp.tile(jnp.where(late, second[None], first[None]), (1, 2))[:, :, None]
-    start = jnp.tile(STEPS * jnp.where(late, block - ends[None], block), (1, 2))[:, :, None]
-    which = jnp.tile(2.0 * jnp.arange(4).astype(F32)[None] + late, (1, 2))[:, :, None]
-    restart = jnp.tile((block == ends[None]).astype(F32), (1, 2))[:, :, None]
-    lane = jnp.arange(128)[None, None, :]
-    step = (lane % STEPS).astype(F32)
-    offset = start + step + 1.0
-    degree = order + offset
-    ahead = jnp.sqrt((4.0 * degree * degree - 1.0) / (offset * (2.0 * order + offset)))
-    below = 4.0 * (degree - 1.0) * (degree - 1.0) - 1.0
-    behind = jnp.sqrt(jnp.maximum((offset - 1.0) * (2.0 * order + offset - 1.0) / below, 0.0))
-    ahead = jnp.where(degree <= NT, ahead, 0.0)
-    row = order + start + step
-    damp = 1.0 / (1.0 + 4.0 * row * (row + 1.0) / (NT * (NT + 1.0)))
-    kind = lane // STEPS
-    last = jnp.where(lane == 96, which, restart)
-    terms = jnp.where(kind == 0, ahead, jnp.where(kind == 1, ahead * behind, jnp.where(kind == 2, damp, last)))
-    return pairs, terms
-
-
 def solution(mesh):
     bands, parts = mesh.shape["band"], mesh.shape["fld"]
 
@@ -465,20 +554,8 @@
             earlier = moved if shift == 1 else earlier + moved
         own, orders = lax.optimization_barrier((mix(own, earlier, bands, nv, nl), orders))
         own = lax.all_to_all(own, "band", split_axis=0, concat_axis=0, tiled=True)
-        half = bands * slots // 2
-        colatitude = (math.pi * (lats + 0.5) / (2.0 * NH)).reshape(2, 1, half)
-        local = lax.dynamic_index_in_dim(orders.reshape(bands, mine), lax.axis_index("band"), 0, False)
-        index = jnp.arange(1, NT + 1).astype(F32)
-        log_norm = 0.5 * math.log(0.5) + 0.5 * jnp.sum(
-            jnp.where(index[None, :] <= local[:, None], jnp.log1p(0.5 / index)[None, :], 0.0), axis=1
-        )
-        log_sine = jnp.log(jnp.sin(colatitude))
-        start_log = log_norm[None, :, None] + local[None, :, None] * log_sine
-        first_log = start_log[:, 0::2].reshape(mine, half)
-        second_log = start_log[:, 1::2].reshape(mine, half)
-        cosines = jnp.broadcast_to(jnp.cos(colatitude), (2, mine // 2, half)).reshape(mine, half)
-        pairs, terms = recurrence_terms(local)
-        back = legendre(pairs, own, cosines, first_log, second_log, terms)
+        band = lax.axis_index("band").astype(jnp.int32).reshape(1)
+        back = legendre(own, early_rows(band, orders, lats))
         back = lax.all_to_all(back, "band", split_axis=0, concat_axis=0, tiled=True)
         rows = synthesise(back, points, lat_ids, orders, nv, nl, width)
         return from_rows(rows, nv, nl, slots, width)

time: 106 us -> 107 us (level)
  Pallas kernels: 48.6 us -> 60.4 us
  waiting for transfers between devices: 14 us -> 8.77 us
  other arithmetic: 5.91 us -> 2.11 us
  local copies, waits for them, and re-layouts: 6.06 us -> 3.34 us
  blocking collectives: 15.3 us -> 17.1 us
    pallas_call x1 -> x2, Pallas kernels: 22 us -> 33.8 us  [the longest x1 20.2 us: legendre(): pl.pallas_call(kernel, name='legendre', grid=(EARLY // WIDE,), in_specs=[...]
    all_to_all x1, waiting for transfers between devices: 6.23 us -> 0.01 us  [on_device(): own = lax.all_to_all(own, 'band', split_axis=0, concat_axis=0, tiled=True)]
    reshape x4 -> x0, local copies, waits for them, and re-layouts: 1.91 us -> none  [the longest x1 0.61 us: on_device(): first_log = start_log[:, 0::2].reshape(mine, half)]
    all_to_all x1, blocking collectives: 15.3 us -> 17.1 us  [on_device(): back = lax.all_to_all(back, 'band', split_axis=0, concat_axis=0, tiled=True)]
    select_n x1 -> x0, other arithmetic: 1.42 us -> none  [recurrence_terms(): jnp.where(kind == 0, ahead, jnp.where(kind == 1, ahead * behind, jnp.wher...]
    optimization_barrier x1 -> x0, other arithmetic: 1.28 us -> none  [on_device(): lax.optimization_barrier((mix(own, earlier, bands, nv, nl), orders))]
  transfers between devices with their start and end apart: 3 -> 3, of which waited for: 3 -> 2; matrix products, arithmetic and copies ran while one was open for 6% -> 2% of each run, Pallas kernels for 0% -> 13%
where the time goes in v5:
time: 107 us; the launch traced here: 106 us
  Pallas kernels  60.4 us (56%)
  blocking collectives  17.1 us (16%)
  starting transfers between devices  14.3 us (13%)
  waiting for transfers between devices  8.77 us (8%)
  local copies, waits for them, and re-layouts  3.34 us (3%)
  other arithmetic  2.11 us (2%)
    pallas_call x1, Pallas kernels, legendre(): pl.pallas_call(kernel, name='legendre', grid=(EARLY // WIDE,), in_specs=[...  20.2 us
    all_to_all x1, blocking collectives, on_device(): back = lax.all_to_all(back, 'band', split_axis=0, concat_axis=0, tiled=True)  17.1 us
    pallas_call x1, Pallas kernels, early_rows(): pl.pallas_call(kernel, name='early_rows', grid=(EARLY,), in_specs=[smem,...  13.6 us
    pallas_call x1, Pallas kernels, analyse(): pl.pallas_call(kernel, name='analyse', grid=(grid,), in_specs=[smem, smem...  12.9 us
    pallas_call x1, Pallas kernels, synthesise(): pl.pallas_call(kernel, name='synthesise', grid=(grid,), in_specs=[smem, s...  11.4 us
    all_to_all x1, starting transfers between devices, on_device(): lax.all_to_all(spread, 'band', split_axis=0, concat_axis=0, tiled=True)  7.39 us
    all_to_all x1, waiting for transfers between devices, on_device(): lax.all_to_all(spread, 'band', split_axis=0, concat_axis=0, tiled=True)  5.07 us
    ppermute x1, waiting for transfers between devices, on_device(): lax.ppermute(sums, 'fld', [(k, k + shift) for k in range(parts - shift)])  3.7 us
  transfers between devices with their start and end apart: 3, of which 2 were waited for; matrix products, arithmetic and copies ran while one was open for 2% of the time, Pallas kernels for 13%

profile of v5, /device:TPU:0, one launch (start us, length us, event | category | flops | bytes accessed | tf_op | source)
XLA Modules:
  0.0 106.2 jit_solution(2848990209423416945)
XLA Ops:
  0.0 0.7 pad_add_fusion
  0.7 0.6 broadcast_in_dim.2
  1.4 7.4 %all-to-all-start = ((s32[16,1,88]{2,1,0:T(1,128)}), s32[16,1,88]{2,1,0:T(1,128)S(1)}, u32[]{:S(2)}, u32[]{:S(2)}) async-start(s32[16,1,88]{2,1,0:T(1,128)} %broadcast_in_dim.2), calls=%async_computation | async-start | bytes 16384 | tf_op jit(solution)/shard_map/all_to_all | solution.py:546
  8.7 1.3 %sine_multiply_fusion.weight_ref = f32[80]{0:T(128)} fusion(s32[80]{0:T(128)} %lat_ref.3), kind=kLoop, calls=%fused_computation.3 | loop fusion | flops 320 | bytes 640 | tf_op jit(solution)/shard_map/mul | solution.py:549
  10.0 5.1 %all-to-all-done = s32[16,1,88]{2,1,0:T(1,128)S(1)} async-done(((s32[16,1,88]{2,1,0:T(1,128)}), s32[16,1,88]{2,1,0:T(1,128)S(1)}, u32[]{:S(2)}, u32[]{:S(2)}) %all-to-all-start) | async-done | bytes 5664 | tf_op jit(solution)/shard_map/all_to_all | solution.py:546
  15.1 0.7 convert_element_type.15.given_ref
  15.8 12.9 %analyse.1 = (f32[16,80,128]{2,1,0:T(8,128)}, bf16[8,80,128]{2,1,0:T(8,128)(2,1)}, f32[1,128]{1,0:T(1,128)}) custom-call(s32[1280]{0:T(1024)} %points_ref.3, s32[80]{0:T(128)} %lat_ref.3, f32[80]{0:T(128)} %sine_multiply_fusion.weight_ref, f32[2,2]{1,0:T(2,128)} %coupling_ref.1, bf16[4,6560,128]{2,1,0:T(8,128)(2,1)} %bitcast.12, ...), custom_call_target="tpu_custom_call" | custom-call | tf_op jit(solution)/shard_map/analyse/pallas_call | solution.py:186
  28.7 3.4 %collective-permute-start = (bf16[8,80,128]{2,1,0:T(8,128)(2,1)}, bf16[8,80,128]{2,1,0:T(8,128)(2,1)S(1)}, u32[]{:S(2)}, u32[]{:S(2)}) collective-permute-start(bf16[8,80,128]{2,1,0:T(8,128)(2,1)} %get-tuple-element.19), channel_id=1, source_target_pairs={{0,1},{2,3},{4,5},{6,7},{8,9},{10,11},{12,13},{14,15},{16,17},{18,... | collective-permute-start | bytes 491528 | tf_op jit(solution)/shard_map/ppermute | solution.py:553
  32.1 3.7 %collective-permute-done.earlier_ref = bf16[8,80,128]{2,1,0:T(8,128)(2,1)S(1)} collective-permute-done((bf16[8,80,128]{2,1,0:T(8,128)(2,1)}, bf16[8,80,128]{2,1,0:T(8,128)(2,1)S(1)}, u32[]{:S(2)}, u32[]{:S(2)}) %collective-permute-start) | collective-permute-done | bytes 163872 | tf_op jit(solution)/shard_map/ppermute | solution.py:553
  35.8 0.0 copy-start.1
  35.8 0.6 copy-done.1
  36.5 2.3 %mix.1 = bf16[16,80,128]{2,1,0:T(8,128)(2,1)} custom-call(f32[16,80,128]{2,1,0:T(8,128)} %get-tuple-element.18.own_ref, bf16[8,80,128]{2,1,0:T(8,128)(2,1)} %copy-done.1), custom_call_target="tpu_custom_call" | custom-call | tf_op jit(solution)/shard_map/mix/pallas_call | solution.py:237
  38.8 3.5 %all-to-all-start.1 = ((bf16[16,80,128]{2,1,0:T(8,128)(2,1)}), bf16[16,80,128]{2,1,0:T(8,128)(2,1)S(1)}, u32[]{:S(2)}, u32[]{:S(2)}) async-start(bf16[16,80,128]{2,1,0:T(8,128)(2,1)} %mix.1), calls=%async_computation.1 | async-start | bytes 655360 | tf_op jit(solution)/shard_map/all_to_all | solution.py:556
  42.4 0.1 slice_convert_fusion
  42.4 0.7 convert_element_type.17.lat_ref
  43.1 13.6 %early_rows.1 = (bf16[8192,640]{1,0:T(8,128)(2,1)}, f32[82,8,128]{2,1,0:T(8,128)}, f32[8,640]{1,0:T(8,128)}, f32[8,640]{1,0:T(8,128)}, f32[8,640]{1,0:T(8,128)},...) custom-call(s32[1]{0:T(128)} %bitcast.4.band_ref, f32[1,128]{1,0:T(1,128)} %get-tuple-element.22.order_ref, ...), custom_call_target="tpu_custom_call" | custom-call | tf_op jit(solution)/shard_map/early_rows/pallas_call | solution.py:339
  56.7 0.0 all-to-all-done.1.own_ref
  56.7 0.0 copy-start
  56.7 0.7 copy-done
  57.5 20.2 %legendre.1 = bf16[16,80,128]{2,1,0:T(8,128)(2,1)} custom-call(bf16[16,80,128]{2,1,0:T(8,128)(2,1)} %copy-done, bf16[8192,640]{1,0:T(8,128)(2,1)} %get-tuple-element.23.early_ref, f32[82,8,128]{2,1,0:T(8,128)} %get-tuple-element.24.term_ref, f32[8,640]{1,0:T(8,128)} %get-tuple-element.25.cos_ref, f32[8,640]{1,0:T(8,128)} %get-tuple-element.26.second_ref, ...), custom_call_target="tpu_custom_call" | custom-call | tf_op jit(solution)/shard_map/legendre/pallas_call | solution.py:435
  77.6 17.1 %all_to_all.19.back_ref = bf16[16,80,128]{2,1,0:T(8,128)(2,1)} all-to-all(bf16[16,80,128]{2,1,0:T(8,128)(2,1)} %legendre.1), channel_id=1, replica_groups=mesh['band'=16,'fld'=2] {'band'}, dimensions={0} | all-to-all | bytes 655360 | tf_op jit(solution)/shard_map/all_to_all | solution.py:559
  94.8 11.4 %synthesise.1 = bf16[4,6560,128]{2,1,0:T(8,128)(2,1)} custom-call(s32[1280]{0:T(1024)} %points_ref.3, s32[80]{0:T(128)} %lat_ref.3, bf16[16,80,128]{2,1,0:T(8,128)(2,1)} %all_to_all.19.back_ref, f32[1,128]{1,0:T(1,128)} %get-tuple-element.22.order_ref), custom_call_target="tpu_custom_call" | custom-call | tf_op jit(solution)/shard_map/synthesise/pallas_call | solution.py:521
  (1 shorter events, 0.0 us)
Async XLA Ops:
  1.4 13.8 %all-to-all-start = ((s32[16,1,88]{2,1,0:T(1,128)}), s32[16,1,88]{2,1,0:T(1,128)S(1)}, u32[]{:S(2)}, u32[]{:S(2)}) async-start(s32[16,1,88]{2,1,0:T(1,128)} %broadcast_in_dim.2), calls=%async_computation | async-start | bytes 16384 | tf_op jit(solution)/shard_map/all_to_all | solution.py:546
  28.7 7.1 %collective-permute-start = (bf16[8,80,128]{2,1,0:T(8,128)(2,1)}, bf16[8,80,128]{2,1,0:T(8,128)(2,1)S(1)}, u32[]{:S(2)}, u32[]{:S(2)}) collective-permute-start(bf16[8,80,128]{2,1,0:T(8,128)(2,1)} %get-tuple-element.19), channel_id=1, source_target_pairs={{0,1},{2,3},{4,5},{6,7},{8,9},{10,11},{12,13},{14,15},{16,17},{18,... | collective-permute-start | bytes 491528 | tf_op jit(solution)/shard_map/ppermute | solution.py:553
  35.8 0.6 copy-start.1
  38.8 17.9 %all-to-all-start.1 = ((bf16[16,80,128]{2,1,0:T(8,128)(2,1)}), bf16[16,80,128]{2,1,0:T(8,128)(2,1)S(1)}, u32[]{:S(2)}, u32[]{:S(2)}) async-start(bf16[16,80,128]{2,1,0:T(8,128)(2,1)} %mix.1), calls=%async_computation.1 | async-start | bytes 655360 | tf_op jit(solution)/shard_map/all_to_all | solution.py:556
  56.7 0.7 copy-start

commit v6 on v4

--- a/solution.py
+++ b/solution.py
@@ -235,58 +235,130 @@
     return pl.pallas_call(kernel, name="mix", out_shape=jax.ShapeDtypeStruct((bands, slots, 128), BF))(own, earlier)
 
 
-def legendre(pairs, own, cosines, first_log, second_log, terms):
+def make_rows(block, term_ref, cos_ref, second_ref, state, rows_ref, base):
+    now, before, log_now = state
+    half = cos_ref.shape[1]
+    info = term_ref[block]
+    restart = jnp.broadcast_to(info[:, 97:98], (8, half)) > 0.5
+    current = jnp.where(restart, 1.0, now[...])
+    previous = jnp.where(restart, 0.0, before[...])
+    running = jnp.where(restart, second_ref[...], log_now[...])
+    cosine = cos_ref[...]
+    scale = None
+    held = None
+    for j in range(STEPS):
+        if j % CHECK == 0:
+            large = jnp.maximum(jnp.abs(current), jnp.abs(previous)) > 1.0
+            shrink = jnp.where(large, 2.0**-60, 1.0)
+            running = running + jnp.where(large, RESCALE_LOG, 0.0)
+            current = current * shrink
+            previous = previous * shrink
+            scale = jnp.exp(running)
+        value = current * scale
+        if j % 2 == 0:
+            held = value
+        else:
+            at = base + 8 * (j - 1)
+            rows_ref[at : at + 16, :] = jnp.concatenate([held, value], axis=0).astype(BF)
+        a = info[:, j : j + 1]
+        b = info[:, STEPS + j : STEPS + j + 1]
+        current, previous = (a * cosine) * current - b * previous, current
+    now[...] = current
+    before[...] = previous
+    log_now[...] = running
+
+
+def plan(band, orders, lats):
+    total = lats.shape[1]
+    half = total // 2
+    count = orders.shape[1]
+    blocks = 4 * (-(-2 * (NT + 1) // (4 * STEPS))) + 2
+
+    def kernel(band_ref, order_ref, lat_ref, term_ref, cos_ref, first_ref, second_ref, quads_ref):
+        line, lane = iota((8, count), 0), iota((8, count), 1)
+        target = 8 * band_ref[0] + 2 * (line % 4)
+        first = jnp.sum(jnp.where(lane == target, order_ref[...], 0.0), axis=1, keepdims=True)
+        second = jnp.sum(jnp.where(lane == target + 1, order_ref[...], 0.0), axis=1, keepdims=True)
+        index = (iota((1, NT + 1), 1) + 1).astype(F32)
+        terms = jnp.log(1.0 + 0.5 / index)
+        turned_cos, turned_sin = turn_cos_sin((lat_ref[...] + 0.5) * (1.0 / (4.0 * NH)))
+        log_sine = jnp.log(turned_sin)
+        top = iota((8, half), 0) < 4
+        cos_ref[...] = jnp.where(top, turned_cos[:, :half], turned_cos[:, half:])
+        side = jnp.where(top, log_sine[:, :half], log_sine[:, half:])
+        for order, target_ref in ((first, first_ref), (second, second_ref)):
+            norm = jnp.sum(jnp.where(index <= order, terms, 0.0), axis=1, keepdims=True)
+            target_ref[...] = (0.5 * math.log(0.5) + 0.5 * norm) + order * side
+        first = jnp.broadcast_to(first, (8, 128))
+        second = jnp.broadcast_to(second, (8, 128))
+        ends = jnp.floor((NT + STEPS - first) * (1.0 / STEPS))
+        stops = ends + jnp.floor((NT + STEPS - second) * (1.0 / STEPS))
+        quads_ref[0] = jnp.max(jnp.floor((stops + 3.0) * 0.25).astype(jnp.int32))
+        lane = iota((8, 128), 1)
+        kind = lane // STEPS
+        tick = (lane % STEPS).astype(F32)
+        chain = 2.0 * (iota((8, 128), 0) % 4).astype(F32)
+
+        def fill(block, carry):
+            at = jnp.full((8, 128), block, jnp.int32).astype(F32)
+            late = at >= ends
+            order = jnp.where(late, second, first)
+            row = order + STEPS * jnp.where(late, at - ends, at) + tick
+            degree = row + 1.0
+            offset = degree - order
+            ahead = jnp.sqrt((4.0 * degree * degree - 1.0) / (offset * (degree + order)))
+            below = jnp.maximum(4.0 * row * row - 1.0, 1.0)
+            behind = jnp.sqrt((offset - 1.0) * (row + order) / below)
+            ahead = jnp.where(degree <= NT, ahead, 0.0)
+            damp = 1.0 / (1.0 + 4.0 * row * (row + 1.0) / (NT * (NT + 1.0)))
+            last = jnp.where(lane == 96, chain + jnp.where(late, 1.0, 0.0), jnp.where(at == ends, 1.0, 0.0))
+            rest = jnp.where(kind == 2, damp, last)
+            term_ref[block] = jnp.where(kind == 0, ahead, jnp.where(kind == 1, ahead * behind, rest))
+            return carry
+
+        lax.fori_loop(0, blocks, fill, 0, unroll=2)
+
+    smem = pl.BlockSpec(memory_space=pltpu.SMEM)
+    vmem = pl.BlockSpec(memory_space=pltpu.VMEM)
+    wide = jax.ShapeDtypeStruct((8, half), F32)
+    return pl.pallas_call(
+        kernel,
+        name="plan",
+        in_specs=[smem, vmem, vmem],
+        out_specs=[vmem] * 4 + [smem],
+        out_shape=[jax.ShapeDtypeStruct((blocks, 8, 128), F32), wide, wide, wide, jax.ShapeDtypeStruct((1,), jnp.int32)],
+    )(band, orders, lats)
+
+
+def legendre(own, tables):
     bands, slots, _ = own.shape
     total = bands * slots
     half = total // 2
     height = 8 * STEPS
 
-    def kernel(pairs_ref, own_ref, cos_ref, first_ref, second_ref, term_ref, out_ref, mixed, weights, even_rows, odd_rows, acc, now, before, log_now):
+    def kernel(own_ref, term_ref, cos_ref, first_ref, second_ref, quads_ref, out_ref, mixed, weights, rows0, rows1, rows2, rows3, kept0, kept1, acc, now, before, log_now):
+        rows = (rows0, rows1, rows2, rows3)
+        kept = (kept0, kept1)
+        line, lane = iota((8, 128), 0), iota((8, 128), 1)
+        low = line < 4
         for b in range(bands):
             mixed[b * slots : (b + 1) * slots] = own_ref[b].astype(F32)
         weights[...] = jnp.concatenate([mixed[:half], mixed[half:]], axis=1).astype(BF)
         acc[...] = jnp.zeros((256, half), F32)
+        rows3[...] = jnp.zeros((height, half), BF)
+        kept1[...] = jnp.zeros((height, 256), BF)
         now[...] = jnp.ones((8, half), F32)
         before[...] = jnp.zeros((8, half), F32)
         log_now[...] = first_ref[...]
-        line, lane = iota((8, 128), 0), iota((8, 128), 1)
-        low = line < 4
-
-        def make(block, rows_ref):
+        state = (now, before, log_now)
+
+        def make(block, target):
+            make_rows(block, term_ref, cos_ref, second_ref, state, target, 0)
+
+        def analysed(block, source, target):
+            found = jnp.dot(source[...], weights[...], preferred_element_type=F32)
             info = term_ref[block]
-            restart = jnp.broadcast_to(info[:, 97:98], (8, half)) > 0.5
-            current = jnp.where(restart, 1.0, now[...])
-            previous = jnp.where(restart, 0.0, before[...])
-            running = jnp.where(restart, second_ref[...], log_now[...])
-            cosine = cos_ref[...]
-            scale = None
-            held = None
-            for j in range(STEPS):
-                if j % CHECK == 0:
-                    large = jnp.maximum(jnp.abs(current), jnp.abs(previous)) > 1.0
-                    shrink = jnp.where(large, 2.0**-60, 1.0)
-                    running = running + jnp.where(large, RESCALE_LOG, 0.0)
-                    current = current * shrink
-                    previous = previous * shrink
-                    scale = jnp.exp(running)
-                value = current * scale
-                if j % 2 == 0:
-                    held = value
-                else:
-                    rows_ref[8 * (j - 1) : 8 * (j + 1), :] = jnp.concatenate([held, value], axis=0).astype(BF)
-                a = info[:, j : j + 1]
-                b = info[:, STEPS + j : STEPS + j + 1]
-                current, previous = (a * cosine) * current - b * previous, current
-            now[...] = current
-            before[...] = previous
-            log_now[...] = running
-
-        def use(block, rows_ref):
-            info = term_ref[block]
-            rows = rows_ref[...]
-            found = jnp.dot(rows, weights[...], preferred_element_type=F32)
-            which = jnp.broadcast_to(info[:, 96:97], (8, 128)).astype(jnp.int32)
-            hit = lane % 8 == which
+            hit = lane % 8 == jnp.broadcast_to(info[:, 96:97], (8, 128)).astype(jnp.int32)
             masks = []
             for parity in range(2):
                 match = hit & (lane // 64 == parity)
@@ -298,19 +370,24 @@
                 part = (part + pltpu.roll(part, 4, 0)) * info[:, 2 * STEPS + j : 2 * STEPS + j + 1]
                 tops.append(jnp.where(masks[j % 2][0], part, 0.0))
                 lows.append(jnp.where(masks[j % 2][1], part, 0.0))
-            kept = jnp.concatenate([jnp.concatenate(tops, axis=0), jnp.concatenate(lows, axis=0)], axis=1).astype(BF)
-            acc[...] += lax.dot_general(kept, rows, (((0,), (0,)), ((), ())), preferred_element_type=F32)
-
-        make(0, even_rows)
+            target[...] = jnp.concatenate([jnp.concatenate(tops, axis=0), jnp.concatenate(lows, axis=0)], axis=1).astype(BF)
+
+        def gathered(coefficients, source):
+            acc[...] += lax.dot_general(
+                coefficients[...], source[...], (((0,), (0,)), ((), ())), preferred_element_type=F32
+            )
+
+        make(0, rows0)
 
         def body(i, carry):
-            make(2 * i + 1, odd_rows)
-            use(2 * i, even_rows)
-            make(2 * i + 2, even_rows)
-            use(2 * i + 1, odd_rows)
+            for k in range(4):
+                analysed(4 * i + k, rows[k], kept[k % 2])
+                gathered(kept[(k + 1) % 2], rows[(k + 3) % 4])
+                make(4 * i + k + 1, rows[(k + 1) % 4])
             return carry
 
-        lax.fori_loop(0, pairs_ref[0], body, 0)
+        lax.fori_loop(0, quads_ref[0], body, 0)
+        gathered(kept1, rows3)
         for h in range(2):
             for c in range(half // 128):
                 at = h * half + 128 * c
@@ -322,7 +399,7 @@
     return pl.pallas_call(
         kernel,
         name="legendre",
-        in_specs=[pl.BlockSpec(memory_space=pltpu.SMEM)] + [vmem] * 5,
+        in_specs=[vmem] * 5 + [pl.BlockSpec(memory_space=pltpu.SMEM)],
         out_specs=vmem,
         out_shape=jax.ShapeDtypeStruct((bands, slots, 128), BF),
         scratch_shapes=[
@@ -330,12 +407,16 @@
             pltpu.VMEM((half, 256), BF),
             pltpu.VMEM((height, half), BF),
             pltpu.VMEM((height, half), BF),
+            pltpu.VMEM((height, half), BF),
+            pltpu.VMEM((height, half), BF),
+            pltpu.VMEM((height, 256), BF),
+            pltpu.VMEM((height, 256), BF),
             pltpu.VMEM((256, half), F32),
             pltpu.VMEM((8, half), F32),
             pltpu.VMEM((8, half), F32),
             pltpu.VMEM((8, half), F32),
         ],
-    )(pairs, own, cosines, first_log, second_log, terms)
+    )(own, *tables)
 
 
 def synthesise(back, points, lat_ids, orders, nv, nl, width):
@@ -418,34 +499,6 @@
     )(points, lat_ids, back, orders)
 
 
-def recurrence_terms(mine):
-    first, second = mine[0::2], mine[1::2]
-    ends = jnp.floor((NT + STEPS - first) / STEPS)
-    stops = ends + jnp.floor((NT + STEPS - second) / STEPS)
-    pairs = jnp.floor((jnp.max(stops) + 1.0) / 2.0).astype(jnp.int32).reshape(1)
-    blocks = 4 * (-(-(NT + 1) // (2 * STEPS))) + 2
-    block = jnp.arange(blocks).astype(F32)[:, None]
-    late = block >= ends[None]
-    order = jnp.tile(jnp.where(late, second[None], first[None]), (1, 2))[:, :, None]
-    start = jnp.tile(STEPS * jnp.where(late, block - ends[None], block), (1, 2))[:, :, None]
-    which = jnp.tile(2.0 * jnp.arange(4).astype(F32)[None] + late, (1, 2))[:, :, None]
-    restart = jnp.tile((block == ends[None]).astype(F32), (1, 2))[:, :, None]
-    lane = jnp.arange(128)[None, None, :]
-    step = (lane % STEPS).astype(F32)
-    offset = start + step + 1.0
-    degree = order + offset
-    ahead = jnp.sqrt((4.0 * degree * degree - 1.0) / (offset * (2.0 * order + offset)))
-    below = 4.0 * (degree - 1.0) * (degree - 1.0) - 1.0
-    behind = jnp.sqrt(jnp.maximum((offset - 1.0) * (2.0 * order + offset - 1.0) / below, 0.0))
-    ahead = jnp.where(degree <= NT, ahead, 0.0)
-    row = order + start + step
-    damp = 1.0 / (1.0 + 4.0 * row * (row + 1.0) / (NT * (NT + 1.0)))
-    kind = lane // STEPS
-    last = jnp.where(lane == 96, which, restart)
-    terms = jnp.where(kind == 0, ahead, jnp.where(kind == 1, ahead * behind, jnp.where(kind == 2, damp, last)))
-    return pairs, terms
-
-
 def solution(mesh):
     bands, parts = mesh.shape["band"], mesh.shape["fld"]
 
@@ -465,20 +518,8 @@
             earlier = moved if shift == 1 else earlier + moved
         own, orders = lax.optimization_barrier((mix(own, earlier, bands, nv, nl), orders))
         own = lax.all_to_all(own, "band", split_axis=0, concat_axis=0, tiled=True)
-        half = bands * slots // 2
-        colatitude = (math.pi * (lats + 0.5) / (2.0 * NH)).reshape(2, 1, half)
-        local = lax.dynamic_index_in_dim(orders.reshape(bands, mine), lax.axis_index("band"), 0, False)
-        index = jnp.arange(1, NT + 1).astype(F32)
-        log_norm = 0.5 * math.log(0.5) + 0.5 * jnp.sum(
-            jnp.where(index[None, :] <= local[:, None], jnp.log1p(0.5 / index)[None, :], 0.0), axis=1
-        )
-        log_sine = jnp.log(jnp.sin(colatitude))
-        start_log = log_norm[None, :, None] + local[None, :, None] * log_sine
-        first_log = start_log[:, 0::2].reshape(mine, half)
-        second_log = start_log[:, 1::2].reshape(mine, half)
-        cosines = jnp.broadcast_to(jnp.cos(colatitude), (2, mine // 2, half)).reshape(mine, half)
-        pairs, terms = recurrence_terms(local)
-        back = legendre(pairs, own, cosines, first_log, second_log, terms)
+        band = lax.axis_index("band").astype(jnp.int32).reshape(1)
+        back = legendre(own, plan(band, orders, lats))
         back = lax.all_to_all(back, "band", split_axis=0, concat_axis=0, tiled=True)
         rows = synthesise(back, points, lat_ids, orders, nv, nl, width)
         return from_rows(rows, nv, nl, slots, width)

time: 106 us -> 99.2 us (0.936)
  other arithmetic: 5.91 us -> 2.11 us
  local copies, waits for them, and re-layouts: 6.06 us -> 3.36 us
  waiting for transfers between devices: 14 us -> 16.2 us
  Pallas kernels: 48.6 us -> 47.2 us
    reshape x4 -> x0, local copies, waits for them, and re-layouts: 1.91 us -> none  [the longest x1 0.61 us: on_device(): first_log = start_log[:, 0::2].reshape(mine, half)]
    pallas_call x1 -> x2, Pallas kernels: 22 us -> 20.6 us  [the longest x1 17.8 us: legendre(): pl.pallas_call(kernel, name='legendre', in_specs=[vmem] * 5 + [pl.BlockSp...]
    select_n x1 -> x0, other arithmetic: 1.42 us -> none  [recurrence_terms(): jnp.where(kind == 0, ahead, jnp.where(kind == 1, ahead * behind, jnp.wher...]
    optimization_barrier x1 -> x0, other arithmetic: 1.28 us -> none  [on_device(): lax.optimization_barrier((mix(own, earlier, bands, nv, nl), orders))]
    all_to_all x1, waiting for transfers between devices: 6.23 us -> 7.47 us  [on_device(): own = lax.all_to_all(own, 'band', split_axis=0, concat_axis=0, tiled=True)]
  transfers between devices with their start and end apart: 3 -> 3, of which waited for: 3 -> 3; matrix products, arithmetic and copies ran while one was open for 6% -> 2% of each run, Pallas kernels for 0% -> 3%
where the time goes in v6:
time: 99.2 us; the launch traced here: 98.5 us
  Pallas kernels  47.2 us (48%)
  waiting for transfers between devices  16.2 us (16%)
  blocking collectives  15.3 us (15%)
  starting transfers between devices  14.3 us (14%)
  local copies, waits for them, and re-layouts  3.36 us (3%)
  other arithmetic  2.11 us (2%)
    pallas_call x1, Pallas kernels, legendre(): pl.pallas_call(kernel, name='legendre', in_specs=[vmem] * 5 + [pl.BlockSp...  17.8 us
    all_to_all x1, blocking collectives, on_device(): back = lax.all_to_all(back, 'band', split_axis=0, concat_axis=0, tiled=True)  15.3 us
    pallas_call x1, Pallas kernels, analyse(): pl.pallas_call(kernel, name='analyse', grid=(grid,), in_specs=[smem, smem...  12.9 us
    pallas_call x1, Pallas kernels, synthesise(): pl.pallas_call(kernel, name='synthesise', grid=(grid,), in_specs=[smem, s...  11.4 us
    all_to_all x1, waiting for transfers between devices, on_device(): own = lax.all_to_all(own, 'band', split_axis=0, concat_axis=0, tiled=True)  7.47 us
    all_to_all x1, starting transfers between devices, on_device(): lax.all_to_all(spread, 'band', split_axis=0, concat_axis=0, tiled=True)  7.39 us
    all_to_all x1, waiting for transfers between devices, on_device(): lax.all_to_all(spread, 'band', split_axis=0, concat_axis=0, tiled=True)  5.07 us
    ppermute x1, waiting for transfers between devices, on_device(): lax.ppermute(sums, 'fld', [(k, k + shift) for k in range(parts - shift)])  3.7 us
  transfers between devices with their start and end apart: 3, of which 3 were waited for; matrix products, arithmetic and copies ran while one was open for 2% of the time, Pallas kernels for 3%

profile of v6, /device:TPU:0, one launch (start us, length us, event | category | flops | bytes accessed | tf_op | source)
XLA Modules:
  0.0 98.5 jit_solution(17868860587637341901)
XLA Ops:
  0.0 0.7 pad_add_fusion
  0.7 0.6 broadcast_in_dim.2
  1.4 7.4 %all-to-all-start = ((s32[16,1,88]{2,1,0:T(1,128)}), s32[16,1,88]{2,1,0:T(1,128)S(1)}, u32[]{:S(2)}, u32[]{:S(2)}) async-start(s32[16,1,88]{2,1,0:T(1,128)} %broadcast_in_dim.2), calls=%async_computation | async-start | bytes 16384 | tf_op jit(solution)/shard_map/all_to_all | solution.py:510
  8.7 1.3 %sine_multiply_fusion.weight_ref = f32[80]{0:T(128)} fusion(s32[80]{0:T(128)} %lat_ref.3), kind=kLoop, calls=%fused_computation.3 | loop fusion | flops 320 | bytes 640 | tf_op jit(solution)/shard_map/mul | solution.py:513
  10.0 5.1 %all-to-all-done = s32[16,1,88]{2,1,0:T(1,128)S(1)} async-done(((s32[16,1,88]{2,1,0:T(1,128)}), s32[16,1,88]{2,1,0:T(1,128)S(1)}, u32[]{:S(2)}, u32[]{:S(2)}) %all-to-all-start) | async-done | bytes 5664 | tf_op jit(solution)/shard_map/all_to_all | solution.py:510
  15.1 0.7 convert_element_type.15.given_ref
  15.8 12.9 %analyse.1 = (f32[16,80,128]{2,1,0:T(8,128)}, bf16[8,80,128]{2,1,0:T(8,128)(2,1)}, f32[1,128]{1,0:T(1,128)}) custom-call(s32[1280]{0:T(1024)} %points_ref.3, s32[80]{0:T(128)} %lat_ref.3, f32[80]{0:T(128)} %sine_multiply_fusion.weight_ref, f32[2,2]{1,0:T(2,128)} %coupling_ref.1, bf16[4,6560,128]{2,1,0:T(8,128)(2,1)} %bitcast.12, ...), custom_call_target="tpu_custom_call" | custom-call | tf_op jit(solution)/shard_map/analyse/pallas_call | solution.py:184
  28.7 3.4 %collective-permute-start = (bf16[8,80,128]{2,1,0:T(8,128)(2,1)}, bf16[8,80,128]{2,1,0:T(8,128)(2,1)S(1)}, u32[]{:S(2)}, u32[]{:S(2)}) collective-permute-start(bf16[8,80,128]{2,1,0:T(8,128)(2,1)} %get-tuple-element.16), channel_id=1, source_target_pairs={{0,1},{2,3},{4,5},{6,7},{8,9},{10,11},{12,13},{14,15},{16,17},{18,... | collective-permute-start | bytes 491528 | tf_op jit(solution)/shard_map/ppermute | solution.py:517
  32.1 3.7 %collective-permute-done.earlier_ref = bf16[8,80,128]{2,1,0:T(8,128)(2,1)S(1)} collective-permute-done((bf16[8,80,128]{2,1,0:T(8,128)(2,1)}, bf16[8,80,128]{2,1,0:T(8,128)(2,1)S(1)}, u32[]{:S(2)}, u32[]{:S(2)}) %collective-permute-start) | collective-permute-done | bytes 163872 | tf_op jit(solution)/shard_map/ppermute | solution.py:517
  35.8 0.0 copy-start.1
  35.8 0.7 copy-done.1
  36.5 2.3 %mix.1 = bf16[16,80,128]{2,1,0:T(8,128)(2,1)} custom-call(f32[16,80,128]{2,1,0:T(8,128)} %get-tuple-element.15.own_ref, bf16[8,80,128]{2,1,0:T(8,128)(2,1)} %copy-done.1), custom_call_target="tpu_custom_call" | custom-call | tf_op jit(solution)/shard_map/mix/pallas_call | solution.py:235
  38.8 3.5 %all-to-all-start.1 = ((bf16[16,80,128]{2,1,0:T(8,128)(2,1)}), bf16[16,80,128]{2,1,0:T(8,128)(2,1)S(1)}, u32[]{:S(2)}, u32[]{:S(2)}) async-start(bf16[16,80,128]{2,1,0:T(8,128)(2,1)} %mix.1), calls=%async_computation.1 | async-start | bytes 655360 | tf_op jit(solution)/shard_map/all_to_all | solution.py:520
  42.3 0.1 slice_convert_fusion
  42.4 0.7 convert_element_type.17.lat_ref
  43.1 2.8 %plan.1 = (f32[82,8,128]{2,1,0:T(8,128)}, f32[8,640]{1,0:T(8,128)}, f32[8,640]{1,0:T(8,128)}, f32[8,640]{1,0:T(8,128)}, s32[1]{0:T(128)}) custom-call(s32[1]{0:T(128)} %bitcast.4.band_ref, f32[1,128]{1,0:T(1,128)} %get-tuple-element.19.order_ref, f32[1,1280]{1,0:T(1,128)} %convert_element_type.17.lat_ref), custom_call_target="tpu_custom_call" | custom-call | tf_op jit(solution)/shard_map/plan/pallas_call | solution.py:324
  45.9 7.5 %all-to-all-done.1.own_ref = bf16[16,80,128]{2,1,0:T(8,128)(2,1)S(1)} async-done(((bf16[16,80,128]{2,1,0:T(8,128)(2,1)}), bf16[16,80,128]{2,1,0:T(8,128)(2,1)S(1)}, u32[]{:S(2)}, u32[]{:S(2)}) %all-to-all-start.1) | async-done | bytes 327712 | tf_op jit(solution)/shard_map/all_to_all | solution.py:520
  53.4 0.0 copy-start
  53.4 0.7 copy-done
  54.1 17.8 %legendre.1 = bf16[16,80,128]{2,1,0:T(8,128)(2,1)} custom-call(bf16[16,80,128]{2,1,0:T(8,128)(2,1)} %copy-done, f32[82,8,128]{2,1,0:T(8,128)} %get-tuple-element.20.term_ref, f32[8,640]{1,0:T(8,128)} %get-tuple-element.21.cos_ref, f32[8,640]{1,0:T(8,128)} %get-tuple-element.22.first_ref, f32[8,640]{1,0:T(8,128)} %get-tuple-element.23.second_ref, ...), custom_call_target="tpu_custom_call" | custom-call | tf_op jit(solution)/shard_map/legendre/pallas_call | solution.py:399
  71.9 15.3 %all_to_all.19.back_ref = bf16[16,80,128]{2,1,0:T(8,128)(2,1)} all-to-all(bf16[16,80,128]{2,1,0:T(8,128)(2,1)} %legendre.1), channel_id=1, replica_groups=mesh['band'=16,'fld'=2] {'band'}, dimensions={0} | all-to-all | bytes 655360 | tf_op jit(solution)/shard_map/all_to_all | solution.py:523
  87.2 11.4 %synthesise.1 = bf16[4,6560,128]{2,1,0:T(8,128)(2,1)} custom-call(s32[1280]{0:T(1024)} %points_ref.3, s32[80]{0:T(128)} %lat_ref.3, bf16[16,80,128]{2,1,0:T(8,128)(2,1)} %all_to_all.19.back_ref, f32[1,128]{1,0:T(1,128)} %get-tuple-element.19.order_ref), custom_call_target="tpu_custom_call" | custom-call | tf_op jit(solution)/shard_map/synthesise/pallas_call | solution.py:485
  (1 shorter events, 0.0 us)
Async XLA Ops:
  1.4 13.8 %all-to-all-start = ((s32[16,1,88]{2,1,0:T(1,128)}), s32[16,1,88]{2,1,0:T(1,128)S(1)}, u32[]{:S(2)}, u32[]{:S(2)}) async-start(s32[16,1,88]{2,1,0:T(1,128)} %broadcast_in_dim.2), calls=%async_computation | async-start | bytes 16384 | tf_op jit(solution)/shard_map/all_to_all | solution.py:510
  28.7 7.1 %collective-permute-start = (bf16[8,80,128]{2,1,0:T(8,128)(2,1)}, bf16[8,80,128]{2,1,0:T(8,128)(2,1)S(1)}, u32[]{:S(2)}, u32[]{:S(2)}) collective-permute-start(bf16[8,80,128]{2,1,0:T(8,128)(2,1)} %get-tuple-element.16), channel_id=1, source_target_pairs={{0,1},{2,3},{4,5},{6,7},{8,9},{10,11},{12,13},{14,15},{16,17},{18,... | collective-permute-start | bytes 491528 | tf_op jit(solution)/shard_map/ppermute | solution.py:517
  35.8 0.7 copy-start.1
  38.8 14.6 %all-to-all-start.1 = ((bf16[16,80,128]{2,1,0:T(8,128)(2,1)}), bf16[16,80,128]{2,1,0:T(8,128)(2,1)S(1)}, u32[]{:S(2)}, u32[]{:S(2)}) async-start(bf16[16,80,128]{2,1,0:T(8,128)(2,1)} %mix.1), calls=%async_computation.1 | async-start | bytes 655360 | tf_op jit(solution)/shard_map/all_to_all | solution.py:520
  53.4 0.7 copy-start

commit v7 on v6

--- a/solution.py
+++ b/solution.py
@@ -14,7 +14,8 @@
 F32 = jnp.float32
 GROUP = 8
 STEPS = 32
-CHECK = 8
+CHECK = 16
+FOLD = 8
 RESCALE_LOG = 60.0 * math.log(2.0)
 
 
@@ -235,7 +236,7 @@
     return pl.pallas_call(kernel, name="mix", out_shape=jax.ShapeDtypeStruct((bands, slots, 128), BF))(own, earlier)
 
 
-def make_rows(block, term_ref, cos_ref, second_ref, state, rows_ref, base):
+def make_rows(block, term_ref, cos_ref, second_ref, state, rows_ref):
     now, before, log_now = state
     half = cos_ref.shape[1]
     info = term_ref[block]
@@ -258,11 +259,12 @@
         if j % 2 == 0:
             held = value
         else:
-            at = base + 8 * (j - 1)
-            rows_ref[at : at + 16, :] = jnp.concatenate([held, value], axis=0).astype(BF)
-        a = info[:, j : j + 1]
-        b = info[:, STEPS + j : STEPS + j + 1]
-        current, previous = (a * cosine) * current - b * previous, current
+            rows_ref[8 * (j - 1) : 8 * (j + 1), :] = jnp.concatenate([held, value], axis=0).astype(BF)
+        current, previous = cosine * current - info[:, STEPS + j : STEPS + j + 1] * previous, current
+        if j % FOLD == FOLD - 1:
+            fold = info[:, j : j + 1]
+            current = current * fold
+            previous = previous * fold
     now[...] = current
     before[...] = previous
     log_now[...] = running
@@ -308,12 +310,15 @@
             offset = degree - order
             ahead = jnp.sqrt((4.0 * degree * degree - 1.0) / (offset * (degree + order)))
             below = jnp.maximum(4.0 * row * row - 1.0, 1.0)
-            behind = jnp.sqrt((offset - 1.0) * (row + order) / below)
-            ahead = jnp.where(degree <= NT, ahead, 0.0)
-            damp = 1.0 / (1.0 + 4.0 * row * (row + 1.0) / (NT * (NT + 1.0)))
+            behind = (offset - 1.0) * (row + order) / below
+            for reach in (1, 2, 4):
+                ahead = ahead * jnp.where(lane % FOLD >= reach, pltpu.roll(ahead, reach, 1), 1.0)
+            kappa = jnp.where(lane % FOLD == 0, 1.0, pltpu.roll(ahead, 1, 1))
+            damp = kappa * kappa / (1.0 + 4.0 * row * (row + 1.0) / (NT * (NT + 1.0)))
+            damp = jnp.where(row <= NT, damp, 0.0)
             last = jnp.where(lane == 96, chain + jnp.where(late, 1.0, 0.0), jnp.where(at == ends, 1.0, 0.0))
             rest = jnp.where(kind == 2, damp, last)
-            term_ref[block] = jnp.where(kind == 0, ahead, jnp.where(kind == 1, ahead * behind, rest))
+            term_ref[block] = jnp.where(kind == 0, ahead, jnp.where(kind == 1, behind, rest))
             return carry
 
         lax.fori_loop(0, blocks, fill, 0, unroll=2)
@@ -353,7 +358,7 @@
         state = (now, before, log_now)
 
         def make(block, target):
-            make_rows(block, term_ref, cos_ref, second_ref, state, target, 0)
+            make_rows(block, term_ref, cos_ref, second_ref, state, target)
 
         def analysed(block, source, target):
             found = jnp.dot(source[...], weights[...], preferred_element_type=F32)
@@ -381,9 +386,9 @@
 
         def body(i, carry):
             for k in range(4):
+                make(4 * i + k + 1, rows[(k + 1) % 4])
                 analysed(4 * i + k, rows[k], kept[k % 2])
                 gathered(kept[(k + 1) % 2], rows[(k + 3) % 4])
-                make(4 * i + k + 1, rows[(k + 1) % 4])
             return carry
 
         lax.fori_loop(0, quads_ref[0], body, 0)
@@ -452,6 +457,19 @@
             table = inner_table(cosv, sinv)
             factor = jnp.where(2.0 * order < period_v, double, 0.0)
             hc, hs = cosv[24:32] * factor, sinv[24:32] * factor
+            turns = []
+            for t in range(0, tiles, 2):
+                pair = []
+                for source in (cosv, sinv):
+                    lines = []
+                    for k in (t, t + 1):
+                        u = k - middle if k >= middle else middle - 1 - k
+                        line = source[16 + u : 17 + u]
+                        if source is sinv and k < middle:
+                            line = -line
+                        lines.append(jnp.broadcast_to(line, (8, count)))
+                    pair.append(jnp.concatenate(lines, axis=0).astype(BF))
+                turns.append(pair)
             parts = []
             for f in range(fields):
                 both = []
@@ -461,13 +479,11 @@
                     both.append(even + sign * odd)
                 re, im = both
                 wr, wi = hc * re - hs * im, hs * re + hc * im
-                zr, zi = [None] * tiles, [None] * tiles
-                for u in range(middle):
-                    c, s = cosv[16 + u : 17 + u], sinv[16 + u : 17 + u]
-                    cr, si, ci, sr = c * wr, s * wi, c * wi, s * wr
-                    zr[middle + u], zr[middle - 1 - u] = cr - si, cr + si
-                    zi[middle + u], zi[middle - 1 - u] = ci + sr, ci - sr
-                parts.append(jnp.concatenate([jnp.concatenate(zr, 0).astype(BF), jnp.concatenate(zi, 0).astype(BF)], axis=1))
+                wr = jnp.concatenate([wr, wr], axis=0).astype(BF)
+                wi = jnp.concatenate([wi, wi], axis=0).astype(BF)
+                zr = [c * wr - s * wi for c, s in turns]
+                zi = [s * wr + c * wi for c, s in turns]
+                parts.append(jnp.concatenate([jnp.concatenate(zr, axis=0), jnp.concatenate(zi, axis=0)], axis=1))
             waves = jnp.concatenate(parts, axis=0)
             values = lax.dot_general(waves, table, (((1,), (1,)), ((), ())), preferred_element_type=F32)
             inside = position < period + 64 * off

time: 99.2 us -> 103 us (1.038); the launches traced: 98.5 us -> 103 us
  Pallas kernels: 47.2 us -> 57.7 us
  waiting for transfers between devices: 16.2 us -> 8.77 us
  blocking collectives: 15.3 us -> 17.1 us
    pallas_call x1, Pallas kernels: 2.79 us -> 14.1 us  [plan(): pl.pallas_call(kernel, name='plan', in_specs=[smem, vmem, vmem], out_spec...]
    all_to_all x1, waiting for transfers between devices: 7.47 us -> 0.01 us  [on_device(): own = lax.all_to_all(own, 'band', split_axis=0, concat_axis=0, tiled=True)]
    all_to_all x1, blocking collectives: 15.3 us -> 17.1 us  [on_device(): back = lax.all_to_all(back, 'band', split_axis=0, concat_axis=0, tiled=True)]
  transfers between devices with their start and end apart: 3 -> 3, of which waited for: 3 -> 2; matrix products, arithmetic and copies ran while one was open for 2% -> 2% of each run, Pallas kernels for 3% -> 14%
where the time goes in v7:
time: 103 us
  Pallas kernels  57.7 us (56%)
  blocking collectives  17.1 us (17%)
  starting transfers between devices  14.3 us (14%)
  waiting for transfers between devices  8.77 us (9%)
  local copies, waits for them, and re-layouts  3.35 us (3%)
  other arithmetic  2.11 us (2%)
    pallas_call x1, Pallas kernels, legendre(): pl.pallas_call(kernel, name='legendre', in_specs=[vmem] * 5 + [pl.BlockSp...  17.4 us
    all_to_all x1, blocking collectives, on_device(): back = lax.all_to_all(back, 'band', split_axis=0, concat_axis=0, tiled=True)  17.1 us
    pallas_call x1, Pallas kernels, plan(): pl.pallas_call(kernel, name='plan', in_specs=[smem, vmem, vmem], out_spec...  14.1 us
    pallas_call x1, Pallas kernels, analyse(): pl.pallas_call(kernel, name='analyse', grid=(grid,), in_specs=[smem, smem...  12.9 us
    pallas_call x1, Pallas kernels, synthesise(): pl.pallas_call(kernel, name='synthesise', grid=(grid,), in_specs=[smem, s...  10.9 us
    all_to_all x1, starting transfers between devices, on_device(): lax.all_to_all(spread, 'band', split_axis=0, concat_axis=0, tiled=True)  7.39 us
    all_to_all x1, waiting for transfers between devices, on_device(): lax.all_to_all(spread, 'band', split_axis=0, concat_axis=0, tiled=True)  5.07 us
    ppermute x1, waiting for transfers between devices, on_device(): lax.ppermute(sums, 'fld', [(k, k + shift) for k in range(parts - shift)])  3.7 us
  transfers between devices with their start and end apart: 3, of which 2 were waited for; matrix products, arithmetic and copies ran while one was open for 2% of the time, Pallas kernels for 14%

profile of v7, /device:TPU:0, one launch (start us, length us, event | category | flops | bytes accessed | tf_op | source)
XLA Modules:
  0.0 103.4 jit_solution(3245779653784582467)
XLA Ops:
  0.0 0.7 pad_add_fusion
  0.7 0.6 broadcast_in_dim.2
  1.4 7.4 %all-to-all-start = ((s32[16,1,88]{2,1,0:T(1,128)}), s32[16,1,88]{2,1,0:T(1,128)S(1)}, u32[]{:S(2)}, u32[]{:S(2)}) async-start(s32[16,1,88]{2,1,0:T(1,128)} %broadcast_in_dim.2), calls=%async_computation | async-start | bytes 16384 | tf_op jit(solution)/shard_map/all_to_all | solution.py:526
  8.7 1.3 %sine_multiply_fusion.weight_ref = f32[80]{0:T(128)} fusion(s32[80]{0:T(128)} %lat_ref.3), kind=kLoop, calls=%fused_computation.3 | loop fusion | flops 320 | bytes 640 | tf_op jit(solution)/shard_map/mul | solution.py:529
  10.0 5.1 %all-to-all-done = s32[16,1,88]{2,1,0:T(1,128)S(1)} async-done(((s32[16,1,88]{2,1,0:T(1,128)}), s32[16,1,88]{2,1,0:T(1,128)S(1)}, u32[]{:S(2)}, u32[]{:S(2)}) %all-to-all-start) | async-done | bytes 5664 | tf_op jit(solution)/shard_map/all_to_all | solution.py:526
  15.1 0.7 convert_element_type.15.given_ref
  15.8 12.9 %analyse.1 = (f32[16,80,128]{2,1,0:T(8,128)}, bf16[8,80,128]{2,1,0:T(8,128)(2,1)}, f32[1,128]{1,0:T(1,128)}) custom-call(s32[1280]{0:T(1024)} %points_ref.3, s32[80]{0:T(128)} %lat_ref.3, f32[80]{0:T(128)} %sine_multiply_fusion.weight_ref, f32[2,2]{1,0:T(2,128)} %coupling_ref.1, bf16[4,6560,128]{2,1,0:T(8,128)(2,1)} %bitcast.12, ...), custom_call_target="tpu_custom_call" | custom-call | tf_op jit(solution)/shard_map/analyse/pallas_call | solution.py:185
  28.7 3.4 %collective-permute-start = (bf16[8,80,128]{2,1,0:T(8,128)(2,1)}, bf16[8,80,128]{2,1,0:T(8,128)(2,1)S(1)}, u32[]{:S(2)}, u32[]{:S(2)}) collective-permute-start(bf16[8,80,128]{2,1,0:T(8,128)(2,1)} %get-tuple-element.16), channel_id=1, source_target_pairs={{0,1},{2,3},{4,5},{6,7},{8,9},{10,11},{12,13},{14,15},{16,17},{18,... | collective-permute-start | bytes 491528 | tf_op jit(solution)/shard_map/ppermute | solution.py:533
  32.1 3.7 %collective-permute-done.earlier_ref = bf16[8,80,128]{2,1,0:T(8,128)(2,1)S(1)} collective-permute-done((bf16[8,80,128]{2,1,0:T(8,128)(2,1)}, bf16[8,80,128]{2,1,0:T(8,128)(2,1)S(1)}, u32[]{:S(2)}, u32[]{:S(2)}) %collective-permute-start) | collective-permute-done | bytes 163872 | tf_op jit(solution)/shard_map/ppermute | solution.py:533
  35.8 0.0 copy-start.1
  35.8 0.7 copy-done.1
  36.5 2.3 %mix.1 = bf16[16,80,128]{2,1,0:T(8,128)(2,1)} custom-call(f32[16,80,128]{2,1,0:T(8,128)} %get-tuple-element.15.own_ref, bf16[8,80,128]{2,1,0:T(8,128)(2,1)} %copy-done.1), custom_call_target="tpu_custom_call" | custom-call | tf_op jit(solution)/shard_map/mix/pallas_call | solution.py:236
  38.8 3.5 %all-to-all-start.1 = ((bf16[16,80,128]{2,1,0:T(8,128)(2,1)}), bf16[16,80,128]{2,1,0:T(8,128)(2,1)S(1)}, u32[]{:S(2)}, u32[]{:S(2)}) async-start(bf16[16,80,128]{2,1,0:T(8,128)(2,1)} %mix.1), calls=%async_computation.1 | async-start | bytes 655360 | tf_op jit(solution)/shard_map/all_to_all | solution.py:536
  42.3 0.1 slice_convert_fusion
  42.4 0.7 convert_element_type.17.lat_ref
  43.1 14.1 %plan.1 = (f32[82,8,128]{2,1,0:T(8,128)}, f32[8,640]{1,0:T(8,128)}, f32[8,640]{1,0:T(8,128)}, f32[8,640]{1,0:T(8,128)}, s32[1]{0:T(128)}) custom-call(s32[1]{0:T(128)} %bitcast.4.band_ref, f32[1,128]{1,0:T(1,128)} %get-tuple-element.19.order_ref, f32[1,1280]{1,0:T(1,128)} %convert_element_type.17.lat_ref), custom_call_target="tpu_custom_call" | custom-call | tf_op jit(solution)/shard_map/plan/pallas_call | solution.py:329
  57.2 0.0 all-to-all-done.1.own_ref
  57.3 0.0 copy-start
  57.3 0.7 copy-done
  58.0 17.4 %legendre.1 = bf16[16,80,128]{2,1,0:T(8,128)(2,1)} custom-call(bf16[16,80,128]{2,1,0:T(8,128)(2,1)} %copy-done, f32[82,8,128]{2,1,0:T(8,128)} %get-tuple-element.20.term_ref, f32[8,640]{1,0:T(8,128)} %get-tuple-element.21.cos_ref, f32[8,640]{1,0:T(8,128)} %get-tuple-element.22.first_ref, f32[8,640]{1,0:T(8,128)} %get-tuple-element.23.second_ref, ...), custom_call_target="tpu_custom_call" | custom-call | tf_op jit(solution)/shard_map/legendre/pallas_call | solution.py:404
  75.4 17.1 %all_to_all.19.back_ref = bf16[16,80,128]{2,1,0:T(8,128)(2,1)} all-to-all(bf16[16,80,128]{2,1,0:T(8,128)(2,1)} %legendre.1), channel_id=1, replica_groups=mesh['band'=16,'fld'=2] {'band'}, dimensions={0} | all-to-all | bytes 655360 | tf_op jit(solution)/shard_map/all_to_all | solution.py:539
  92.6 10.9 %synthesise.1 = bf16[4,6560,128]{2,1,0:T(8,128)(2,1)} custom-call(s32[1280]{0:T(1024)} %points_ref.3, s32[80]{0:T(128)} %lat_ref.3, bf16[16,80,128]{2,1,0:T(8,128)(2,1)} %all_to_all.19.back_ref, f32[1,128]{1,0:T(1,128)} %get-tuple-element.19.order_ref), custom_call_target="tpu_custom_call" | custom-call | tf_op jit(solution)/shard_map/synthesise/pallas_call | solution.py:501
  (1 shorter events, 0.0 us)
Async XLA Ops:
  1.4 13.8 %all-to-all-start = ((s32[16,1,88]{2,1,0:T(1,128)}), s32[16,1,88]{2,1,0:T(1,128)S(1)}, u32[]{:S(2)}, u32[]{:S(2)}) async-start(s32[16,1,88]{2,1,0:T(1,128)} %broadcast_in_dim.2), calls=%async_computation | async-start | bytes 16384 | tf_op jit(solution)/shard_map/all_to_all | solution.py:526
  28.7 7.1 %collective-permute-start = (bf16[8,80,128]{2,1,0:T(8,128)(2,1)}, bf16[8,80,128]{2,1,0:T(8,128)(2,1)S(1)}, u32[]{:S(2)}, u32[]{:S(2)}) collective-permute-start(bf16[8,80,128]{2,1,0:T(8,128)(2,1)} %get-tuple-element.16), channel_id=1, source_target_pairs={{0,1},{2,3},{4,5},{6,7},{8,9},{10,11},{12,13},{14,15},{16,17},{18,... | collective-permute-start | bytes 491528 | tf_op jit(solution)/shard_map/ppermute | solution.py:533
  35.8 0.7 copy-start.1
  38.8 18.5 %all-to-all-start.1 = ((bf16[16,80,128]{2,1,0:T(8,128)(2,1)}), bf16[16,80,128]{2,1,0:T(8,128)(2,1)S(1)}, u32[]{:S(2)}, u32[]{:S(2)}) async-start(bf16[16,80,128]{2,1,0:T(8,128)(2,1)} %mix.1), calls=%async_computation.1 | async-start | bytes 655360 | tf_op jit(solution)/shard_map/all_to_all | solution.py:536
  57.3 0.7 copy-start

commit v8 on v7

--- a/solution.py
+++ b/solution.py
@@ -17,6 +17,10 @@
 CHECK = 16
 FOLD = 8
 RESCALE_LOG = 60.0 * math.log(2.0)
+
+
+def resident(*arrays):
+    return [pltpu.with_memory_space_constraint(a, pltpu.VMEM) for a in arrays]
 
 
 def iota(shape, dim):
@@ -115,8 +119,8 @@
     span = window_rows(width)
     tiles = span // 8
     middle = tiles // 2
-    count = orders.shape[1]
-    bands = count // 8
+    bands = orders.shape[0]
+    count = 8 * bands
     grid = slots // GROUP
 
     def kernel(points_ref, lat_ref, weight_ref, coupling_ref, x_ref, given_ref, own_ref, sum_ref, order_ref, planes):
@@ -192,7 +196,7 @@
             smem,
             smem,
             pl.BlockSpec((fields, GROUP * rows, 128), lambda i: (0, i, 0)),
-            pl.BlockSpec((1, count), lambda i: (0, 0)),
+            pl.BlockSpec((bands, 8), lambda i: (0, 0)),
         ],
         out_specs=[
             pl.BlockSpec((16, slots, count), lambda i: (0, 0, 0)),
@@ -209,8 +213,13 @@
     )(points, lat_ids, weights, coupling, points_rows, orders)
 
 
-def deal(row, bands):
-    count = row.shape[1]
+def deal(given, bands):
+    count = bands * 8
+    line, lane = iota((bands, count), 0), iota((bands, count), 1)
+    spots = jnp.zeros((bands, count), F32)
+    for e in range(8):
+        spots = jnp.where(lane == 8 * line + e, given[:, e : e + 1], spots)
+    row = jnp.sum(spots, axis=0, keepdims=True)
     line, lane = iota((count, count), 0), iota((count, count), 1)
     column = jnp.sum(jnp.where(line == lane, row, 0.0), axis=1, keepdims=True)
     rank = jnp.sum(jnp.where(row < column, 1.0, 0.0), axis=1, keepdims=True).astype(jnp.int32)
@@ -233,7 +242,7 @@
             for d, w in enumerate(block_transpose(value)):
                 out_ref[16 * tile + d] = w.astype(BF)
 
-    return pl.pallas_call(kernel, name="mix", out_shape=jax.ShapeDtypeStruct((bands, slots, 128), BF))(own, earlier)
+    return pl.pallas_call(kernel, name="mix", out_shape=jax.ShapeDtypeStruct((bands, slots, 128), BF))(*resident(own, earlier))
 
 
 def make_rows(block, term_ref, cos_ref, second_ref, state, rows_ref):
@@ -274,7 +283,7 @@
     total = lats.shape[1]
     half = total // 2
     count = orders.shape[1]
-    blocks = 4 * (-(-2 * (NT + 1) // (4 * STEPS))) + 2
+    blocks = 8 * (-(-(4 * (-(-2 * (NT + 1) // (4 * STEPS))) + 2) // 8))
 
     def kernel(band_ref, order_ref, lat_ref, term_ref, cos_ref, first_ref, second_ref, quads_ref):
         line, lane = iota((8, count), 0), iota((8, count), 1)
@@ -301,7 +310,7 @@
         tick = (lane % STEPS).astype(F32)
         chain = 2.0 * (iota((8, 128), 0) % 4).astype(F32)
 
-        def fill(block, carry):
+        def fill(block):
             at = jnp.full((8, 128), block, jnp.int32).astype(F32)
             late = at >= ends
             order = jnp.where(late, second, first)
@@ -319,9 +328,13 @@
             last = jnp.where(lane == 96, chain + jnp.where(late, 1.0, 0.0), jnp.where(at == ends, 1.0, 0.0))
             rest = jnp.where(kind == 2, damp, last)
             term_ref[block] = jnp.where(kind == 0, ahead, jnp.where(kind == 1, behind, rest))
+
+        def several(i, carry):
+            for k in range(8):
+                fill(8 * i + k)
             return carry
 
-        lax.fori_loop(0, blocks, fill, 0, unroll=2)
+        lax.fori_loop(0, blocks // 8, several, 0)
 
     smem = pl.BlockSpec(memory_space=pltpu.SMEM)
     vmem = pl.BlockSpec(memory_space=pltpu.VMEM)
@@ -421,7 +434,7 @@
             pltpu.VMEM((8, half), F32),
             pltpu.VMEM((8, half), F32),
         ],
-    )(own, *tables)
+    )(*resident(own, *tables[:4]), tables[4])
 
 
 def synthesise(back, points, lat_ids, orders, nv, nl, width):
@@ -521,10 +534,11 @@
     def on_device(grid_field, coupling, points, lat_ids, wn_ids):
         nv, nl, slots, _, width = grid_field.shape
         mine = wn_ids.shape[0]
-        packed = jnp.concatenate([wn_ids, lat_ids])
-        spread = jnp.broadcast_to(packed[None], (bands, mine + slots))
+        spread = jnp.concatenate(
+            [jnp.broadcast_to(wn_ids[None], (bands, mine)), jnp.broadcast_to(lat_ids[None], (bands, slots))], axis=1
+        )
         known = lax.all_to_all(spread, "band", split_axis=0, concat_axis=0, tiled=True)
-        orders = known[:, :mine].reshape(1, bands * mine).astype(F32)
+        orders = known[:, :mine].astype(F32)
         lats = known[:, mine:].reshape(1, bands * slots).astype(F32)
         weights = math.pi / (2.0 * NH) * jnp.sin(math.pi * (lat_ids.astype(F32) + 0.5) / (2.0 * NH))
         own, sums, orders = analyse(as_rows(grid_field), points, lat_ids, weights, orders, coupling, nv, nl, width)

time: 103 us -> 99.3 us (0.964); the launches traced: 103 us -> 98.4 us
  Pallas kernels: 57.7 us -> 46.6 us
  waiting for transfers between devices: 8.77 us -> 14 us
  local copies, waits for them, and re-layouts: 3.35 us -> 5.52 us
  blocking collectives: 17.1 us -> 15.3 us
    pallas_call x1, Pallas kernels: 14.1 us -> 5.14 us  [plan(): pl.pallas_call(kernel, name='plan', in_specs=[smem, vmem, vmem], out_spec...]
    all_to_all x1, waiting for transfers between devices: 0.01 us -> 5.14 us  [on_device(): own = lax.all_to_all(own, 'band', split_axis=0, concat_axis=0, tiled=True)]
    unnamed x4 -> x10, local copies, waits for them, and re-layouts: 1.39 us -> 4.25 us
    all_to_all x1, blocking collectives: 17.1 us -> 15.3 us  [on_device(): back = lax.all_to_all(back, 'band', split_axis=0, concat_axis=0, tiled=True)]
    pallas_call x1, Pallas kernels: 2.28 us -> 1.17 us  [mix(): pl.pallas_call(kernel, name='mix', out_shape=jax.ShapeDtypeStruct((bands,...]
  transfers between devices with their start and end apart: 3 -> 3, of which waited for: 2 -> 3; matrix products, arithmetic and copies ran while one was open for 2% -> 2% of each run, Pallas kernels for 14% -> 5%
where the time goes in v8:
time: 99.3 us; the launch traced here: 98.4 us
  Pallas kernels  46.6 us (47%)
  blocking collectives  15.3 us (15%)
  starting transfers between devices  14.3 us (14%)
  waiting for transfers between devices  14 us (14%)
  local copies, waits for them, and re-layouts  5.52 us (6%)
  other arithmetic  2.66 us (3%)
    pallas_call x1, Pallas kernels, legendre(): pl.pallas_call(kernel, name='legendre', in_specs=[vmem] * 5 + [pl.BlockSp...  16.4 us
    all_to_all x1, blocking collectives, on_device(): back = lax.all_to_all(back, 'band', split_axis=0, concat_axis=0, tiled=True)  15.3 us
    pallas_call x1, Pallas kernels, analyse(): pl.pallas_call(kernel, name='analyse', grid=(grid,), in_specs=[smem, smem...  13 us
    pallas_call x1, Pallas kernels, synthesise(): pl.pallas_call(kernel, name='synthesise', grid=(grid,), in_specs=[smem, s...  10.8 us
    all_to_all x1, starting transfers between devices, on_device(): lax.all_to_all(spread, 'band', split_axis=0, concat_axis=0, tiled=True)  7.39 us
    pallas_call x1, Pallas kernels, plan(): pl.pallas_call(kernel, name='plan', in_specs=[smem, vmem, vmem], out_spec...  5.14 us
    all_to_all x1, waiting for transfers between devices, on_device(): own = lax.all_to_all(own, 'band', split_axis=0, concat_axis=0, tiled=True)  5.14 us
    all_to_all x1, waiting for transfers between devices, on_device(): lax.all_to_all(spread, 'band', split_axis=0, concat_axis=0, tiled=True)  5.11 us
  transfers between devices with their start and end apart: 3, of which 3 were waited for; matrix products, arithmetic and copies ran while one was open for 2% of the time, Pallas kernels for 5%

profile of v8, /device:TPU:0, one launch (start us, length us, event | category | flops | bytes accessed | tf_op | source)
XLA Modules:
  0.0 98.4 jit_solution(15397845573236120452)
XLA Ops:
  0.0 0.7 pad_add_fusion
  0.7 0.6 broadcast.6
  1.3 7.4 %all-to-all-start = ((s32[16,1,88]{2,1,0:T(1,128)}), s32[16,1,88]{2,1,0:T(1,128)S(1)}, u32[]{:S(2)}, u32[]{:S(2)}) async-start(s32[16,1,88]{2,1,0:T(1,128)} %bitcast.3), calls=%async_computation | async-start | bytes 16384 | tf_op jit(solution)/shard_map/all_to_all | solution.py:540
  8.7 1.2 %sine_multiply_fusion.weight_ref = f32[80]{0:T(128)} fusion(s32[80]{0:T(128)} %lat_ref.3), kind=kLoop, calls=%fused_computation.3 | loop fusion | flops 320 | bytes 640 | tf_op jit(solution)/shard_map/mul | solution.py:543
  10.0 5.1 %all-to-all-done = s32[16,1,88]{2,1,0:T(1,128)S(1)} async-done(((s32[16,1,88]{2,1,0:T(1,128)}), s32[16,1,88]{2,1,0:T(1,128)S(1)}, u32[]{:S(2)}, u32[]{:S(2)}) %all-to-all-start) | async-done | bytes 5664 | tf_op jit(solution)/shard_map/all_to_all | solution.py:540
  15.1 0.6 slice_convert_fusion.1.given_ref
  15.7 13.0 %analyse.1 = (f32[16,80,128]{2,1,0:T(8,128)}, bf16[8,80,128]{2,1,0:T(8,128)(2,1)}, f32[1,128]{1,0:T(1,128)}) custom-call(s32[1280]{0:T(1024)} %points_ref.3, s32[80]{0:T(128)} %lat_ref.3, f32[80]{0:T(128)} %sine_multiply_fusion.weight_ref, f32[2,2]{1,0:T(2,128)} %coupling_ref.1, bf16[4,6560,128]{2,1,0:T(8,128)(2,1)} %bitcast.13, ...), custom_call_target="tpu_custom_call" | custom-call | tf_op jit(solution)/shard_map/analyse/pallas_call | solution.py:189
  28.7 3.4 %collective-permute-start = (bf16[8,80,128]{2,1,0:T(8,128)(2,1)}, bf16[8,80,128]{2,1,0:T(8,128)(2,1)S(1)}, u32[]{:S(2)}, u32[]{:S(2)}) collective-permute-start(bf16[8,80,128]{2,1,0:T(8,128)(2,1)} %get-tuple-element.16), channel_id=1, source_target_pairs={{0,1},{2,3},{4,5},{6,7},{8,9},{10,11},{12,13},{14,15},{16,17},{18,... | collective-permute-start | bytes 491528 | tf_op jit(solution)/shard_map/ppermute | solution.py:547
  32.1 3.7 %collective-permute-done.earlier_ref = bf16[8,80,128]{2,1,0:T(8,128)(2,1)S(1)} collective-permute-done((bf16[8,80,128]{2,1,0:T(8,128)(2,1)}, bf16[8,80,128]{2,1,0:T(8,128)(2,1)S(1)}, u32[]{:S(2)}, u32[]{:S(2)}) %collective-permute-start) | collective-permute-done | bytes 163872 | tf_op jit(solution)/shard_map/ppermute | solution.py:547
  35.8 0.0 copy-start
  35.8 1.1 %copy-done = f32[16,80,128]{2,1,0:T(8,128)S(1)} copy-done((f32[16,80,128]{2,1,0:T(8,128)S(1)}, f32[16,80,128]{2,1,0:T(8,128)}, u32[]{:S(2)}) %copy-start) | copy-done | bytes 655384
  36.9 1.2 %mix.1 = bf16[16,80,128]{2,1,0:T(8,128)(2,1)} custom-call(f32[16,80,128]{2,1,0:T(8,128)S(1)} %copy-done, bf16[8,80,128]{2,1,0:T(8,128)(2,1)S(1)} %collective-permute-done.earlier_ref), custom_call_target="tpu_custom_call" | custom-call | tf_op jit(solution)/shard_map/mix/pallas_call | solution.py:245
  38.1 3.5 %all-to-all-start.1 = ((bf16[16,80,128]{2,1,0:T(8,128)(2,1)}), bf16[16,80,128]{2,1,0:T(8,128)(2,1)S(1)}, u32[]{:S(2)}, u32[]{:S(2)}) async-start(bf16[16,80,128]{2,1,0:T(8,128)(2,1)} %mix.1), calls=%async_computation.1 | async-start | bytes 655360 | tf_op jit(solution)/shard_map/all_to_all | solution.py:550
  41.7 0.1 slice_convert_fusion
  41.7 0.7 convert_element_type.14.lat_ref
  42.4 5.1 %plan.1 = (f32[88,8,128]{2,1,0:T(8,128)}, f32[8,640]{1,0:T(8,128)}, f32[8,640]{1,0:T(8,128)}, f32[8,640]{1,0:T(8,128)}, s32[1]{0:T(128)}) custom-call(s32[1]{0:T(128)} %bitcast.5.band_ref, f32[1,128]{1,0:T(1,128)} %get-tuple-element.19.order_ref, f32[1,1280]{1,0:T(1,128)} %convert_element_type.14.lat_ref), custom_call_target="tpu_custom_call" | custom-call | tf_op jit(solution)/shard_map/plan/pallas_call | solution.py:342
  47.5 5.1 %all-to-all-done.1.own_ref = bf16[16,80,128]{2,1,0:T(8,128)(2,1)S(1)} async-done(((bf16[16,80,128]{2,1,0:T(8,128)(2,1)}), bf16[16,80,128]{2,1,0:T(8,128)(2,1)S(1)}, u32[]{:S(2)}, u32[]{:S(2)}) %all-to-all-start.1) | async-done | bytes 327712 | tf_op jit(solution)/shard_map/all_to_all | solution.py:550
  52.7 0.0 copy-start.1
  52.7 1.0 copy-done.1
  53.7 0.0 copy-start.2
  53.7 0.7 copy-done.2
  54.4 0.0 copy-start.3
  54.4 0.7 copy-done.3
  55.1 0.0 copy-start.4
  55.1 0.7 copy-done.4
  55.9 16.4 %legendre.1 = bf16[16,80,128]{2,1,0:T(8,128)(2,1)} custom-call(bf16[16,80,128]{2,1,0:T(8,128)(2,1)S(1)} %all-to-all-done.1.own_ref, f32[88,8,128]{2,1,0:T(8,128)S(1)} %copy-done.1, f32[8,640]{1,0:T(8,128)S(1)} %copy-done.2, f32[8,640]{1,0:T(8,128)S(1)} %copy-done.3, f32[8,640]{1,0:T(8,128)S(1)} %copy-done.4, s32[1]{0:T(128)} %get-tuple-element.24.quads_ref), custom_call_target="tpu_custom_call" | custom-call | tf_op jit(solution)/shard_map/legendre/pallas_call | solution.py:417
  72.3 15.3 %all_to_all.22.back_ref = bf16[16,80,128]{2,1,0:T(8,128)(2,1)} all-to-all(bf16[16,80,128]{2,1,0:T(8,128)(2,1)} %legendre.1), channel_id=1, replica_groups=mesh['band'=16,'fld'=2] {'band'}, dimensions={0} | all-to-all | bytes 655360 | tf_op jit(solution)/shard_map/all_to_all | solution.py:553
  87.6 10.8 %synthesise.1 = bf16[4,6560,128]{2,1,0:T(8,128)(2,1)} custom-call(s32[1280]{0:T(1024)} %points_ref.3, s32[80]{0:T(128)} %lat_ref.3, bf16[16,80,128]{2,1,0:T(8,128)(2,1)} %all_to_all.22.back_ref, f32[1,128]{1,0:T(1,128)} %get-tuple-element.19.order_ref), custom_call_target="tpu_custom_call" | custom-call | tf_op jit(solution)/shard_map/synthesise/pallas_call | solution.py:514
Async XLA Ops:
  1.3 13.8 %all-to-all-start = ((s32[16,1,88]{2,1,0:T(1,128)}), s32[16,1,88]{2,1,0:T(1,128)S(1)}, u32[]{:S(2)}, u32[]{:S(2)}) async-start(s32[16,1,88]{2,1,0:T(1,128)} %bitcast.3), calls=%async_computation | async-start | bytes 16384 | tf_op jit(solution)/shard_map/all_to_all | solution.py:540
  28.7 7.1 %collective-permute-start = (bf16[8,80,128]{2,1,0:T(8,128)(2,1)}, bf16[8,80,128]{2,1,0:T(8,128)(2,1)S(1)}, u32[]{:S(2)}, u32[]{:S(2)}) collective-permute-start(bf16[8,80,128]{2,1,0:T(8,128)(2,1)} %get-tuple-element.16), channel_id=1, source_target_pairs={{0,1},{2,3},{4,5},{6,7},{8,9},{10,11},{12,13},{14,15},{16,17},{18,... | collective-permute-start | bytes 491528 | tf_op jit(solution)/shard_map/ppermute | solution.py:547
  35.8 1.1 %copy-start = (f32[16,80,128]{2,1,0:T(8,128)S(1)}, f32[16,80,128]{2,1,0:T(8,128)}, u32[]{:S(2)}) copy-start(f32[16,80,128]{2,1,0:T(8,128)} %get-tuple-element.15.own_ref) | copy-start | bytes 1966084
  38.1 14.6 %all-to-all-start.1 = ((bf16[16,80,128]{2,1,0:T(8,128)(2,1)}), bf16[16,80,128]{2,1,0:T(8,128)(2,1)S(1)}, u32[]{:S(2)}, u32[]{:S(2)}) async-start(bf16[16,80,128]{2,1,0:T(8,128)(2,1)} %mix.1), calls=%async_computation.1 | async-start | bytes 655360 | tf_op jit(solution)/shard_map/all_to_all | solution.py:550
  52.7 1.0 %copy-start.1 = (f32[88,8,128]{2,1,0:T(8,128)S(1)}, f32[88,8,128]{2,1,0:T(8,128)}, u32[]{:S(2)}) copy-start(f32[88,8,128]{2,1,0:T(8,128)} %get-tuple-element.20.term_ref) | copy-start | bytes 1081348
  53.7 0.7 copy-start.2
  54.4 0.7 copy-start.3
  55.1 0.7 copy-start.4

commit v9 on v8

--- a/solution.py
+++ b/solution.py
@@ -199,12 +199,12 @@
             pl.BlockSpec((bands, 8), lambda i: (0, 0)),
         ],
         out_specs=[
-            pl.BlockSpec((16, slots, count), lambda i: (0, 0, 0)),
+            pl.BlockSpec(memory_space=pltpu.VMEM),
             pl.BlockSpec((16 // nl, slots, count), lambda i: (0, 0, 0)),
             pl.BlockSpec((1, count), lambda i: (0, 0)),
         ],
         out_shape=[
-            jax.ShapeDtypeStruct((16, slots, count), F32),
+            pltpu.VMEM((16, slots, count), F32),
             jax.ShapeDtypeStruct((16 // nl, slots, count), BF),
             jax.ShapeDtypeStruct((1, count), F32),
         ],
@@ -338,13 +338,13 @@
 
     smem = pl.BlockSpec(memory_space=pltpu.SMEM)
     vmem = pl.BlockSpec(memory_space=pltpu.VMEM)
-    wide = jax.ShapeDtypeStruct((8, half), F32)
+    wide = pltpu.VMEM((8, half), F32)
     return pl.pallas_call(
         kernel,
         name="plan",
         in_specs=[smem, vmem, vmem],
         out_specs=[vmem] * 4 + [smem],
-        out_shape=[jax.ShapeDtypeStruct((blocks, 8, 128), F32), wide, wide, wide, jax.ShapeDtypeStruct((1,), jnp.int32)],
+        out_shape=[pltpu.VMEM((blocks, 8, 128), F32), wide, wide, wide, jax.ShapeDtypeStruct((1,), jnp.int32)],
     )(band, orders, lats)
 
 

time: 99.3 us -> 94.6 us (0.953)
  local copies, waits for them, and re-layouts: 5.52 us -> 1.29 us
    unnamed x10 -> x0, local copies, waits for them, and re-layouts: 4.25 us -> none
where the time goes in v9:
time: 94.6 us; the launch traced here: 94 us
  Pallas kernels  45.9 us (49%)
  blocking collectives  15.3 us (16%)
  waiting for transfers between devices  14.5 us (15%)
  starting transfers between devices  14.3 us (15%)
  other arithmetic  2.63 us (3%)
  local copies, waits for them, and re-layouts  1.29 us (1%)
    pallas_call x1, Pallas kernels, legendre(): pl.pallas_call(kernel, name='legendre', in_specs=[vmem] * 5 + [pl.BlockSp...  16.5 us
    all_to_all x1, blocking collectives, on_device(): back = lax.all_to_all(back, 'band', split_axis=0, concat_axis=0, tiled=True)  15.3 us
    pallas_call x1, Pallas kernels, analyse(): pl.pallas_call(kernel, name='analyse', grid=(grid,), in_specs=[smem, smem...  12.8 us
    pallas_call x1, Pallas kernels, synthesise(): pl.pallas_call(kernel, name='synthesise', grid=(grid,), in_specs=[smem, s...  10.9 us
    all_to_all x1, starting transfers between devices, on_device(): lax.all_to_all(spread, 'band', split_axis=0, concat_axis=0, tiled=True)  7.39 us
    all_to_all x1, waiting for transfers between devices, on_device(): own = lax.all_to_all(own, 'band', split_axis=0, concat_axis=0, tiled=True)  5.66 us
    all_to_all x1, waiting for transfers between devices, on_device(): lax.all_to_all(spread, 'band', split_axis=0, concat_axis=0, tiled=True)  5.15 us
    pallas_call x1, Pallas kernels, plan(): pl.pallas_call(kernel, name='plan', in_specs=[smem, vmem, vmem], out_spec...  4.59 us
  transfers between devices with their start and end apart: 3, of which 3 were waited for; matrix products, arithmetic and copies ran while one was open for 2% of the time, Pallas kernels for 5%

profile of v9, /device:TPU:0, one launch (start us, length us, event | category | flops | bytes accessed | tf_op | source)
XLA Modules:
  0.0 94.0 jit_solution(14195810580893852224)
XLA Ops:
  0.0 0.7 pad_add_fusion
  0.7 0.6 broadcast.6
  1.3 7.4 %all-to-all-start = ((s32[16,1,88]{2,1,0:T(1,128)}), s32[16,1,88]{2,1,0:T(1,128)S(1)}, u32[]{:S(2)}, u32[]{:S(2)}) async-start(s32[16,1,88]{2,1,0:T(1,128)} %bitcast.3), calls=%async_computation | async-start | bytes 16384 | tf_op jit(solution)/shard_map/all_to_all | solution.py:540
  8.7 1.2 %sine_multiply_fusion.weight_ref = f32[80]{0:T(128)} fusion(s32[80]{0:T(128)} %lat_ref.3), kind=kLoop, calls=%fused_computation.3 | loop fusion | flops 320 | bytes 640 | tf_op jit(solution)/shard_map/mul | solution.py:543
  9.9 5.2 %all-to-all-done = s32[16,1,88]{2,1,0:T(1,128)S(1)} async-done(((s32[16,1,88]{2,1,0:T(1,128)}), s32[16,1,88]{2,1,0:T(1,128)S(1)}, u32[]{:S(2)}, u32[]{:S(2)}) %all-to-all-start) | async-done | bytes 5664 | tf_op jit(solution)/shard_map/all_to_all | solution.py:540
  15.1 0.6 slice_convert_fusion.1.given_ref
  15.7 12.8 %analyse.1 = (f32[16,80,128]{2,1,0:T(8,128)S(1)}, bf16[8,80,128]{2,1,0:T(8,128)(2,1)}, f32[1,128]{1,0:T(1,128)}) custom-call(s32[1280]{0:T(1024)} %points_ref.3, s32[80]{0:T(128)} %lat_ref.3, f32[80]{0:T(128)} %sine_multiply_fusion.weight_ref, f32[2,2]{1,0:T(2,128)} %coupling_ref.1, bf16[4,6560,128]{2,1,0:T(8,128)(2,1)} %bitcast.13, ...), custom_call_target="tpu_custom_call" | custom-call | tf_op jit(solution)/shard_map/analyse/pallas_call | solution.py:189
  28.5 3.4 %collective-permute-start = (bf16[8,80,128]{2,1,0:T(8,128)(2,1)}, bf16[8,80,128]{2,1,0:T(8,128)(2,1)S(1)}, u32[]{:S(2)}, u32[]{:S(2)}) collective-permute-start(bf16[8,80,128]{2,1,0:T(8,128)(2,1)} %get-tuple-element.16), channel_id=1, source_target_pairs={{0,1},{2,3},{4,5},{6,7},{8,9},{10,11},{12,13},{14,15},{16,17},{18,... | collective-permute-start | bytes 491528 | tf_op jit(solution)/shard_map/ppermute | solution.py:547
  31.9 3.7 %collective-permute-done.earlier_ref = bf16[8,80,128]{2,1,0:T(8,128)(2,1)S(1)} collective-permute-done((bf16[8,80,128]{2,1,0:T(8,128)(2,1)}, bf16[8,80,128]{2,1,0:T(8,128)(2,1)S(1)}, u32[]{:S(2)}, u32[]{:S(2)}) %collective-permute-start) | collective-permute-done | bytes 163872 | tf_op jit(solution)/shard_map/ppermute | solution.py:547
  35.6 1.2 %mix.1 = bf16[16,80,128]{2,1,0:T(8,128)(2,1)} custom-call(f32[16,80,128]{2,1,0:T(8,128)S(1)} %get-tuple-element.15.own_ref, bf16[8,80,128]{2,1,0:T(8,128)(2,1)S(1)} %collective-permute-done.earlier_ref), custom_call_target="tpu_custom_call" | custom-call | tf_op jit(solution)/shard_map/mix/pallas_call | solution.py:245
  36.8 3.5 %all-to-all-start.1 = ((bf16[16,80,128]{2,1,0:T(8,128)(2,1)}), bf16[16,80,128]{2,1,0:T(8,128)(2,1)S(1)}, u32[]{:S(2)}, u32[]{:S(2)}) async-start(bf16[16,80,128]{2,1,0:T(8,128)(2,1)} %mix.1), calls=%async_computation.1 | async-start | bytes 655360 | tf_op jit(solution)/shard_map/all_to_all | solution.py:550
  40.3 0.1 slice_convert_fusion
  40.4 0.7 convert_element_type.14.lat_ref
  41.1 4.6 %plan.1 = (f32[88,8,128]{2,1,0:T(8,128)S(1)}, f32[8,640]{1,0:T(8,128)S(1)}, f32[8,640]{1,0:T(8,128)S(1)}, f32[8,640]{1,0:T(8,128)S(1)}, s32[1]{0:T(128)}) custom-call(s32[1]{0:T(128)} %bitcast.5.band_ref, f32[1,128]{1,0:T(1,128)} %get-tuple-element.19.order_ref, f32[1,1280]{1,0:T(1,128)} %convert_element_type.14.lat_ref), custom_call_target="tpu_custom_call" | custom-call | tf_op jit(solution)/shard_map/plan/pallas_call | solution.py:342
  45.7 5.7 %all-to-all-done.1.own_ref = bf16[16,80,128]{2,1,0:T(8,128)(2,1)S(1)} async-done(((bf16[16,80,128]{2,1,0:T(8,128)(2,1)}), bf16[16,80,128]{2,1,0:T(8,128)(2,1)S(1)}, u32[]{:S(2)}, u32[]{:S(2)}) %all-to-all-start.1) | async-done | bytes 327712 | tf_op jit(solution)/shard_map/all_to_all | solution.py:550
  51.4 16.5 %legendre.1 = bf16[16,80,128]{2,1,0:T(8,128)(2,1)} custom-call(bf16[16,80,128]{2,1,0:T(8,128)(2,1)S(1)} %all-to-all-done.1.own_ref, f32[88,8,128]{2,1,0:T(8,128)S(1)} %get-tuple-element.20.term_ref, f32[8,640]{1,0:T(8,128)S(1)} %get-tuple-element.21.cos_ref, f32[8,640]{1,0:T(8,128)S(1)} %get-tuple-element.22.first_ref, ...), custom_call_target="tpu_custom_call" | custom-call | tf_op jit(solution)/shard_map/legendre/pallas_call | solution.py:417
  67.9 15.3 %all_to_all.22.back_ref = bf16[16,80,128]{2,1,0:T(8,128)(2,1)} all-to-all(bf16[16,80,128]{2,1,0:T(8,128)(2,1)} %legendre.1), channel_id=1, replica_groups=mesh['band'=16,'fld'=2] {'band'}, dimensions={0} | all-to-all | bytes 655360 | tf_op jit(solution)/shard_map/all_to_all | solution.py:553
  83.1 10.9 %synthesise.1 = bf16[4,6560,128]{2,1,0:T(8,128)(2,1)} custom-call(s32[1280]{0:T(1024)} %points_ref.3, s32[80]{0:T(128)} %lat_ref.3, bf16[16,80,128]{2,1,0:T(8,128)(2,1)} %all_to_all.22.back_ref, f32[1,128]{1,0:T(1,128)} %get-tuple-element.19.order_ref), custom_call_target="tpu_custom_call" | custom-call | tf_op jit(solution)/shard_map/synthesise/pallas_call | solution.py:514
Async XLA Ops:
  1.3 13.8 %all-to-all-start = ((s32[16,1,88]{2,1,0:T(1,128)}), s32[16,1,88]{2,1,0:T(1,128)S(1)}, u32[]{:S(2)}, u32[]{:S(2)}) async-start(s32[16,1,88]{2,1,0:T(1,128)} %bitcast.3), calls=%async_computation | async-start | bytes 16384 | tf_op jit(solution)/shard_map/all_to_all | solution.py:540
  28.5 7.1 %collective-permute-start = (bf16[8,80,128]{2,1,0:T(8,128)(2,1)}, bf16[8,80,128]{2,1,0:T(8,128)(2,1)S(1)}, u32[]{:S(2)}, u32[]{:S(2)}) collective-permute-start(bf16[8,80,128]{2,1,0:T(8,128)(2,1)} %get-tuple-element.16), channel_id=1, source_target_pairs={{0,1},{2,3},{4,5},{6,7},{8,9},{10,11},{12,13},{14,15},{16,17},{18,... | collective-permute-start | bytes 491528 | tf_op jit(solution)/shard_map/ppermute | solution.py:547
  36.8 14.6 %all-to-all-start.1 = ((bf16[16,80,128]{2,1,0:T(8,128)(2,1)}), bf16[16,80,128]{2,1,0:T(8,128)(2,1)S(1)}, u32[]{:S(2)}, u32[]{:S(2)}) async-start(bf16[16,80,128]{2,1,0:T(8,128)(2,1)} %mix.1), calls=%async_computation.1 | async-start | bytes 655360 | tf_op jit(solution)/shard_map/all_to_all | solution.py:550

commit v10 on v9

--- a/solution.py
+++ b/solution.py
@@ -518,14 +518,14 @@
         in_specs=[
             smem,
             smem,
-            pl.BlockSpec((bands, slots, 128), lambda i: (0, 0, 0)),
+            pl.BlockSpec(memory_space=pltpu.VMEM),
             pl.BlockSpec((1, count), lambda i: (0, 0)),
         ],
         out_specs=pl.BlockSpec((fields, GROUP * rows, 128), lambda i: (0, i, 0)),
         out_shape=jax.ShapeDtypeStruct((fields, slots * rows, 128), BF),
         scratch_shapes=[pltpu.VMEM((16, slots, count), F32)],
         compiler_params=pltpu.CompilerParams(dimension_semantics=("arbitrary",)),
-    )(points, lat_ids, back, orders)
+    )(points, lat_ids, *resident(back), orders)
 
 
 def solution(mesh):

time: 94.6 us -> 94.1 us (level)
  no operation moved by 1% of the time
where the time goes in v10:
time: 94.1 us; the launch traced here: 93 us
  Pallas kernels  45.6 us (48%)
  blocking collectives  14.6 us (16%)
  waiting for transfers between devices  14.4 us (15%)
  starting transfers between devices  14.3 us (15%)
  other arithmetic  2.71 us (3%)
  local copies, waits for them, and re-layouts  1.29 us (1%)
    pallas_call x1, Pallas kernels, legendre(): pl.pallas_call(kernel, name='legendre', in_specs=[vmem] * 5 + [pl.BlockSp...  16.4 us
    all_to_all x1, blocking collectives, on_device(): back = lax.all_to_all(back, 'band', split_axis=0, concat_axis=0, tiled=True)  14.6 us
    pallas_call x1, Pallas kernels, analyse(): pl.pallas_call(kernel, name='analyse', grid=(grid,), in_specs=[smem, smem...  12.8 us
    pallas_call x1, Pallas kernels, synthesise(): pl.pallas_call(kernel, name='synthesise', grid=(grid,), in_specs=[smem, s...  10.6 us
    all_to_all x1, starting transfers between devices, on_device(): lax.all_to_all(spread, 'band', split_axis=0, concat_axis=0, tiled=True)  7.39 us
    all_to_all x1, waiting for transfers between devices, on_device(): own = lax.all_to_all(own, 'band', split_axis=0, concat_axis=0, tiled=True)  5.66 us
    all_to_all x1, waiting for transfers between devices, on_device(): lax.all_to_all(spread, 'band', split_axis=0, concat_axis=0, tiled=True)  5.08 us
    pallas_call x1, Pallas kernels, plan(): pl.pallas_call(kernel, name='plan', in_specs=[smem, vmem, vmem], out_spec...  4.59 us
  transfers between devices with their start and end apart: 3, of which 3 were waited for; matrix products, arithmetic and copies ran while one was open for 2% of the time, Pallas kernels for 5%

profile of v10, /device:TPU:0, one launch (start us, length us, event | category | flops | bytes accessed | tf_op | source)
XLA Modules:
  0.0 93.0 jit_solution(18114978766581915584)
XLA Ops:
  0.0 0.7 pad_add_fusion
  0.7 0.6 broadcast.6
  1.3 7.4 %all-to-all-start = ((s32[16,1,88]{2,1,0:T(1,128)}), s32[16,1,88]{2,1,0:T(1,128)S(1)}, u32[]{:S(2)}, u32[]{:S(2)}) async-start(s32[16,1,88]{2,1,0:T(1,128)} %bitcast.3), calls=%async_computation | async-start | bytes 16384 | tf_op jit(solution)/shard_map/all_to_all | solution.py:540
  8.7 1.3 %sine_multiply_fusion.weight_ref = f32[80]{0:T(128)} fusion(s32[80]{0:T(128)} %lat_ref.3), kind=kLoop, calls=%fused_computation.3 | loop fusion | flops 320 | bytes 640 | tf_op jit(solution)/shard_map/mul | solution.py:543
  10.0 5.1 %all-to-all-done = s32[16,1,88]{2,1,0:T(1,128)S(1)} async-done(((s32[16,1,88]{2,1,0:T(1,128)}), s32[16,1,88]{2,1,0:T(1,128)S(1)}, u32[]{:S(2)}, u32[]{:S(2)}) %all-to-all-start) | async-done | bytes 5664 | tf_op jit(solution)/shard_map/all_to_all | solution.py:540
  15.1 0.6 slice_convert_fusion.1.given_ref
  15.7 12.8 %analyse.1 = (f32[16,80,128]{2,1,0:T(8,128)S(1)}, bf16[8,80,128]{2,1,0:T(8,128)(2,1)}, f32[1,128]{1,0:T(1,128)}) custom-call(s32[1280]{0:T(1024)} %points_ref.3, s32[80]{0:T(128)} %lat_ref.3, f32[80]{0:T(128)} %sine_multiply_fusion.weight_ref, f32[2,2]{1,0:T(2,128)} %coupling_ref.1, bf16[4,6560,128]{2,1,0:T(8,128)(2,1)} %bitcast.13, ...), custom_call_target="tpu_custom_call" | custom-call | tf_op jit(solution)/shard_map/analyse/pallas_call | solution.py:189
  28.5 3.4 %collective-permute-start = (bf16[8,80,128]{2,1,0:T(8,128)(2,1)}, bf16[8,80,128]{2,1,0:T(8,128)(2,1)S(1)}, u32[]{:S(2)}, u32[]{:S(2)}) collective-permute-start(bf16[8,80,128]{2,1,0:T(8,128)(2,1)} %get-tuple-element.16), channel_id=1, source_target_pairs={{0,1},{2,3},{4,5},{6,7},{8,9},{10,11},{12,13},{14,15},{16,17},{18,... | collective-permute-start | bytes 491528 | tf_op jit(solution)/shard_map/ppermute | solution.py:547
  31.9 3.7 %collective-permute-done.earlier_ref = bf16[8,80,128]{2,1,0:T(8,128)(2,1)S(1)} collective-permute-done((bf16[8,80,128]{2,1,0:T(8,128)(2,1)}, bf16[8,80,128]{2,1,0:T(8,128)(2,1)S(1)}, u32[]{:S(2)}, u32[]{:S(2)}) %collective-permute-start) | collective-permute-done | bytes 163872 | tf_op jit(solution)/shard_map/ppermute | solution.py:547
  35.6 1.2 %mix.1 = bf16[16,80,128]{2,1,0:T(8,128)(2,1)} custom-call(f32[16,80,128]{2,1,0:T(8,128)S(1)} %get-tuple-element.15.own_ref, bf16[8,80,128]{2,1,0:T(8,128)(2,1)S(1)} %collective-permute-done.earlier_ref), custom_call_target="tpu_custom_call" | custom-call | tf_op jit(solution)/shard_map/mix/pallas_call | solution.py:245
  36.8 3.5 %all-to-all-start.1 = ((bf16[16,80,128]{2,1,0:T(8,128)(2,1)}), bf16[16,80,128]{2,1,0:T(8,128)(2,1)S(1)}, u32[]{:S(2)}, u32[]{:S(2)}) async-start(bf16[16,80,128]{2,1,0:T(8,128)(2,1)} %mix.1), calls=%async_computation.1 | async-start | bytes 655360 | tf_op jit(solution)/shard_map/all_to_all | solution.py:550
  40.3 0.1 slice_convert_fusion
  40.4 0.7 convert_element_type.14.lat_ref
  41.1 4.6 %plan.1 = (f32[88,8,128]{2,1,0:T(8,128)S(1)}, f32[8,640]{1,0:T(8,128)S(1)}, f32[8,640]{1,0:T(8,128)S(1)}, f32[8,640]{1,0:T(8,128)S(1)}, s32[1]{0:T(128)}) custom-call(s32[1]{0:T(128)} %bitcast.5.band_ref, f32[1,128]{1,0:T(1,128)} %get-tuple-element.19.order_ref, f32[1,1280]{1,0:T(1,128)} %convert_element_type.14.lat_ref), custom_call_target="tpu_custom_call" | custom-call | tf_op jit(solution)/shard_map/plan/pallas_call | solution.py:342
  45.7 5.7 %all-to-all-done.1.own_ref = bf16[16,80,128]{2,1,0:T(8,128)(2,1)S(1)} async-done(((bf16[16,80,128]{2,1,0:T(8,128)(2,1)}), bf16[16,80,128]{2,1,0:T(8,128)(2,1)S(1)}, u32[]{:S(2)}, u32[]{:S(2)}) %all-to-all-start.1) | async-done | bytes 327712 | tf_op jit(solution)/shard_map/all_to_all | solution.py:550
  51.4 16.4 %legendre.1 = bf16[16,80,128]{2,1,0:T(8,128)(2,1)} custom-call(bf16[16,80,128]{2,1,0:T(8,128)(2,1)S(1)} %all-to-all-done.1.own_ref, f32[88,8,128]{2,1,0:T(8,128)S(1)} %get-tuple-element.20.term_ref, f32[8,640]{1,0:T(8,128)S(1)} %get-tuple-element.21.cos_ref, f32[8,640]{1,0:T(8,128)S(1)} %get-tuple-element.22.first_ref, ...), custom_call_target="tpu_custom_call" | custom-call | tf_op jit(solution)/shard_map/legendre/pallas_call | solution.py:417
  67.8 14.6 %all_to_all.22.back_ref = bf16[16,80,128]{2,1,0:T(8,128)(2,1)S(1)} all-to-all(bf16[16,80,128]{2,1,0:T(8,128)(2,1)} %legendre.1), channel_id=1, replica_groups=mesh['band'=16,'fld'=2] {'band'}, dimensions={0} | all-to-all | bytes 655360 | tf_op jit(solution)/shard_map/all_to_all | solution.py:553
  82.4 10.6 %synthesise.1 = bf16[4,6560,128]{2,1,0:T(8,128)(2,1)} custom-call(s32[1280]{0:T(1024)} %points_ref.3, s32[80]{0:T(128)} %lat_ref.3, bf16[16,80,128]{2,1,0:T(8,128)(2,1)S(1)} %all_to_all.22.back_ref, f32[1,128]{1,0:T(1,128)} %get-tuple-element.19.order_ref), custom_call_target="tpu_custom_call" | custom-call | tf_op jit(solution)/shard_map/synthesise/pallas_call | solution.py:514
Async XLA Ops:
  1.3 13.8 %all-to-all-start = ((s32[16,1,88]{2,1,0:T(1,128)}), s32[16,1,88]{2,1,0:T(1,128)S(1)}, u32[]{:S(2)}, u32[]{:S(2)}) async-start(s32[16,1,88]{2,1,0:T(1,128)} %bitcast.3), calls=%async_computation | async-start | bytes 16384 | tf_op jit(solution)/shard_map/all_to_all | solution.py:540
  28.5 7.1 %collective-permute-start = (bf16[8,80,128]{2,1,0:T(8,128)(2,1)}, bf16[8,80,128]{2,1,0:T(8,128)(2,1)S(1)}, u32[]{:S(2)}, u32[]{:S(2)}) collective-permute-start(bf16[8,80,128]{2,1,0:T(8,128)(2,1)} %get-tuple-element.16), channel_id=1, source_target_pairs={{0,1},{2,3},{4,5},{6,7},{8,9},{10,11},{12,13},{14,15},{16,17},{18,... | collective-permute-start | bytes 491528 | tf_op jit(solution)/shard_map/ppermute | solution.py:547
  36.8 14.6 %all-to-all-start.1 = ((bf16[16,80,128]{2,1,0:T(8,128)(2,1)}), bf16[16,80,128]{2,1,0:T(8,128)(2,1)S(1)}, u32[]{:S(2)}, u32[]{:S(2)}) async-start(bf16[16,80,128]{2,1,0:T(8,128)(2,1)} %mix.1), calls=%async_computation.1 | async-start | bytes 655360 | tf_op jit(solution)/shard_map/all_to_all | solution.py:550
